TPU v7x, 32 devices: a whole 2x2x4 slice. The times are simulated.
32 devices in a mesh: dom: 32 (over z, y, x, core).
Axes of the slice: x: 2, y: 2, z: 4, core: 2. Of those that a mesh axis runs over, the one named last changes fastest.
Arguments:
- right_side: float32 [8, 524288], P(None, 'dom'), may hold values from -24 to 24, as said below
- stiffness: float32 [3, 125, 8192], P(None, None, 'dom'), may hold values from 0.005 to 0.05
- mass: float32 [125, 8192], P(None, 'dom'), may hold values from 0.5 to 2
- region: int32 [8192], P('dom'), may hold values from 0 to 2
- density: float32 [3], replicated, may hold values from 0.5 to 2
- elem_nodes: int32 [125, 8192], P(None, 'dom'), may hold values from 0 to 20479, as said below
- peer_rank: int32 [32, 5], P('dom'), may hold values from 0 to 31, as said below
- send_nodes: int32 [32, 5, 128], P('dom'), may hold values from 0 to 16383, as said below
Outputs:
- solution: float32 [8, 524288], P(None, 'dom')
- residual: float32 [8, 524288], P(None, 'dom')
Inputs may be any that keep to these rules, and one draw needn't show every extreme that they name: `right_side`: A mean scale that rises along the partitions. `peer_rank`: the peers of partition r, in a drawn order: r + 1 and r - 1 modulo 32, and r XOR 2**k for 3 bit positions k between 1 and log2(32) - 1 that are the same for every partition, the highest one among them. Peers are mutual. `send_nodes`: repeats are possible within one list. `elem_nodes`: A value 16384 + s * 128 + c names slot c of what peer s shares with this partition. Elements 2 g and 2 g + 1 of a partition name own nodes only from 128 g to 128 g + 127, each of them at least once. List the received slots of a partition in the order of its peer_rank slots, slot c fastest, and repeat that list cyclically: for g < 64 the elements 2 g and 2 g + 1 also name exactly the entries g * 10 to (g + 1) * 10 - 1 of it, each once; other elements name no received slot.
All inputs are finite; a program needn't handle non-finite values.
Results may differ from a plain program's by a relative error of at most 0.0003.
Values sent between devices are 32-bit elements; how exact they have to be, the bound alone decides.
No kernel may reach another device: no remote copies, remote signals or barrier semaphores. Data moves between devices by JAX's collectives and lax.ppermute only.
A program may use at most 128 MiB of HBM per device.

v0:
```python
import functools

import jax
import jax.numpy as jnp
import numpy as np
from jax import lax
from jax.experimental import pallas as pl
from jax.experimental.pallas import tpu as pltpu
from jax.sharding import PartitionSpec as P

ITERS = 2
LANES = 128
ROWS = 8
NONE = 255
SIDE = 5
NPE = SIDE**3


def gll_matrix():
    points = np.array([-1.0, -np.sqrt(3.0 / 7.0), 0.0, np.sqrt(3.0 / 7.0), 1.0])
    weights = np.array(
        [
            1.0 / np.prod([points[column] - points[other] for other in range(5) if other != column])
            for column in range(5)
        ]
    )
    matrix = np.zeros((5, 5))
    for row_index in range(5):
        for column in range(5):
            if row_index != column:
                matrix[row_index, column] = (
                    weights[column] / weights[row_index] / (points[row_index] - points[column])
                )
        matrix[row_index, row_index] = -np.sum(matrix[row_index])
    return matrix


def direction_matrices():
    base = np.asarray(gll_matrix(), np.float32)
    eye = np.eye(SIDE, dtype=np.float32)
    return [
        np.einsum("ai,bj,ck->abcijk", *factors).reshape(NPE, NPE)
        for factors in ((base, eye, eye), (eye, base, eye), (eye, eye, base))
    ]


def split_np(values):
    high = values.astype(jnp.bfloat16)
    low = (values - high.astype(np.float32)).astype(jnp.bfloat16)
    return high, low


def constant_operands():
    mats = direction_matrices()
    grad = np.zeros((LANES, 3 * LANES), np.float32)
    for d in range(3):
        grad[:NPE, d * LANES : d * LANES + NPE] = mats[d].T
    high, low = split_np(grad)
    first = np.block([[high, low], [high, np.zeros_like(low)]])
    back_high, back_low = high.T, low.T
    second = np.block([[back_high, back_low], [back_high, back_low]])
    squares = np.stack(split_np(np.stack([m.T * m.T for m in mats])))
    return jnp.asarray(first), jnp.asarray(second), jnp.asarray(squares)


def take(values, index):
    numbers = lax.GatherDimensionNumbers(
        offset_dims=(),
        collapsed_slice_dims=(1,),
        start_index_map=(1,),
        operand_batching_dims=(0,),
        start_indices_batching_dims=(0,),
    )
    return lax.gather(
        values, index[..., None], numbers, (1, 1), mode=lax.GatherScatterMode.PROMISE_IN_BOUNDS
    )


def iota(shape, axis):
    return lax.broadcasted_iota(jnp.int32, shape, axis)


def spread(row, rows=ROWS):
    return jnp.broadcast_to(row, (rows, row.shape[-1]))


def codes_of(nodes, lane_offset, peer_ref, own_count, peer_count, window):
    pair = (iota(nodes.shape, 1) + lane_offset) >> 1
    own = nodes - pair * window
    ref = nodes - own_count
    sender = ref // LANES
    slot = jnp.zeros_like(ref)
    for p in range(1, peer_count):
        slot = jnp.where(sender == peer_ref[0, p], p, slot)
    return jnp.where(ref >= 0, window + slot * LANES + (ref & (LANES - 1)), own)


def vmem():
    return pl.BlockSpec(memory_space=pltpu.VMEM)


def smem():
    return pl.BlockSpec(memory_space=pltpu.SMEM)


def hbm():
    return pl.BlockSpec(memory_space=pltpu.HBM)


def call(body, name, in_specs, outs, stay, scratch=(), resident=(), grid=()):
    kernel = pl.pallas_call(
        body,
        name=name,
        grid=grid,
        in_specs=in_specs,
        out_specs=tuple(vmem() for _ in outs),
        out_shape=tuple(
            pltpu.VMEM(shape, dtype) if k in stay else jax.ShapeDtypeStruct(shape, dtype)
            for k, (shape, dtype) in enumerate(outs)
        ),
        scratch_shapes=list(scratch),
        compiler_params=pltpu.CompilerParams(vmem_limit_bytes=24 << 20),
    )

    def run(*operands):
        return kernel(
            *[
                pltpu.with_memory_space_constraint(operand, pltpu.VMEM if k in resident else pltpu.HBM)
                for k, operand in enumerate(operands)
            ]
        )

    return run


def element_sums(mass, region, density, stiff, squares):
    dens = jnp.where(region == 0, density[0], jnp.where(region == 1, density[1], density[2]))
    term = mass * dens
    total = term
    for d in range(3):
        high = stiff[d].astype(jnp.bfloat16)
        low = (stiff[d] - high.astype(jnp.float32)).astype(jnp.bfloat16)
        for weight, part in ((squares[0, d], high), (squares[0, d], low), (squares[1, d], high)):
            total = total + jnp.dot(weight, part, preferred_element_type=jnp.float32)
    return term, total


def ghost_diag_body(cfg, peer, density, nodes, stiff, mass, region, squares, send, pos):
    run = cfg["run"]
    _, edge = element_sums(mass[...], region[...], density, stiff, squares)
    code = codes_of(nodes[...], 0, peer, cfg["own"], cfg["peers"], cfg["window"])
    lane = iota(code.shape, 1)
    base = code - (cfg["window"] + run * (lane >> 1))
    place = iota(code.shape, 0) + LANES * (lane & 1)
    flat = iota((ROWS, LANES), 0) * LANES + iota((ROWS, LANES), 1)
    pair = (flat * cfg["magic"]) >> 16
    hop = flat - pair * run
    pair_lane = jnp.minimum(2 * pair, LANES - 1)
    got = jnp.zeros((ROWS, LANES), jnp.float32)
    where_at = jnp.zeros((ROWS, LANES), jnp.int32)
    for h in range(run):
        hit = base == h
        position = jnp.sum(jnp.where(hit, place, 0), axis=0, keepdims=True)
        value = jnp.sum(jnp.where(hit, edge, 0.0), axis=0, keepdims=True)
        position, value = spread(position), spread(value)
        position = position + pltpu.roll(position, LANES - 1, 1)
        value = value + pltpu.roll(value, LANES - 1, 1)
        got = jnp.where(hop == h, take(value, pair_lane), got)
        where_at = jnp.where(hop == h, take(position, pair_lane), where_at)
    pos[...] = where_at
    send[...] = jnp.zeros(send.shape, jnp.float32)
    for p in range(cfg["peers"]):
        send[peer[0, p]] = got[p : p + 1]


def tables_body(
    cfg, peer, density, nodes, stiff, mass, region, squares, send_s, send_v, right,
    idx, st_edge, mt_edge, st_inner, mt_inner, own_diag, right_at, diag_at, same,
    code_pad, value_pad, rows,
):
    code_pad[...] = jnp.full(code_pad.shape, NONE, jnp.int32)
    value_pad[...] = jnp.zeros(value_pad.shape, jnp.float32)

    def turned(ref):
        return jnp.concatenate([ref[:, :LANES].T, ref[:, LANES:].T], axis=0)

    for b in range(2):
        cols = slice(b * LANES, (b + 1) * LANES)
        code_pad[:NPE, cols] = codes_of(
            nodes[:, cols], b * LANES, peer, cfg["own"], cfg["peers"], cfg["window"]
        )
    idx[...] = turned(code_pad)
    term, diag = element_sums(mass[...], region[...], density, stiff, squares)
    value_pad[:NPE] = diag
    rows[...] = turned(value_pad)
    for g in range(cfg["pairs"]):
        row = jnp.concatenate([rows[2 * g : 2 * g + 1, :], rows[2 * g + 1 : 2 * g + 2, :]], axis=1)
        own_diag[g : g + 1, :] = scatter_rows(spread(row), idx, g)[:1]
    for d in range(3):
        value_pad[:NPE] = stiff[d]
        cols = slice(d * LANES, (d + 1) * LANES)
        st_edge[:, cols] = value_pad[:, :LANES].T
        st_inner[:, cols] = value_pad[:, LANES:].T
    value_pad[:NPE] = term
    mt_edge[...] = value_pad[:, :LANES].T
    mt_inner[...] = value_pad[:, LANES:].T
    pick(cfg, right, send_s, send_v, right_at)
    node = slot_nodes(cfg, send_v)
    wide = node.shape[1]
    hot = jnp.where(iota((LANES, wide), 0) == (node & (LANES - 1)), 1.0, 0.0).astype(jnp.bfloat16)
    here = iota((LANES, wide), 0) == (node >> 7)
    at_slots = jnp.zeros((1, wide), jnp.float32)
    for part in reversed(parts_of(own_diag[...], 3)):
        seen = jnp.dot(part.astype(jnp.bfloat16), hot, preferred_element_type=jnp.float32)
        at_slots = at_slots + jnp.sum(jnp.where(here, seen, 0.0), axis=0, keepdims=True)
    diag_at[...] = spread(at_slots)
    for p in range(cfg["peers"]):
        column = jnp.broadcast_to(send_v[p], (LANES, LANES)).T
        for q in range(cfg["peers"]):
            same[p * LANES : (p + 1) * LANES, q * LANES : (q + 1) * LANES] = jnp.where(
                column == send_v[q], 1.0, 0.0
            ).astype(jnp.bfloat16)


def scatter_rows(rows, idx, g):
    node = iota((LANES, LANES), 0)
    spots = jnp.concatenate(
        [jnp.where(node == idx[2 * g + k : 2 * g + k + 1, :], 1.0, 0.0) for k in range(2)], axis=1
    ).astype(jnp.bfloat16)
    high = rows.astype(jnp.bfloat16).astype(jnp.float32)
    both = jnp.concatenate([high, rows - high], axis=0).astype(jnp.bfloat16)
    sums = lax.dot_general(both, spots, (((1,), (1,)), ((), ())), preferred_element_type=jnp.float32)
    return sums[:ROWS] + sums[ROWS:]


def pick(cfg, field, send_s, send_v, out):
    lane = iota((ROWS, LANES), 1)
    for p in range(cfg["peers"]):
        low = spread(send_v[p] & (LANES - 1))
        got = jnp.zeros((ROWS, LANES), jnp.float32)
        for c in range(LANES):
            base = pl.multiple_of((send_s[p, 0, c] >> 7) * LANES, LANES)
            got = jnp.where(lane == c, take(field[:, pl.ds(base, LANES)], low), got)
        out[:, p * LANES : (p + 1) * LANES] = got


def slot_nodes(cfg, send_v):
    return jnp.concatenate([send_v[p] for p in range(cfg["peers"])], axis=1)


def nt_dot(left, right):
    return lax.dot_general(left, right, (((1,), (1,)), ((), ())), preferred_element_type=jnp.float32)


def parts_of(values, count):
    parts = []
    for _ in range(count):
        part = values.astype(jnp.bfloat16).astype(jnp.float32)
        parts.append(part)
        values = values - part
    return parts


def received_diag(cfg, peer, recv):
    return jnp.concatenate([recv[peer[0, p]] for p in range(cfg["peers"])], axis=1)


def received_rows(cfg, peer, recv):
    blocks = []
    for p in range(cfg["peers"]):
        first = peer[0, p] * (ROWS + 1)
        blocks.append(jnp.concatenate([recv[first + v] for v in range(ROWS)], axis=0))
    return jnp.concatenate(blocks, axis=1)


def put_slots(cfg, peer, values, out):
    for p in range(cfg["peers"]):
        out[peer[0, p]] = values[:, p * LANES : (p + 1) * LANES]


def start_body(cfg, peer, recv, right_at, diag_at, same, out, inverse_at):
    got = spread(received_diag(cfg, peer, recv))
    top, middle, bottom = parts_of(got, 3)
    both = jnp.concatenate([top, middle], axis=0).astype(jnp.bfloat16)
    more = jnp.concatenate([bottom, bottom], axis=0).astype(jnp.bfloat16)
    first = nt_dot(both, same[...])
    total = diag_at[...] + (first[:ROWS] + (first[ROWS:] + nt_dot(more, same[...])[:ROWS]))
    inverse = 1.0 / total
    inverse_at[...] = inverse
    out[...] = jnp.zeros(out.shape, jnp.float32)
    put_slots(cfg, peer, right_at[...] * inverse, out)


def first_fields_body(cfg, peer, send_v, recv, own_diag, right_hbm, inverse, z, energy, right, arrived):
    fetch = pltpu.make_async_copy(right_hbm, right, arrived)
    fetch.start()
    windows = cfg["pairs"]
    node, got = slot_nodes(cfg, send_v), received_diag(cfg, peer, recv)
    here = iota((windows, got.shape[1]), 0) == (node >> 7)
    hot = jnp.where(iota((LANES, got.shape[1]), 0) == (node & (LANES - 1)), 1.0, 0.0).astype(jnp.bfloat16)
    total = own_diag[...]
    for part in parts_of(got, 3):
        total = total + nt_dot(jnp.where(here, spread(part, windows), 0.0).astype(jnp.bfloat16), hot)
    inverse[...] = 1.0 / total
    fetch.wait()
    acc = jnp.zeros((ROWS, LANES), jnp.float32)
    for g in range(windows):
        cols = slice(g * LANES, (g + 1) * LANES)
        scaled = right[:, cols] * spread(inverse[g : g + 1, :])
        z[:, cols] = scaled
        acc = acc + right[:, cols] * scaled
    energy[...] = acc


def apply_rows(values, st, mt, weights1, weights2):
    count = values.shape[0] // ROWS

    def halves(x):
        high = x.astype(jnp.bfloat16)
        return jnp.concatenate([high, (x - high.astype(jnp.float32)).astype(jnp.bfloat16)], axis=1)

    both = jnp.dot(halves(values), weights1[...], preferred_element_type=jnp.float32)
    wide = 3 * LANES
    grad = (both[:, :wide] + both[:, wide:]).reshape(count, ROWS, wide)
    flux = (grad * st[:, None, :]).reshape(count * ROWS, wide)
    both = jnp.dot(halves(flux), weights2[...], preferred_element_type=jnp.float32)
    lumped = (values.reshape(count, ROWS, LANES) * mt[:, None, :]).reshape(count * ROWS, LANES)
    return both[:, :LANES] + both[:, LANES:] + lumped


CHUNK = 64


def apply_half(values, result, st, mt, weights1, weights2):
    acc = jnp.zeros((ROWS, LANES), jnp.float32)
    for c in range(values.shape[0] // (ROWS * CHUNK)):
        rows = slice(c * CHUNK * ROWS, (c + 1) * CHUNK * ROWS)
        elems = slice(c * CHUNK, (c + 1) * CHUNK)
        v = values[rows]
        r = apply_rows(v, st[elems], mt[elems], weights1, weights2)
        result[rows] = r
        acc = acc + jnp.sum((v * r).reshape(CHUNK, ROWS, LANES), axis=0)
    return acc


def scatter_half(result, idx, out, first_pair, pair_count):
    for g in range(pair_count):
        e = 2 * g * ROWS
        rows = jnp.concatenate([result[e : e + ROWS], result[e + ROWS : e + 2 * ROWS]], axis=1)
        out[:, g * LANES : (g + 1) * LANES] = scatter_rows(rows, idx, first_pair + g)


def inner_body(cfg, z, idx, st, mt, w1, w2, out, curve, values, result):
    edge, pairs = cfg["edge_pairs"], cfg["pairs"]
    for g in range(edge, pairs):
        window = z[:, g * LANES : (g + 1) * LANES]
        for parity in range(2):
            e = 2 * g + parity
            at = (e - 2 * edge) * ROWS
            values[at : at + ROWS] = take(window, spread(idx[e : e + 1, :] & (LANES - 1)))
    curve[...] = apply_half(values, result, st, mt, w1, w2)
    scatter_half(result, idx, out, edge, pairs - edge)


def edge_body(cfg, peer, recv, z, idx, st, mt, pos, w1, w2, energy, curve, result, out, values, ghosts):
    run, edge, peers = cfg["run"], cfg["edge_pairs"], cfg["peers"]
    for p in range(peers):
        ghosts[p] = recv[peer[0, p]]
    spans = []
    for g in range(edge):
        low, high = run * g // LANES, (run * (g + 1) - 1) // LANES
        spans.append((low, high))
        window = z[:, g * LANES : (g + 1) * LANES]
        for parity in range(2):
            e = 2 * g + parity
            code = spread(idx[e : e + 1, :])
            at = code & (LANES - 1)
            got = take(ghosts[low], at)
            if high > low:
                got = jnp.where(code < LANES * (high + 1), got, take(ghosts[high], at))
            values[e * ROWS : (e + 1) * ROWS] = jnp.where(code < LANES, take(window, at), got)
    acc = apply_half(values, result, st, mt, w1, w2) + curve[...]
    lane = iota((ROWS, LANES), 1)
    sums = [jnp.zeros((ROWS, LANES), jnp.float32) for _ in range(peers)]
    for g in range(edge):
        for p in range(spans[g][0], spans[g][1] + 1):
            place = spread(pos[p : p + 1, :])
            at = place & (LANES - 1)
            e = 2 * g * ROWS
            value = jnp.where(
                place < LANES, take(result[e : e + ROWS], at), take(result[e + ROWS : e + 2 * ROWS], at)
            )
            begin, end = run * g - p * LANES, run * (g + 1) - p * LANES
            sums[p] = jnp.where((lane >= begin) & (lane < end), value, sums[p])
    row = iota((ROWS, LANES), 0)
    dots = jnp.where(lane == row, jnp.sum(energy[...], axis=1, keepdims=True), 0.0)
    dots = jnp.where(lane == row + ROWS, jnp.sum(acc, axis=1, keepdims=True), dots)
    dots = jnp.sum(dots, axis=0, keepdims=True)
    out[...] = jnp.zeros(out.shape, jnp.float32)
    for n in range(out.shape[0] // (ROWS + 1)):
        out[n * (ROWS + 1) + ROWS] = dots
    for p in range(peers):
        for v in range(ROWS):
            out[peer[0, p] * (ROWS + 1) + v] = sums[p][v : v + 1]


def edge_scatter_body(cfg, result, idx, inner, out):
    split = cfg["edge_pairs"] * LANES
    scatter_half(result, idx, out, 0, cfg["edge_pairs"])
    out[:, split:] = inner[...]


def edge_scatter_pick_body(cfg, send_s, send_v, result, idx, inner, out, at_slots):
    edge_scatter_body(cfg, result, idx, inner, out)
    pick(cfg, out, send_s, send_v, at_slots)


def returned_sums(cfg, peer, send_v, recv, left, hot):
    windows = cfg["pairs"]
    node, value = slot_nodes(cfg, send_v), received_rows(cfg, peer, recv)
    wide = node.shape[1]
    high, low = parts_of(value, 2)
    lanes = jnp.where(iota((LANES, wide), 0) == (node & (LANES - 1)), 1.0, 0.0).astype(jnp.bfloat16)
    hot[:, :wide] = lanes
    hot[:, wide:] = lanes
    block = spread(node >> 7)
    for g in range(0, windows, 2):
        rows = slice(g * ROWS, (g + 2) * ROWS)
        even, odd = block == g, block == g + 1
        left[rows, :wide] = jnp.concatenate(
            [jnp.where(even, high, 0.0), jnp.where(odd, high, 0.0)], axis=0
        ).astype(jnp.bfloat16)
        left[rows, wide:] = jnp.concatenate(
            [jnp.where(even, low, 0.0), jnp.where(odd, low, 0.0)], axis=0
        ).astype(jnp.bfloat16)
    return nt_dot(left[...], hot[...])


def dot_totals(recv):
    total = recv[ROWS]
    for n in range(1, recv.shape[0] // (ROWS + 1)):
        total = total + recv[n * (ROWS + 1) + ROWS]
    total = spread(total)
    lane, row = iota((ROWS, LANES), 1), iota((ROWS, LANES), 0)
    return [
        jnp.broadcast_to(
            jnp.sum(jnp.where(lane == row + k * ROWS, total, 0.0), axis=1, keepdims=True), (ROWS, LANES)
        )
        for k in range(2)
    ]


def step_body(cfg, peer, recv, right_at, inverse_at, image_at, same, out, coefs):
    energy_now, curve_now = dot_totals(recv)
    alpha = energy_now / curve_now
    coefs[0] = alpha
    coefs[1] = energy_now
    both = jnp.concatenate(parts_of(received_rows(cfg, peer, recv), 2), axis=0).astype(jnp.bfloat16)
    got = nt_dot(both, same[...])
    image = image_at[...] + (got[:ROWS] + got[ROWS:])
    left_over = right_at[...] - spread_lanes(alpha, image.shape[1]) * image
    out[...] = jnp.zeros(out.shape, jnp.float32)
    put_slots(cfg, peer, left_over * inverse_at[...], out)


def spread_lanes(tile, wide):
    return jnp.concatenate([tile] * (wide // LANES), axis=1)


def next_fields_body(
    cfg, peer, send_v, recv, own, right_hbm, inverse, coefs, w, z1, energy, left, hot, sums, right, arrived
):
    fetch = pltpu.make_async_copy(right_hbm, right, arrived)
    fetch.start()
    windows = cfg["pairs"]
    sums[...] = returned_sums(cfg, peer, send_v, recv, left, hot)
    alpha = coefs[0]
    fetch.wait()
    acc = jnp.zeros((ROWS, LANES), jnp.float32)
    for g in range(windows):
        cols = slice(g * LANES, (g + 1) * LANES)
        image = own[:, cols] + sums[g * ROWS : (g + 1) * ROWS]
        w[:, cols] = image
        left_over = right[:, cols] - alpha * image
        scaled = left_over * spread(inverse[g : g + 1, :])
        z1[:, cols] = scaled
        acc = acc + left_over * scaled
    energy[...] = acc


def last_body(
    cfg, peer, send_v, recv, own, right_hbm, inverse, w, z1, coefs,
    solution, residual, left, hot, sums, right, arrived,
):
    fetch = pltpu.make_async_copy(right_hbm, right, arrived)
    fetch.start()
    windows = cfg["pairs"]
    sums[...] = returned_sums(cfg, peer, send_v, recv, left, hot)
    energy_next, curve_next = dot_totals(recv)
    alpha, energy_now = coefs[0], coefs[1]
    beta = energy_next / energy_now
    step = energy_next / (curve_next - beta * energy_next / alpha)
    fetch.wait()
    for g in range(windows):
        cols = slice(g * LANES, (g + 1) * LANES)
        image = own[:, cols] + sums[g * ROWS : (g + 1) * ROWS]
        start, before = right[:, cols], w[:, cols]
        z0 = start * spread(inverse[g : g + 1, :])
        residual[:, cols] = (start - alpha * before) - step * (image + beta * before)
        solution[:, cols] = alpha * z0 + step * (z1[:, cols] + beta * z0)


def on_device(right_side, stiffness, mass, region, density, elem_nodes, peer_rank, send_nodes):
    vectors, own_count = right_side.shape
    elem_count = elem_nodes.shape[1]
    pairs = elem_count // 2
    edge_pairs = pairs // 2
    peers, slots = send_nodes.shape[1], send_nodes.shape[2]
    devices = lax.axis_size("dom")
    run = peers * slots // edge_pairs
    magic = (1 << 16) // run + 1
    flat = np.arange(ROWS * LANES)
    if (
        vectors != ROWS or own_count != pairs * LANES or slots != LANES or pairs != LANES
        or peers * slots != run * edge_pairs or peers > ROWS or run > LANES
        or ((flat * magic) >> 16 != flat // run).any()
    ):
        raise ValueError("unsupported sizes")
    cfg = dict(
        own=own_count, pairs=pairs, edge_pairs=edge_pairs, peers=peers, run=run, magic=magic,
        window=own_count // pairs,
    )
    f32, i32 = jnp.float32, jnp.int32
    weights1, weights2, squares = constant_operands()
    V, S = vmem(), smem()
    field = ((vectors, own_count), f32)
    half_field = ((vectors, own_count // 2), f32)
    tile = ((ROWS, LANES), f32)
    square = ((LANES, LANES), f32)
    half_rows = ((elem_count // 2 * ROWS, LANES), f32)

    def bind(body):
        return functools.partial(body, cfg)

    def exchange(values):
        return lax.all_to_all(values, "dom", split_axis=0, concat_axis=0, tiled=True)

    regions = region.reshape(1, elem_count)
    half_specs = [
        pl.BlockSpec((NPE, LANES), lambda _: (0, 0)),
        pl.BlockSpec((3, NPE, LANES), lambda _: (0, 0, 0)),
        pl.BlockSpec((NPE, LANES), lambda _: (0, 0)),
        pl.BlockSpec((1, LANES), lambda _: (0, 0)),
    ]
    send, pos = call(
        bind(ghost_diag_body), "ghost_diag", [S, S, *half_specs, V],
        [((devices, 1, LANES), f32), ((ROWS, LANES), i32)], (1,), grid=(1,),
    )(peer_rank, density, elem_nodes, stiffness, mass, regions, squares)
    recv = exchange(send)
    shared = jnp.transpose(send_nodes, (1, 0, 2))
    slots_all = ((vectors, peers * slots), f32)
    edge_count = elem_count // 2
    idx, st_edge, mt_edge, st_inner, mt_inner, own_diag, right_at, diag_at, same = call(
        bind(tables_body), "tables", [S, S] + [V] * 5 + [S, V, V],
        [
            ((elem_count, LANES), i32),
            ((edge_count, 3 * LANES), f32), ((edge_count, LANES), f32),
            ((elem_count - edge_count, 3 * LANES), f32), ((elem_count - edge_count, LANES), f32),
            square, slots_all, slots_all, ((peers * slots, peers * slots), jnp.bfloat16),
        ],
        (0, 1, 2, 5, 6, 7, 8),
        [
            pltpu.VMEM((LANES, elem_count), i32), pltpu.VMEM((LANES, elem_count), f32),
            pltpu.VMEM((elem_count, LANES), f32),
        ],
    )(peer_rank, density, elem_nodes, stiffness, mass, regions, squares, shared, shared, right_side)

    send_shape = ((devices, ROWS, LANES), f32)
    copied = [pltpu.VMEM(*field), pltpu.SemaphoreType.DMA(())]
    send, inverse_at = call(
        bind(start_body), "start", [S] + [V] * 4, [send_shape, slots_all], (1,), (), (1, 2, 3, 4)
    )(peer_rank, recv, right_at, diag_at, same)
    diag_recv = recv
    recv = exchange(send)
    inverse, z, energy = call(
        bind(first_fields_body), "first_fields", [S, V, V, V, hbm()], [square, field, tile], range(3),
        copied, (2, 3),
    )(peer_rank, shared, diag_recv, own_diag, right_side)

    def inner_part(z):
        return call(
            bind(inner_body), "inner", [V] * 6, [half_field, tile], range(2),
            [pltpu.VMEM(*half_rows), pltpu.VMEM(*half_rows)], (0, 1, 4, 5),
        )(z, idx, st_inner, mt_inner, weights1, weights2)

    def edge_part(recv, z, energy, curve):
        return call(
            bind(edge_body), "edge", [S] + [V] * 10,
            [half_rows, ((devices * (ROWS + 1), 1, LANES), f32)], (0,),
            [pltpu.VMEM(*half_rows), pltpu.VMEM((peers, ROWS, LANES), f32)], range(1, 11),
        )(peer_rank, recv, z, idx, st_edge, mt_edge, pos, weights1, weights2, energy, curve)

    wide = 2 * peers * slots
    scratch = [
        pltpu.VMEM((vectors * pairs, wide), jnp.bfloat16), pltpu.VMEM((LANES, wide), jnp.bfloat16),
        pltpu.VMEM((vectors * pairs, LANES), f32), *copied,
    ]
    inner, curve = inner_part(z)
    result, send = edge_part(recv, z, energy, curve)
    recv = exchange(send)
    own, image_at = call(
        bind(edge_scatter_pick_body), "edge_scatter_pick", [S] + [V] * 4, [field, slots_all], range(2), (),
        (2, 3, 4),
    )(shared, shared, result, idx, inner)
    send, coefs = call(
        bind(step_body), "step", [S] + [V] * 5, [send_shape, ((2, ROWS, LANES), f32)], (1,), (),
        range(1, 6),
    )(peer_rank, recv, right_at, inverse_at, image_at, same)
    sum_recv = recv
    recv = exchange(send)
    w, z, energy = call(
        bind(next_fields_body), "next_fields", [S] + [V] * 3 + [hbm()] + [V] * 2, [field, field, tile],
        range(3), scratch, (2, 3, 5, 6),
    )(peer_rank, shared, sum_recv, own, right_side, inverse, coefs)
    inner, curve = inner_part(z)
    result, send = edge_part(recv, z, energy, curve)
    recv = exchange(send)
    (own,) = call(bind(edge_scatter_body), "edge_scatter", [V] * 3, [field], (0,), (), range(3))(
        result, idx, inner
    )
    return call(
        bind(last_body), "last", [S] + [V] * 3 + [hbm()] + [V] * 4, [field, field], (), scratch,
        (2, 3, 5, 6, 7, 8),
    )(peer_rank, shared, recv, own, right_side, inverse, w, z, coefs)


def solution(mesh):
    placed = (
        P(None, "dom"),
        P(None, None, "dom"),
        P(None, "dom"),
        P("dom"),
        P(),
        P(None, "dom"),
        P("dom", None),
        P("dom", None, None),
    )
    return jax.shard_map(
        on_device,
        mesh=mesh,
        in_specs=placed,
        out_specs=(P(None, "dom"), P(None, "dom")),
        check_vma=False,
    )
```

profile of v0, /device:TPU:0, one launch (start us, length us, event | category | flops | bytes accessed | tf_op | source)
XLA Modules:
  0.0 79.8 jit_solution(15729625992971846430)
XLA Ops:
  0.6 2.2 %ghost_diag.1 = (f32[32,1,128]{2,1,0:T(1,128)}, s32[8,128]{1,0:T(8,128)S(1)}) custom-call(s32[1,5]{1,0:T(1,128)} %peer.17, f32[3]{0:T(128)} %density.3, s32[125,256]{1,0:T(8,128)} %nodes.3, f32[3,125,256]{2,1,0:T(8,128)} %stiff.3, f32[125,256]{1,0:T(8,128)} %mass.3, s32[1,256]{1,0:T(1,128)} %bitcast.9, bf16[2,3,125,125]{3,2,1,0:T(8,128)(2,1)} %constant.8.clone.squares), custom_call_target="tpu_custom_call" | custom-call | tf_op jit(solution)/shard_map/ghost_diag/pallas_call | solution.py:126
  2.9 7.3 %all-to-all-start = ((f32[32,1,128]{2,1,0:T(1,128)}), f32[32,1,128]{2,1,0:T(1,128)S(1)}, u32[]{:S(2)}, u32[]{:S(2)}) async-start(f32[32,1,128]{2,1,0:T(1,128)} %get-tuple-element.33), calls=%async_computation | async-start | bytes 32768 | tf_op jit(solution)/shard_map/all_to_all | solution.py:546
  10.2 4.8 %tables.1 = (s32[256,128]{1,0:T(8,128)S(1)}, f32[128,384]{1,0:T(8,128)S(1)}, f32[128,128]{1,0:T(8,128)S(1)}, f32[128,384]{1,0:T(8,128)S(1)}, f32[128,128]{1,0:T(...) custom-call(s32[1,5]{1,0:T(1,128)} %peer.17, ...), custom_call_target="tpu_custom_call" | custom-call | tf_op jit(solution)/shard_map/tables/pallas_call | solution.py:126
  15.0 0.0 copy-start.2
  15.0 0.7 copy-done.2
  15.7 0.0 copy-start.5
  15.7 0.6 copy-done.5
  16.3 1.0 %all-to-all-done.recv = f32[32,1,128]{2,1,0:T(1,128)S(1)} async-done(((f32[32,1,128]{2,1,0:T(1,128)}), f32[32,1,128]{2,1,0:T(1,128)S(1)}, u32[]{:S(2)}, u32[]{:S(2)}) %all-to-all-start) | async-done | bytes 16416 | tf_op jit(solution)/shard_map/all_to_all | solution.py:546
  17.3 1.9 %start.1 = (f32[32,8,128]{2,1,0:T(8,128)}, f32[8,640]{1,0:T(8,128)S(1)}) custom-call(s32[1,5]{1,0:T(1,128)} %peer.17, f32[32,1,128]{2,1,0:T(1,128)S(1)} %all-to-all-done.recv, f32[8,640]{1,0:T(8,128)S(1)} %get-tuple-element.34.right_at, f32[8,640]{1,0:T(8,128)S(1)} %get-tuple-element.35.diag_at, bf16[640,640]{1,0:T(8,128)(2,1)S(1)} %get-tuple-element.36.same), custom_call_target="tpu_custom_call" | custom-call | tf_op jit(solution)/shard_map/start/pallas_call | solution.py:126
  19.2 0.0 copy-start.6
  19.2 0.6 copy-done.6
  19.8 0.0 copy-start
  19.8 0.0 copy-start.1
  19.8 4.8 %all-to-all-start.1 = ((f32[32,8,128]{2,1,0:T(8,128)}), f32[32,8,128]{2,1,0:T(8,128)S(1)}, u32[]{:S(2)}, u32[]{:S(2)}) async-start(f32[32,8,128]{2,1,0:T(8,128)} %get-tuple-element.37), calls=%async_computation.1 | async-start | bytes 262144 | tf_op jit(solution)/shard_map/all_to_all | solution.py:546
  24.6 1.9 %first_fields.1 = (f32[128,128]{1,0:T(8,128)S(1)}, f32[8,16384]{1,0:T(8,128)S(1)}, f32[8,128]{1,0:T(8,128)S(1)}) custom-call(s32[1,5]{1,0:T(1,128)} %peer.17, s32[5,1,128]{2,1,0:T(1,128)} %bitcast.4, f32[32,1,128]{2,1,0:T(1,128)S(1)} %all-to-all-done.recv, f32[128,128]{1,0:T(8,128)S(1)} %get-tuple-element.38.own_diag, f32[8,16384]{1,0:T(8,128)} %right_hbm.5), custom_call_target="tpu_custom_call" | custom-call | tf_op jit(solution)/shard_map/first_fields/pallas_call | solution.py:126
  26.5 0.0 copy-done
  26.6 0.0 copy-done.1
  26.6 3.2 %inner.2 = (f32[8,8192]{1,0:T(8,128)S(1)}, f32[8,128]{1,0:T(8,128)S(1)}) custom-call(f32[8,16384]{1,0:T(8,128)S(1)} %get-tuple-element.39.z, s32[256,128]{1,0:T(8,128)S(1)} %get-tuple-element.40.idx, f32[128,384]{1,0:T(8,128)} %copy-done.2, f32[128,128]{1,0:T(8,128)} %copy-done.5, bf16[256,768]{1,0:T(8,128)(2,1)S(1)} %copy-done.1, bf16[768,256]{1,0:T(8,128)(2,1)S(1)} %copy-done), custom_call_target="tpu_custom_call" | custom-call | tf_op jit(solution)/shard_map/inner/pallas_call | solution.py:126
  29.7 3.1 %all-to-all-done.1.recv = f32[32,8,128]{2,1,0:T(8,128)S(1)} async-done(((f32[32,8,128]{2,1,0:T(8,128)}), f32[32,8,128]{2,1,0:T(8,128)S(1)}, u32[]{:S(2)}, u32[]{:S(2)}) %all-to-all-start.1) | async-done | bytes 131104 | tf_op jit(solution)/shard_map/all_to_all | solution.py:546
  32.9 3.0 %edge.2 = (f32[1024,128]{1,0:T(8,128)S(1)}, f32[288,1,128]{2,1,0:T(1,128)}) custom-call(s32[1,5]{1,0:T(1,128)} %peer.17, f32[32,8,128]{2,1,0:T(8,128)S(1)} %all-to-all-done.1.recv, f32[8,16384]{1,0:T(8,128)S(1)} %get-tuple-element.39.z, s32[256,128]{1,0:T(8,128)S(1)} %get-tuple-element.40.idx, f32[128,384]{1,0:T(8,128)S(1)} %get-tuple-element.41.st, ...), custom_call_target="tpu_custom_call" | custom-call | tf_op jit(solution)/shard_map/edge/pallas_call | solution.py:126
  35.9 0.0 copy-start.3
  35.9 0.8 copy-done.3
  36.7 2.8 %all-to-all-start.2 = ((f32[288,1,128]{2,1,0:T(1,128)}), f32[288,1,128]{2,1,0:T(1,128)S(1)}, u32[]{:S(2)}, u32[]{:S(2)}) async-start(f32[288,1,128]{2,1,0:T(1,128)} %get-tuple-element.48), calls=%async_computation.2 | async-start | bytes 294912 | tf_op jit(solution)/shard_map/all_to_all | solution.py:546
  39.4 0.0 copy-start.4
  39.4 1.0 %copy-done.4 = f32[1024,128]{1,0:T(8,128)S(1)} copy-done((f32[1024,128]{1,0:T(8,128)S(1)}, f32[1024,128]{1,0:T(8,128)}, u32[]{:S(2)}) %copy-start.4) | copy-done | bytes 524312
  40.5 3.0 %edge_scatter_pick.1 = (f32[8,16384]{1,0:T(8,128)S(1)}, f32[8,640]{1,0:T(8,128)S(1)}) custom-call(s32[5,1,128]{2,1,0:T(1,128)} %bitcast.5, s32[5,1,128]{2,1,0:T(1,128)} %bitcast.6, f32[1024,128]{1,0:T(8,128)S(1)} %copy-done.4, s32[256,128]{1,0:T(8,128)S(1)} %get-tuple-element.40.idx, f32[8,8192]{1,0:T(8,128)S(1)} %get-tuple-element.51.inner), custom_call_target="tpu_custom_call" | custom-call | tf_op jit(solution)/shard_map/edge_scatter_pick/pallas_call | solution.py:126
  43.5 0.0 copy-start.8
  43.5 0.6 copy-done.8
  44.1 3.8 %all-to-all-done.2.recv = f32[288,1,128]{2,1,0:T(1,128)S(1)} async-done(((f32[288,1,128]{2,1,0:T(1,128)}), f32[288,1,128]{2,1,0:T(1,128)S(1)}, u32[]{:S(2)}, u32[]{:S(2)}) %all-to-all-start.2) | async-done | bytes 147488 | tf_op jit(solution)/shard_map/all_to_all | solution.py:546
  47.8 0.0 copy-start.7
  47.8 0.7 copy-done.7
  48.6 0.0 copy-start.9
  48.6 0.7 copy-done.9
  49.3 1.7 %step.1 = (f32[32,8,128]{2,1,0:T(8,128)}, f32[2,8,128]{2,1,0:T(8,128)S(1)}) custom-call(s32[1,5]{1,0:T(1,128)} %peer.17, f32[288,1,128]{2,1,0:T(1,128)S(1)} %all-to-all-done.2.recv, f32[8,640]{1,0:T(8,128)S(1)} %get-tuple-element.34.right_at, f32[8,640]{1,0:T(8,128)S(1)} %copy-done.7, f32[8,640]{1,0:T(8,128)S(1)} %copy-done.9, ...), custom_call_target="tpu_custom_call" | custom-call | tf_op jit(solution)/shard_map/step/pallas_call | solution.py:126
  51.0 2.8 %all-to-all-start.3 = ((f32[32,8,128]{2,1,0:T(8,128)}), f32[32,8,128]{2,1,0:T(8,128)S(1)}, u32[]{:S(2)}, u32[]{:S(2)}) async-start(f32[32,8,128]{2,1,0:T(8,128)} %get-tuple-element.53), calls=%async_computation.3 | async-start | bytes 262144 | tf_op jit(solution)/shard_map/all_to_all | solution.py:546
  53.7 1.9 %next_fields.1 = (f32[8,16384]{1,0:T(8,128)S(1)}, f32[8,16384]{1,0:T(8,128)S(1)}, f32[8,128]{1,0:T(8,128)S(1)}) custom-call(s32[1,5]{1,0:T(1,128)} %peer.17, s32[5,1,128]{2,1,0:T(1,128)} %bitcast.7, f32[288,1,128]{2,1,0:T(1,128)S(1)} %all-to-all-done.2.recv, f32[8,16384]{1,0:T(8,128)S(1)} %get-tuple-element.54.own, f32[8,16384]{1,0:T(8,128)} %right_hbm.5, ...), custom_call_target="tpu_custom_call" | custom-call | tf_op jit(solution)/shard_map/next_fields/pallas_call | solution.py:126
  55.7 3.2 %inner.3 = (f32[8,8192]{1,0:T(8,128)S(1)}, f32[8,128]{1,0:T(8,128)S(1)}) custom-call(f32[8,16384]{1,0:T(8,128)S(1)} %get-tuple-element.57.z.z1, s32[256,128]{1,0:T(8,128)S(1)} %get-tuple-element.40.idx, f32[128,384]{1,0:T(8,128)} %copy-done.2, f32[128,128]{1,0:T(8,128)} %copy-done.5, bf16[256,768]{1,0:T(8,128)(2,1)S(1)} %copy-done.1, ...), custom_call_target="tpu_custom_call" | custom-call | tf_op jit(solution)/shard_map/inner/pallas_call | solution.py:126
  58.8 2.9 %all-to-all-done.3.recv = f32[32,8,128]{2,1,0:T(8,128)S(1)} async-done(((f32[32,8,128]{2,1,0:T(8,128)}), f32[32,8,128]{2,1,0:T(8,128)S(1)}, u32[]{:S(2)}, u32[]{:S(2)}) %all-to-all-start.3) | async-done | bytes 131104 | tf_op jit(solution)/shard_map/all_to_all | solution.py:546
  61.8 3.0 %edge.3 = (f32[1024,128]{1,0:T(8,128)S(1)}, f32[288,1,128]{2,1,0:T(1,128)}) custom-call(s32[1,5]{1,0:T(1,128)} %peer.17, f32[32,8,128]{2,1,0:T(8,128)S(1)} %all-to-all-done.3.recv, f32[8,16384]{1,0:T(8,128)S(1)} %get-tuple-element.57.z.z1, s32[256,128]{1,0:T(8,128)S(1)} %get-tuple-element.40.idx, f32[128,384]{1,0:T(8,128)S(1)} %get-tuple-element.41.st, ...), custom_call_target="tpu_custom_call" | custom-call | tf_op jit(solution)/shard_map/edge/pallas_call | solution.py:126
  64.8 2.8 %all-to-all-start.4 = ((f32[288,1,128]{2,1,0:T(1,128)}), f32[288,1,128]{2,1,0:T(1,128)S(1)}, u32[]{:S(2)}, u32[]{:S(2)}) async-start(f32[288,1,128]{2,1,0:T(1,128)} %get-tuple-element.60), calls=%async_computation.4 | async-start | bytes 294912 | tf_op jit(solution)/shard_map/all_to_all | solution.py:546
  67.6 1.2 %edge_scatter.1.own = f32[8,16384]{1,0:T(8,128)S(1)} custom-call(f32[1024,128]{1,0:T(8,128)S(1)} %get-tuple-element.61.result, s32[256,128]{1,0:T(8,128)S(1)} %get-tuple-element.40.idx, f32[8,8192]{1,0:T(8,128)S(1)} %get-tuple-element.62.inner), custom_call_target="tpu_custom_call" | custom-call | tf_op jit(solution)/shard_map/edge_scatter/pallas_call | solution.py:126
  68.8 7.2 %all-to-all-done.4.recv = f32[288,1,128]{2,1,0:T(1,128)S(1)} async-done(((f32[288,1,128]{2,1,0:T(1,128)}), f32[288,1,128]{2,1,0:T(1,128)S(1)}, u32[]{:S(2)}, u32[]{:S(2)}) %all-to-all-start.4) | async-done | bytes 147488 | tf_op jit(solution)/shard_map/all_to_all | solution.py:546
  76.0 3.7 %last.1 = (f32[8,16384]{1,0:T(8,128)}, f32[8,16384]{1,0:T(8,128)}) custom-call(s32[1,5]{1,0:T(1,128)} %peer.17, s32[5,1,128]{2,1,0:T(1,128)} %bitcast.8, f32[288,1,128]{2,1,0:T(1,128)S(1)} %all-to-all-done.4.recv, f32[8,16384]{1,0:T(8,128)S(1)} %edge_scatter.1.own, f32[8,16384]{1,0:T(8,128)} %right_hbm.5, f32[128,128]{1,0:T(8,128)S(1)} %get-tuple-element.55.inverse, ...), custom_call_target="tpu_custom_call" | custom-call | tf_op jit(solution)/shard_map/last/pallas_call | solution.py:126
Async XLA Ops:
  2.9 14.4 %all-to-all-start = ((f32[32,1,128]{2,1,0:T(1,128)}), f32[32,1,128]{2,1,0:T(1,128)S(1)}, u32[]{:S(2)}, u32[]{:S(2)}) async-start(f32[32,1,128]{2,1,0:T(1,128)} %get-tuple-element.33), calls=%async_computation | async-start | bytes 32768 | tf_op jit(solution)/shard_map/all_to_all | solution.py:546
  15.0 0.7 copy-start.2
  15.7 0.6 copy-start.5
  19.2 0.6 copy-start.6
  19.8 6.8 %copy-start = (bf16[768,256]{1,0:T(8,128)(2,1)S(1)}, bf16[768,256]{1,0:T(8,128)(2,1)}, u32[]{:S(2)}) copy-start(bf16[768,256]{1,0:T(8,128)(2,1)} %constant.7.clone.w2) | copy-start | bytes 1179652
  19.8 6.8 %copy-start.1 = (bf16[256,768]{1,0:T(8,128)(2,1)S(1)}, bf16[256,768]{1,0:T(8,128)(2,1)}, u32[]{:S(2)}) copy-start(bf16[256,768]{1,0:T(8,128)(2,1)} %constant.6.clone.w1) | copy-start | bytes 1179652
  19.8 13.1 %all-to-all-start.1 = ((f32[32,8,128]{2,1,0:T(8,128)}), f32[32,8,128]{2,1,0:T(8,128)S(1)}, u32[]{:S(2)}, u32[]{:S(2)}) async-start(f32[32,8,128]{2,1,0:T(8,128)} %get-tuple-element.37), calls=%async_computation.1 | async-start | bytes 262144 | tf_op jit(solution)/shard_map/all_to_all | solution.py:546
  35.9 0.8 copy-start.3
  36.7 11.2 %all-to-all-start.2 = ((f32[288,1,128]{2,1,0:T(1,128)}), f32[288,1,128]{2,1,0:T(1,128)S(1)}, u32[]{:S(2)}, u32[]{:S(2)}) async-start(f32[288,1,128]{2,1,0:T(1,128)} %get-tuple-element.48), calls=%async_computation.2 | async-start | bytes 294912 | tf_op jit(solution)/shard_map/all_to_all | solution.py:546
  39.4 1.0 %copy-start.4 = (f32[1024,128]{1,0:T(8,128)S(1)}, f32[1024,128]{1,0:T(8,128)}, u32[]{:S(2)}) copy-start(f32[1024,128]{1,0:T(8,128)} %copy-done.3) | copy-start | bytes 1572868
  43.5 0.6 copy-start.8
  47.8 0.7 copy-start.7
  48.6 0.7 copy-start.9
  51.0 10.8 %all-to-all-start.3 = ((f32[32,8,128]{2,1,0:T(8,128)}), f32[32,8,128]{2,1,0:T(8,128)S(1)}, u32[]{:S(2)}, u32[]{:S(2)}) async-start(f32[32,8,128]{2,1,0:T(8,128)} %get-tuple-element.53), calls=%async_computation.3 | async-start | bytes 262144 | tf_op jit(solution)/shard_map/all_to_all | solution.py:546
  64.8 11.2 %all-to-all-start.4 = ((f32[288,1,128]{2,1,0:T(1,128)}), f32[288,1,128]{2,1,0:T(1,128)S(1)}, u32[]{:S(2)}, u32[]{:S(2)}) async-start(f32[288,1,128]{2,1,0:T(1,128)} %get-tuple-element.60), calls=%async_computation.4 | async-start | bytes 294912 | tf_op jit(solution)/shard_map/all_to_all | solution.py:546
where the time goes:
time: 80.7 us; the launch traced here: 79.8 us
  Pallas kernels  34.7 us (43%)
  starting transfers between devices  20.5 us (25%)
  waiting for transfers between devices  18 us (22%)
  local copies, waits for them, and re-layouts  5.78 us (7%)
  between operations  0.91 us (1%)
    pallas_call x13, Pallas kernels, run(): kernel(*[pltpu.with_memory_space_constraint(operand, pltpu.VMEM if k in r...  34.7 us
    all_to_all x5, starting transfers between devices, exchange(): lax.all_to_all(values, 'dom', split_axis=0, concat_axis=0, tiled=True)  20.5 us
    all_to_all x5, waiting for transfers between devices, exchange(): lax.all_to_all(values, 'dom', split_axis=0, concat_axis=0, tiled=True)  18 us
    unnamed x20, local copies, waits for them, and re-layouts  5.78 us
  transfers between devices with their start and end apart: 5, of which 5 were waited for; matrix products, arithmetic and copies ran while one was open for 0% of the time, Pallas kernels for 24%

commit v1 on v0

--- a/solution.py
+++ b/solution.py
@@ -56,9 +56,8 @@
     for d in range(3):
         grad[:NPE, d * LANES : d * LANES + NPE] = mats[d].T
     high, low = split_np(grad)
-    first = np.block([[high, low], [high, np.zeros_like(low)]])
-    back_high, back_low = high.T, low.T
-    second = np.block([[back_high, back_low], [back_high, back_low]])
+    first = np.concatenate([high, low], axis=1)
+    second = np.concatenate([high.T, low.T], axis=1)
     squares = np.stack(split_np(np.stack([m.T * m.T for m in mats])))
     return jnp.asarray(first), jnp.asarray(second), jnp.asarray(squares)
 
@@ -107,15 +106,15 @@
     return pl.BlockSpec(memory_space=pltpu.HBM)
 
 
-def call(body, name, in_specs, outs, stay, scratch=(), resident=(), grid=()):
+def call(body, name, in_specs, outs, stay, scratch=(), resident=(), grid=(), out_specs=None):
     kernel = pl.pallas_call(
         body,
         name=name,
         grid=grid,
         in_specs=in_specs,
-        out_specs=tuple(vmem() for _ in outs),
+        out_specs=out_specs or tuple(vmem() for _ in outs),
         out_shape=tuple(
-            pltpu.VMEM(shape, dtype) if k in stay else jax.ShapeDtypeStruct(shape, dtype)
+            (pltpu.VMEM if k in stay else pltpu.HBM)(shape, dtype)
             for k, (shape, dtype) in enumerate(outs)
         ),
         scratch_shapes=list(scratch),
@@ -145,7 +144,16 @@
     return term, total
 
 
-def ghost_diag_body(cfg, peer, density, nodes, stiff, mass, region, squares, send, pos):
+def ghost_diag_body(
+    cfg, peer, density, nodes, stiff, mass, region, squares, shared, send, pos, peer_row, base, node_row
+):
+    lanes = iota((1, LANES), 1)
+    row = jnp.zeros((1, LANES), jnp.int32)
+    for p in range(cfg["peers"]):
+        row = jnp.where(lanes == p, peer[0, p], row)
+        base[p] = shared[p] & (-LANES)
+        node_row[:, p * LANES : (p + 1) * LANES] = shared[p]
+    peer_row[...] = row
     run = cfg["run"]
     _, edge = element_sums(mass[...], region[...], density, stiff, squares)
     code = codes_of(nodes[...], 0, peer, cfg["own"], cfg["peers"], cfg["window"])
@@ -174,7 +182,7 @@
 
 
 def tables_body(
-    cfg, peer, density, nodes, stiff, mass, region, squares, send_s, send_v, right,
+    cfg, peer, density, nodes, stiff, mass, region, squares, base_s, node_row, right,
     idx, st_edge, mt_edge, st_inner, mt_inner, own_diag, right_at, diag_at, same,
     code_pad, value_pad, rows,
 ):
@@ -204,8 +212,8 @@
     value_pad[:NPE] = term
     mt_edge[...] = value_pad[:, :LANES].T
     mt_inner[...] = value_pad[:, LANES:].T
-    pick(cfg, right, send_s, send_v, right_at)
-    node = slot_nodes(cfg, send_v)
+    pick(cfg, right, base_s, node_row, right_at)
+    node = node_row[...]
     wide = node.shape[1]
     hot = jnp.where(iota((LANES, wide), 0) == (node & (LANES - 1)), 1.0, 0.0).astype(jnp.bfloat16)
     here = iota((LANES, wide), 0) == (node >> 7)
@@ -215,10 +223,10 @@
         at_slots = at_slots + jnp.sum(jnp.where(here, seen, 0.0), axis=0, keepdims=True)
     diag_at[...] = spread(at_slots)
     for p in range(cfg["peers"]):
-        column = jnp.broadcast_to(send_v[p], (LANES, LANES)).T
+        column = jnp.broadcast_to(node[:, p * LANES : (p + 1) * LANES], (LANES, LANES)).T
         for q in range(cfg["peers"]):
             same[p * LANES : (p + 1) * LANES, q * LANES : (q + 1) * LANES] = jnp.where(
-                column == send_v[q], 1.0, 0.0
+                column == node[:, q * LANES : (q + 1) * LANES], 1.0, 0.0
             ).astype(jnp.bfloat16)
 
 
@@ -233,19 +241,20 @@
     return sums[:ROWS] + sums[ROWS:]
 
 
-def pick(cfg, field, send_s, send_v, out):
+def peers_of(cfg, peer_row):
+    lane = iota((1, LANES), 1)
+    return [jnp.max(jnp.where(lane == p, peer_row[...], 0)) for p in range(cfg["peers"])]
+
+
+def pick(cfg, field, base_s, node_row, out):
     lane = iota((ROWS, LANES), 1)
     for p in range(cfg["peers"]):
-        low = spread(send_v[p] & (LANES - 1))
+        low = spread(node_row[:, p * LANES : (p + 1) * LANES] & (LANES - 1))
         got = jnp.zeros((ROWS, LANES), jnp.float32)
         for c in range(LANES):
-            base = pl.multiple_of((send_s[p, 0, c] >> 7) * LANES, LANES)
+            base = pl.multiple_of(base_s[p, 0, c], LANES)
             got = jnp.where(lane == c, take(field[:, pl.ds(base, LANES)], low), got)
         out[:, p * LANES : (p + 1) * LANES] = got
-
-
-def slot_nodes(cfg, send_v):
-    return jnp.concatenate([send_v[p] for p in range(cfg["peers"])], axis=1)
 
 
 def nt_dot(left, right):
@@ -262,23 +271,24 @@
 
 
 def received_diag(cfg, peer, recv):
-    return jnp.concatenate([recv[peer[0, p]] for p in range(cfg["peers"])], axis=1)
+    return jnp.concatenate([recv[peer[p]] for p in range(cfg["peers"])], axis=1)
 
 
 def received_rows(cfg, peer, recv):
     blocks = []
     for p in range(cfg["peers"]):
-        first = peer[0, p] * (ROWS + 1)
+        first = peer[p] * (ROWS + 1)
         blocks.append(jnp.concatenate([recv[first + v] for v in range(ROWS)], axis=0))
     return jnp.concatenate(blocks, axis=1)
 
 
 def put_slots(cfg, peer, values, out):
     for p in range(cfg["peers"]):
-        out[peer[0, p]] = values[:, p * LANES : (p + 1) * LANES]
-
-
-def start_body(cfg, peer, recv, right_at, diag_at, same, out, inverse_at):
+        out[peer[p]] = values[:, p * LANES : (p + 1) * LANES]
+
+
+def start_body(cfg, peer_row, recv, right_at, diag_at, same, out, inverse_at):
+    peer = peers_of(cfg, peer_row)
     got = spread(received_diag(cfg, peer, recv))
     top, middle, bottom = parts_of(got, 3)
     both = jnp.concatenate([top, middle], axis=0).astype(jnp.bfloat16)
@@ -291,18 +301,16 @@
     put_slots(cfg, peer, right_at[...] * inverse, out)
 
 
-def first_fields_body(cfg, peer, send_v, recv, own_diag, right_hbm, inverse, z, energy, right, arrived):
-    fetch = pltpu.make_async_copy(right_hbm, right, arrived)
-    fetch.start()
+def first_fields_body(cfg, peer_row, node_row, recv, own_diag, right, inverse, z, energy):
+    peer = peers_of(cfg, peer_row)
     windows = cfg["pairs"]
-    node, got = slot_nodes(cfg, send_v), received_diag(cfg, peer, recv)
+    node, got = node_row[...], received_diag(cfg, peer, recv)
     here = iota((windows, got.shape[1]), 0) == (node >> 7)
     hot = jnp.where(iota((LANES, got.shape[1]), 0) == (node & (LANES - 1)), 1.0, 0.0).astype(jnp.bfloat16)
     total = own_diag[...]
     for part in parts_of(got, 3):
         total = total + nt_dot(jnp.where(here, spread(part, windows), 0.0).astype(jnp.bfloat16), hot)
     inverse[...] = 1.0 / total
-    fetch.wait()
     acc = jnp.zeros((ROWS, LANES), jnp.float32)
     for g in range(windows):
         cols = slice(g * LANES, (g + 1) * LANES)
@@ -326,6 +334,15 @@
     both = jnp.dot(halves(flux), weights2[...], preferred_element_type=jnp.float32)
     lumped = (values.reshape(count, ROWS, LANES) * mt[:, None, :]).reshape(count * ROWS, LANES)
     return both[:, :LANES] + both[:, LANES:] + lumped
+
+
+def fill_weights(weights1, weights2, both1, both2):
+    wide = 3 * LANES
+    both1[:LANES] = weights1[...]
+    both1[LANES:, :wide] = weights1[:, :wide]
+    both1[LANES:, wide:] = jnp.zeros((LANES, wide), jnp.bfloat16)
+    both2[:wide] = weights2[...]
+    both2[wide:] = weights2[...]
 
 
 CHUNK = 64
@@ -343,14 +360,16 @@
     return acc
 
 
-def scatter_half(result, idx, out, first_pair, pair_count):
-    for g in range(pair_count):
-        e = 2 * g * ROWS
-        rows = jnp.concatenate([result[e : e + ROWS], result[e + ROWS : e + 2 * ROWS]], axis=1)
-        out[:, g * LANES : (g + 1) * LANES] = scatter_rows(rows, idx, first_pair + g)
-
-
-def inner_body(cfg, z, idx, st, mt, w1, w2, out, curve, values, result):
+def scatter_half(edge, inner, idx, out):
+    count = edge.shape[0] // (2 * ROWS)
+    for g in range(idx.shape[0] // 2):
+        half, e = (edge, 2 * g * ROWS) if g < count else (inner, 2 * (g - count) * ROWS)
+        rows = jnp.concatenate([half[e : e + ROWS], half[e + ROWS : e + 2 * ROWS]], axis=1)
+        out[:, g * LANES : (g + 1) * LANES] = scatter_rows(rows, idx, g)
+
+
+def inner_body(cfg, z, idx, st, mt, w1, w2, result, curve, values, both1, both2):
+    fill_weights(w1, w2, both1, both2)
     edge, pairs = cfg["edge_pairs"], cfg["pairs"]
     for g in range(edge, pairs):
         window = z[:, g * LANES : (g + 1) * LANES]
@@ -358,14 +377,17 @@
             e = 2 * g + parity
             at = (e - 2 * edge) * ROWS
             values[at : at + ROWS] = take(window, spread(idx[e : e + 1, :] & (LANES - 1)))
-    curve[...] = apply_half(values, result, st, mt, w1, w2)
-    scatter_half(result, idx, out, edge, pairs - edge)
-
-
-def edge_body(cfg, peer, recv, z, idx, st, mt, pos, w1, w2, energy, curve, result, out, values, ghosts):
+    curve[...] = apply_half(values, result, st, mt, both1, both2)
+
+
+def edge_body(
+    cfg, peer_row, recv, z, idx, st, mt, pos, w1, w2, energy, curve, result, out, values, ghosts, both1, both2
+):
+    peer = peers_of(cfg, peer_row)
+    fill_weights(w1, w2, both1, both2)
     run, edge, peers = cfg["run"], cfg["edge_pairs"], cfg["peers"]
     for p in range(peers):
-        ghosts[p] = recv[peer[0, p]]
+        ghosts[p] = recv[peer[p]]
     spans = []
     for g in range(edge):
         low, high = run * g // LANES, (run * (g + 1) - 1) // LANES
@@ -379,7 +401,7 @@
             if high > low:
                 got = jnp.where(code < LANES * (high + 1), got, take(ghosts[high], at))
             values[e * ROWS : (e + 1) * ROWS] = jnp.where(code < LANES, take(window, at), got)
-    acc = apply_half(values, result, st, mt, w1, w2) + curve[...]
+    acc = apply_half(values, result, st, mt, both1, both2) + curve[...]
     lane = iota((ROWS, LANES), 1)
     sums = [jnp.zeros((ROWS, LANES), jnp.float32) for _ in range(peers)]
     for g in range(edge):
@@ -401,23 +423,21 @@
         out[n * (ROWS + 1) + ROWS] = dots
     for p in range(peers):
         for v in range(ROWS):
-            out[peer[0, p] * (ROWS + 1) + v] = sums[p][v : v + 1]
+            out[peer[p] * (ROWS + 1) + v] = sums[p][v : v + 1]
 
 
 def edge_scatter_body(cfg, result, idx, inner, out):
-    split = cfg["edge_pairs"] * LANES
-    scatter_half(result, idx, out, 0, cfg["edge_pairs"])
-    out[:, split:] = inner[...]
-
-
-def edge_scatter_pick_body(cfg, send_s, send_v, result, idx, inner, out, at_slots):
+    scatter_half(result, inner, idx, out)
+
+
+def edge_scatter_pick_body(cfg, base_s, node_row, result, idx, inner, out, at_slots):
     edge_scatter_body(cfg, result, idx, inner, out)
-    pick(cfg, out, send_s, send_v, at_slots)
-
-
-def returned_sums(cfg, peer, send_v, recv, left, hot):
+    pick(cfg, out, base_s, node_row, at_slots)
+
+
+def returned_sums(cfg, peer, node_row, recv, left, hot):
     windows = cfg["pairs"]
-    node, value = slot_nodes(cfg, send_v), received_rows(cfg, peer, recv)
+    node, value = node_row[...], received_rows(cfg, peer, recv)
     wide = node.shape[1]
     high, low = parts_of(value, 2)
     lanes = jnp.where(iota((LANES, wide), 0) == (node & (LANES - 1)), 1.0, 0.0).astype(jnp.bfloat16)
@@ -450,7 +470,8 @@
     ]
 
 
-def step_body(cfg, peer, recv, right_at, inverse_at, image_at, same, out, coefs):
+def step_body(cfg, peer_row, recv, right_at, inverse_at, image_at, same, out, coefs):
+    peer = peers_of(cfg, peer_row)
     energy_now, curve_now = dot_totals(recv)
     alpha = energy_now / curve_now
     coefs[0] = alpha
@@ -468,14 +489,19 @@
 
 
 def next_fields_body(
-    cfg, peer, send_v, recv, own, right_hbm, inverse, coefs, w, z1, energy, left, hot, sums, right, arrived
+    cfg, peer_row, node_row, recv, own_hbm, right_hbm, inverse, coefs, w, z1, energy, left, hot, sums, right, own, arrived
 ):
-    fetch = pltpu.make_async_copy(right_hbm, right, arrived)
-    fetch.start()
+    fetches = [
+        pltpu.make_async_copy(there, here, arrived.at[k]) for k, (there, here) in enumerate(((right_hbm, right), (own_hbm, own)))
+    ]
+    for fetch in fetches:
+        fetch.start()
+    peer = peers_of(cfg, peer_row)
     windows = cfg["pairs"]
-    sums[...] = returned_sums(cfg, peer, send_v, recv, left, hot)
+    sums[...] = returned_sums(cfg, peer, node_row, recv, left, hot)
     alpha = coefs[0]
-    fetch.wait()
+    for fetch in fetches:
+        fetch.wait()
     acc = jnp.zeros((ROWS, LANES), jnp.float32)
     for g in range(windows):
         cols = slice(g * LANES, (g + 1) * LANES)
@@ -488,19 +514,28 @@
     energy[...] = acc
 
 
+LAST_STEP = 32
+
+
 def last_body(
-    cfg, peer, send_v, recv, own, right_hbm, inverse, w, z1, coefs,
-    solution, residual, left, hot, sums, right, arrived,
+    cfg, peer_row, node_row, recv, own, right_hbm, inverse, w_hbm, z1, coefs,
+    solution_hbm, residual_hbm, left, hot, sums, right, w, arrived, solution, residual, sent,
 ):
-    fetch = pltpu.make_async_copy(right_hbm, right, arrived)
-    fetch.start()
+    fetches = [
+        pltpu.make_async_copy(there, here, arrived.at[k]) for k, (there, here) in enumerate(((right_hbm, right), (w_hbm, w)))
+    ]
+    for fetch in fetches:
+        fetch.start()
+    peer = peers_of(cfg, peer_row)
     windows = cfg["pairs"]
-    sums[...] = returned_sums(cfg, peer, send_v, recv, left, hot)
+    sums[...] = returned_sums(cfg, peer, node_row, recv, left, hot)
     energy_next, curve_next = dot_totals(recv)
     alpha, energy_now = coefs[0], coefs[1]
     beta = energy_next / energy_now
     step = energy_next / (curve_next - beta * energy_next / alpha)
-    fetch.wait()
+    copies = []
+    for fetch in fetches:
+        fetch.wait()
     for g in range(windows):
         cols = slice(g * LANES, (g + 1) * LANES)
         image = own[:, cols] + sums[g * ROWS : (g + 1) * ROWS]
@@ -508,6 +543,15 @@
         z0 = start * spread(inverse[g : g + 1, :])
         residual[:, cols] = (start - alpha * before) - step * (image + beta * before)
         solution[:, cols] = alpha * z0 + step * (z1[:, cols] + beta * z0)
+        if (g + 1) % LAST_STEP == 0:
+            done = slice((g + 1 - LAST_STEP) * LANES, (g + 1) * LANES)
+            for k, (here, there) in enumerate(((solution, solution_hbm), (residual, residual_hbm))):
+                copies.append(
+                    pltpu.make_async_copy(here.at[:, done], there.at[:, done], sent.at[g // LAST_STEP, k])
+                )
+                copies[-1].start()
+    for copy in copies:
+        copy.wait()
 
 
 def on_device(right_side, stiffness, mass, region, density, elem_nodes, peer_rank, send_nodes):
@@ -534,7 +578,6 @@
     weights1, weights2, squares = constant_operands()
     V, S = vmem(), smem()
     field = ((vectors, own_count), f32)
-    half_field = ((vectors, own_count // 2), f32)
     tile = ((ROWS, LANES), f32)
     square = ((LANES, LANES), f32)
     half_rows = ((elem_count // 2 * ROWS, LANES), f32)
@@ -552,12 +595,16 @@
         pl.BlockSpec((NPE, LANES), lambda _: (0, 0)),
         pl.BlockSpec((1, LANES), lambda _: (0, 0)),
     ]
-    send, pos = call(
-        bind(ghost_diag_body), "ghost_diag", [S, S, *half_specs, V],
-        [((devices, 1, LANES), f32), ((ROWS, LANES), i32)], (1,), grid=(1,),
-    )(peer_rank, density, elem_nodes, stiffness, mass, regions, squares)
+    shared = jnp.transpose(send_nodes, (1, 0, 2))
+    send, pos, peer_row, base, node_row = call(
+        bind(ghost_diag_body), "ghost_diag", [S, S, *half_specs, V, V],
+        [
+            ((devices, 1, LANES), f32), ((ROWS, LANES), i32), ((1, LANES), i32), ((peers, 1, slots), i32),
+            ((1, peers * slots), i32),
+        ],
+        (1, 2, 4), grid=(1,),
+    )(peer_rank, density, elem_nodes, stiffness, mass, regions, squares, shared)
     recv = exchange(send)
-    shared = jnp.transpose(send_nodes, (1, 0, 2))
     slots_all = ((vectors, peers * slots), f32)
     edge_count = elem_count // 2
     idx, st_edge, mt_edge, st_inner, mt_inner, own_diag, right_at, diag_at, same = call(
@@ -573,55 +620,59 @@
             pltpu.VMEM((LANES, elem_count), i32), pltpu.VMEM((LANES, elem_count), f32),
             pltpu.VMEM((elem_count, LANES), f32),
         ],
-    )(peer_rank, density, elem_nodes, stiffness, mass, regions, squares, shared, shared, right_side)
+        (8,),
+    )(peer_rank, density, elem_nodes, stiffness, mass, regions, squares, base, node_row, right_side)
 
     send_shape = ((devices, ROWS, LANES), f32)
-    copied = [pltpu.VMEM(*field), pltpu.SemaphoreType.DMA(())]
     send, inverse_at = call(
-        bind(start_body), "start", [S] + [V] * 4, [send_shape, slots_all], (1,), (), (1, 2, 3, 4)
-    )(peer_rank, recv, right_at, diag_at, same)
+        bind(start_body), "start", [V] * 5, [send_shape, slots_all], (1,), (), range(5)
+    )(peer_row, recv, right_at, diag_at, same)
     diag_recv = recv
     recv = exchange(send)
     inverse, z, energy = call(
-        bind(first_fields_body), "first_fields", [S, V, V, V, hbm()], [square, field, tile], range(3),
-        copied, (2, 3),
-    )(peer_rank, shared, diag_recv, own_diag, right_side)
+        bind(first_fields_body), "first_fields", [V] * 5, [square, field, tile], range(3), (), range(5),
+    )(peer_row, node_row, diag_recv, own_diag, right_side)
+
+    weight_rows = [
+        pltpu.VMEM((2 * LANES, 6 * LANES), jnp.bfloat16), pltpu.VMEM((6 * LANES, 2 * LANES), jnp.bfloat16)
+    ]
 
     def inner_part(z):
         return call(
-            bind(inner_body), "inner", [V] * 6, [half_field, tile], range(2),
-            [pltpu.VMEM(*half_rows), pltpu.VMEM(*half_rows)], (0, 1, 4, 5),
+            bind(inner_body), "inner", [V] * 6, [half_rows, tile], range(2),
+            [pltpu.VMEM(*half_rows), *weight_rows], (0, 1, 4, 5),
         )(z, idx, st_inner, mt_inner, weights1, weights2)
 
     def edge_part(recv, z, energy, curve):
         return call(
-            bind(edge_body), "edge", [S] + [V] * 10,
+            bind(edge_body), "edge", [V] * 11,
             [half_rows, ((devices * (ROWS + 1), 1, LANES), f32)], (0,),
-            [pltpu.VMEM(*half_rows), pltpu.VMEM((peers, ROWS, LANES), f32)], range(1, 11),
-        )(peer_rank, recv, z, idx, st_edge, mt_edge, pos, weights1, weights2, energy, curve)
+            [pltpu.VMEM(*half_rows), pltpu.VMEM((peers, ROWS, LANES), f32), *weight_rows], range(11),
+        )(peer_row, recv, z, idx, st_edge, mt_edge, pos, weights1, weights2, energy, curve)
 
     wide = 2 * peers * slots
     scratch = [
         pltpu.VMEM((vectors * pairs, wide), jnp.bfloat16), pltpu.VMEM((LANES, wide), jnp.bfloat16),
-        pltpu.VMEM((vectors * pairs, LANES), f32), *copied,
+        pltpu.VMEM((vectors * pairs, LANES), f32), pltpu.VMEM(*field), pltpu.VMEM(*field),
+        pltpu.SemaphoreType.DMA((2,)),
     ]
     inner, curve = inner_part(z)
     result, send = edge_part(recv, z, energy, curve)
     recv = exchange(send)
     own, image_at = call(
-        bind(edge_scatter_pick_body), "edge_scatter_pick", [S] + [V] * 4, [field, slots_all], range(2), (),
-        (2, 3, 4),
-    )(shared, shared, result, idx, inner)
+        bind(edge_scatter_pick_body), "edge_scatter_pick", [S] + [V] * 4, [field, slots_all], (1,), (),
+        (1, 2, 3, 4),
+    )(base, node_row, result, idx, inner)
     send, coefs = call(
-        bind(step_body), "step", [S] + [V] * 5, [send_shape, ((2, ROWS, LANES), f32)], (1,), (),
-        range(1, 6),
-    )(peer_rank, recv, right_at, inverse_at, image_at, same)
+        bind(step_body), "step", [V] * 6, [send_shape, ((2, ROWS, LANES), f32)], (1,), (),
+        range(6),
+    )(peer_row, recv, right_at, inverse_at, image_at, same)
     sum_recv = recv
     recv = exchange(send)
     w, z, energy = call(
-        bind(next_fields_body), "next_fields", [S] + [V] * 3 + [hbm()] + [V] * 2, [field, field, tile],
-        range(3), scratch, (2, 3, 5, 6),
-    )(peer_rank, shared, sum_recv, own, right_side, inverse, coefs)
+        bind(next_fields_body), "next_fields", [V] * 3 + [hbm(), hbm()] + [V] * 2, [field, field, tile], (1, 2), scratch,
+        (0, 1, 2, 5, 6),
+    )(peer_row, node_row, sum_recv, own, right_side, inverse, coefs)
     inner, curve = inner_part(z)
     result, send = edge_part(recv, z, energy, curve)
     recv = exchange(send)
@@ -629,9 +680,12 @@
         result, idx, inner
     )
     return call(
-        bind(last_body), "last", [S] + [V] * 3 + [hbm()] + [V] * 4, [field, field], (), scratch,
-        (2, 3, 5, 6, 7, 8),
-    )(peer_rank, shared, recv, own, right_side, inverse, w, z, coefs)
+        bind(last_body), "last", [V] * 4 + [hbm(), V, hbm()] + [V] * 2, [field, field], (),
+        scratch + [
+            pltpu.VMEM(*field), pltpu.VMEM(*field), pltpu.SemaphoreType.DMA((pairs // LAST_STEP, 2)),
+        ],
+        (0, 1, 2, 3, 5, 7, 8), out_specs=(hbm(), hbm()),
+    )(peer_row, node_row, recv, own, right_side, inverse, w, z, coefs)
 
 
 def solution(mesh):

time: 80.7 us -> 73.9 us (0.916)
  local copies, waits for them, and re-layouts: 5.78 us -> 0.33 us
  waiting for transfers between devices: 18 us -> 20 us
  Pallas kernels: 34.7 us -> 33.1 us
  starting transfers between devices: 20.5 us -> 19.1 us
    unnamed x20 -> x6, local copies, waits for them, and re-layouts: 5.78 us -> 0.33 us
    all_to_all x5, waiting for transfers between devices: 18 us -> 20 us  [exchange(): lax.all_to_all(values, 'dom', split_axis=0, concat_axis=0, tiled=True)]
    pallas_call x13, Pallas kernels: 34.7 us -> 33.1 us  [run(): kernel(*[pltpu.with_memory_space_constraint(operand, pltpu.VMEM if k in r...]
    all_to_all x5, starting transfers between devices: 20.5 us -> 19.1 us  [exchange(): lax.all_to_all(values, 'dom', split_axis=0, concat_axis=0, tiled=True)]
  transfers between devices with their start and end apart: 5 -> 5, of which waited for: 5 -> 5; matrix products, arithmetic and copies ran while one was open for 0% -> 0% of each run, Pallas kernels for 24% -> 27%
where the time goes in v1:
time: 73.9 us; the launch traced here: 73.4 us
  Pallas kernels  33.1 us (45%)
  waiting for transfers between devices  20 us (27%)
  starting transfers between devices  19.1 us (26%)
  between operations  0.88 us (1%)
    pallas_call x13, Pallas kernels, run(): kernel(*[pltpu.with_memory_space_constraint(operand, pltpu.VMEM if k in r...  33.1 us
    all_to_all x5, waiting for transfers between devices, exchange(): lax.all_to_all(values, 'dom', split_axis=0, concat_axis=0, tiled=True)  20 us
    all_to_all x5, starting transfers between devices, exchange(): lax.all_to_all(values, 'dom', split_axis=0, concat_axis=0, tiled=True)  19.1 us
  transfers between devices with their start and end apart: 5, of which 5 were waited for; matrix products, arithmetic and copies ran while one was open for 0% of the time, Pallas kernels for 27%

profile of v1, /device:TPU:0, one launch (start us, length us, event | category | flops | bytes accessed | tf_op | source)
XLA Modules:
  0.0 73.4 jit_solution(16126440320363986888)
XLA Ops:
  0.6 2.2 %ghost_diag.1 = (f32[32,1,128]{2,1,0:T(1,128)}, s32[8,128]{1,0:T(8,128)S(1)}, s32[1,128]{1,0:T(1,128)S(1)}, s32[5,1,128]{2,1,0:T(1,128)}, s32[1,640]{1,0:T(1,128)S(1)}) custom-call(s32[1,5]{1,0:T(1,128)} %peer.3, f32[3]{0:T(128)} %density.3, s32[125,256]{1,0:T(8,128)} %nodes.3, f32[3,125,256]{2,1,0:T(8,128)} %stiff.3, f32[125,256]{1,0:T(8,128)} %mass.3, ...), custom_call_target="tpu_custom_call" | custom-call | tf_op jit(solution)/shard_map/ghost_diag/pallas_call | solution.py:125
  2.9 7.3 %all-to-all-start = ((f32[32,1,128]{2,1,0:T(1,128)}), f32[32,1,128]{2,1,0:T(1,128)S(1)}, u32[]{:S(2)}, u32[]{:S(2)}) async-start(f32[32,1,128]{2,1,0:T(1,128)} %get-tuple-element.38), calls=%async_computation | async-start | bytes 32768 | tf_op jit(solution)/shard_map/all_to_all | solution.py:589
  10.2 5.1 %tables.1 = (s32[256,128]{1,0:T(8,128)S(1)}, f32[128,384]{1,0:T(8,128)S(1)}, f32[128,128]{1,0:T(8,128)S(1)}, f32[128,384]{1,0:T(8,128)}, f32[128,128]{1,0:T(8,12...) custom-call(s32[1,5]{1,0:T(1,128)} %peer.3, ...), custom_call_target="tpu_custom_call" | custom-call | tf_op jit(solution)/shard_map/tables/pallas_call | solution.py:125
  15.3 2.0 %all-to-all-done.recv = f32[32,1,128]{2,1,0:T(1,128)S(1)} async-done(((f32[32,1,128]{2,1,0:T(1,128)}), f32[32,1,128]{2,1,0:T(1,128)S(1)}, u32[]{:S(2)}, u32[]{:S(2)}) %all-to-all-start) | async-done | bytes 16416 | tf_op jit(solution)/shard_map/all_to_all | solution.py:589
  17.3 0.0 copy-start
  17.3 1.4 %start.1 = (f32[32,8,128]{2,1,0:T(8,128)}, f32[8,640]{1,0:T(8,128)S(1)}) custom-call(s32[1,128]{1,0:T(1,128)S(1)} %get-tuple-element.36.peer_row, f32[32,1,128]{2,1,0:T(1,128)S(1)} %all-to-all-done.recv, f32[8,640]{1,0:T(8,128)S(1)} %get-tuple-element.40.right_at, f32[8,640]{1,0:T(8,128)S(1)} %get-tuple-element.41.diag_at, ...), custom_call_target="tpu_custom_call" | custom-call | tf_op jit(solution)/shard_map/start/pallas_call | solution.py:125
  18.7 3.8 %all-to-all-start.1 = ((f32[32,8,128]{2,1,0:T(8,128)}), f32[32,8,128]{2,1,0:T(8,128)S(1)}, u32[]{:S(2)}, u32[]{:S(2)}) async-start(f32[32,8,128]{2,1,0:T(8,128)} %get-tuple-element.43), calls=%async_computation.1 | async-start | bytes 262144 | tf_op jit(solution)/shard_map/all_to_all | solution.py:589
  22.5 0.0 copy-done
  22.6 0.0 copy-start.1
  22.6 0.0 copy-start.2
  22.6 0.7 first_fields.1
  23.3 0.2 copy-done.1
  23.5 0.1 copy-done.2
  23.6 2.4 %inner.2 = (f32[1024,128]{1,0:T(8,128)S(1)}, f32[8,128]{1,0:T(8,128)S(1)}) custom-call(f32[8,16384]{1,0:T(8,128)S(1)} %get-tuple-element.45.z, s32[256,128]{1,0:T(8,128)S(1)} %get-tuple-element.46.idx, f32[128,384]{1,0:T(8,128)} %get-tuple-element.51.st, f32[128,128]{1,0:T(8,128)} %get-tuple-element.52.mt, bf16[128,768]{1,0:T(8,128)(2,1)S(1)} %copy-done.2, ...), custom_call_target="tpu_custom_call" | custom-call | tf_op jit(solution)/shard_map/inner/pallas_call | solution.py:125
  26.0 4.7 %all-to-all-done.1.recv = f32[32,8,128]{2,1,0:T(8,128)S(1)} async-done(((f32[32,8,128]{2,1,0:T(8,128)}), f32[32,8,128]{2,1,0:T(8,128)S(1)}, u32[]{:S(2)}, u32[]{:S(2)}) %all-to-all-start.1) | async-done | bytes 131104 | tf_op jit(solution)/shard_map/all_to_all | solution.py:589
  30.7 2.7 %edge.2 = (f32[1024,128]{1,0:T(8,128)S(1)}, f32[288,1,128]{2,1,0:T(1,128)}) custom-call(s32[1,128]{1,0:T(1,128)S(1)} %get-tuple-element.36.peer_row, f32[32,8,128]{2,1,0:T(8,128)S(1)} %all-to-all-done.1.recv, f32[8,16384]{1,0:T(8,128)S(1)} %get-tuple-element.45.z, s32[256,128]{1,0:T(8,128)S(1)} %get-tuple-element.46.idx, ...), custom_call_target="tpu_custom_call" | custom-call | tf_op jit(solution)/shard_map/edge/pallas_call | solution.py:125
  33.4 2.6 %all-to-all-start.2 = ((f32[288,1,128]{2,1,0:T(1,128)}), f32[288,1,128]{2,1,0:T(1,128)S(1)}, u32[]{:S(2)}, u32[]{:S(2)}) async-start(f32[288,1,128]{2,1,0:T(1,128)} %get-tuple-element.54), calls=%async_computation.2 | async-start | bytes 294912 | tf_op jit(solution)/shard_map/all_to_all | solution.py:589
  36.0 4.5 %edge_scatter_pick.1 = (f32[8,16384]{1,0:T(8,128)}, f32[8,640]{1,0:T(8,128)S(1)}) custom-call(s32[5,1,128]{2,1,0:T(1,128)} %get-tuple-element.39.base_s, s32[1,640]{1,0:T(1,128)S(1)} %get-tuple-element.37.node_row, f32[1024,128]{1,0:T(8,128)S(1)} %get-tuple-element.56.result, s32[256,128]{1,0:T(8,128)S(1)} %get-tuple-element.46.idx, ...), custom_call_target="tpu_custom_call" | custom-call | tf_op jit(solution)/shard_map/edge_scatter_pick/pallas_call | solution.py:125
  40.4 4.0 %all-to-all-done.2.recv = f32[288,1,128]{2,1,0:T(1,128)S(1)} async-done(((f32[288,1,128]{2,1,0:T(1,128)}), f32[288,1,128]{2,1,0:T(1,128)S(1)}, u32[]{:S(2)}, u32[]{:S(2)}) %all-to-all-start.2) | async-done | bytes 147488 | tf_op jit(solution)/shard_map/all_to_all | solution.py:589
  44.4 1.2 %step.1 = (f32[32,8,128]{2,1,0:T(8,128)}, f32[2,8,128]{2,1,0:T(8,128)S(1)}) custom-call(s32[1,128]{1,0:T(1,128)S(1)} %get-tuple-element.36.peer_row, f32[288,1,128]{2,1,0:T(1,128)S(1)} %all-to-all-done.2.recv, f32[8,640]{1,0:T(8,128)S(1)} %get-tuple-element.40.right_at, f32[8,640]{1,0:T(8,128)S(1)} %get-tuple-element.55.inverse_at, ...), custom_call_target="tpu_custom_call" | custom-call | tf_op jit(solution)/shard_map/step/pallas_call | solution.py:125
  45.6 2.7 %all-to-all-start.3 = ((f32[32,8,128]{2,1,0:T(8,128)}), f32[32,8,128]{2,1,0:T(8,128)S(1)}, u32[]{:S(2)}, u32[]{:S(2)}) async-start(f32[32,8,128]{2,1,0:T(8,128)} %get-tuple-element.59), calls=%async_computation.3 | async-start | bytes 262144 | tf_op jit(solution)/shard_map/all_to_all | solution.py:589
  48.3 2.4 %next_fields.1 = (f32[8,16384]{1,0:T(8,128)}, f32[8,16384]{1,0:T(8,128)S(1)}, f32[8,128]{1,0:T(8,128)S(1)}) custom-call(s32[1,128]{1,0:T(1,128)S(1)} %get-tuple-element.36.peer_row, s32[1,640]{1,0:T(1,128)S(1)} %get-tuple-element.37.node_row, f32[288,1,128]{2,1,0:T(1,128)S(1)} %all-to-all-done.2.recv, f32[8,16384]{1,0:T(8,128)} %get-tuple-element.60.own_hbm, ...), custom_call_target="tpu_custom_call" | custom-call | tf_op jit(solution)/shard_map/next_fields/pallas_call | solution.py:125
  50.7 2.4 %inner.3 = (f32[1024,128]{1,0:T(8,128)S(1)}, f32[8,128]{1,0:T(8,128)S(1)}) custom-call(f32[8,16384]{1,0:T(8,128)S(1)} %get-tuple-element.63.z.z1, s32[256,128]{1,0:T(8,128)S(1)} %get-tuple-element.46.idx, f32[128,384]{1,0:T(8,128)} %get-tuple-element.51.st, f32[128,128]{1,0:T(8,128)} %get-tuple-element.52.mt, bf16[128,768]{1,0:T(8,128)(2,1)S(1)} %copy-done.2, ...), custom_call_target="tpu_custom_call" | custom-call | tf_op jit(solution)/shard_map/inner/pallas_call | solution.py:125
  53.1 3.2 %all-to-all-done.3.recv = f32[32,8,128]{2,1,0:T(8,128)S(1)} async-done(((f32[32,8,128]{2,1,0:T(8,128)}), f32[32,8,128]{2,1,0:T(8,128)S(1)}, u32[]{:S(2)}, u32[]{:S(2)}) %all-to-all-start.3) | async-done | bytes 131104 | tf_op jit(solution)/shard_map/all_to_all | solution.py:589
  56.3 2.7 %edge.3 = (f32[1024,128]{1,0:T(8,128)S(1)}, f32[288,1,128]{2,1,0:T(1,128)}) custom-call(s32[1,128]{1,0:T(1,128)S(1)} %get-tuple-element.36.peer_row, f32[32,8,128]{2,1,0:T(8,128)S(1)} %all-to-all-done.3.recv, f32[8,16384]{1,0:T(8,128)S(1)} %get-tuple-element.63.z.z1, s32[256,128]{1,0:T(8,128)S(1)} %get-tuple-element.46.idx, ...), custom_call_target="tpu_custom_call" | custom-call | tf_op jit(solution)/shard_map/edge/pallas_call | solution.py:125
  59.0 2.6 %all-to-all-start.4 = ((f32[288,1,128]{2,1,0:T(1,128)}), f32[288,1,128]{2,1,0:T(1,128)S(1)}, u32[]{:S(2)}, u32[]{:S(2)}) async-start(f32[288,1,128]{2,1,0:T(1,128)} %get-tuple-element.66), calls=%async_computation.4 | async-start | bytes 294912 | tf_op jit(solution)/shard_map/all_to_all | solution.py:589
  61.6 2.3 %edge_scatter.1.own = f32[8,16384]{1,0:T(8,128)S(1)} custom-call(f32[1024,128]{1,0:T(8,128)S(1)} %get-tuple-element.67.result, s32[256,128]{1,0:T(8,128)S(1)} %get-tuple-element.46.idx, f32[1024,128]{1,0:T(8,128)S(1)} %get-tuple-element.68.inner), custom_call_target="tpu_custom_call" | custom-call | tf_op jit(solution)/shard_map/edge_scatter/pallas_call | solution.py:125
  63.9 6.1 %all-to-all-done.4.recv = f32[288,1,128]{2,1,0:T(1,128)S(1)} async-done(((f32[288,1,128]{2,1,0:T(1,128)}), f32[288,1,128]{2,1,0:T(1,128)S(1)}, u32[]{:S(2)}, u32[]{:S(2)}) %all-to-all-start.4) | async-done | bytes 147488 | tf_op jit(solution)/shard_map/all_to_all | solution.py:589
  70.0 3.2 %last.1 = (f32[8,16384]{1,0:T(8,128)}, f32[8,16384]{1,0:T(8,128)}) custom-call(s32[1,128]{1,0:T(1,128)S(1)} %get-tuple-element.36.peer_row, s32[1,640]{1,0:T(1,128)S(1)} %get-tuple-element.37.node_row, f32[288,1,128]{2,1,0:T(1,128)S(1)} %all-to-all-done.4.recv, f32[8,16384]{1,0:T(8,128)S(1)} %edge_scatter.1.own, f32[8,16384]{1,0:T(8,128)} %right_hbm.3, ...), custom_call_target="tpu_custom_call" | custom-call | tf_op jit(solution)/shard_map/last/pallas_call | solution.py:125
Async XLA Ops:
  2.9 14.4 %all-to-all-start = ((f32[32,1,128]{2,1,0:T(1,128)}), f32[32,1,128]{2,1,0:T(1,128)S(1)}, u32[]{:S(2)}, u32[]{:S(2)}) async-start(f32[32,1,128]{2,1,0:T(1,128)} %get-tuple-element.38), calls=%async_computation | async-start | bytes 32768 | tf_op jit(solution)/shard_map/all_to_all | solution.py:589
  17.3 5.2 %copy-start = (f32[8,16384]{1,0:T(8,128)S(1)}, f32[8,16384]{1,0:T(8,128)}, u32[]{:S(2)}) copy-start(f32[8,16384]{1,0:T(8,128)} %right_hbm.3) | copy-start | bytes 1572868
  18.7 12.1 %all-to-all-start.1 = ((f32[32,8,128]{2,1,0:T(8,128)}), f32[32,8,128]{2,1,0:T(8,128)S(1)}, u32[]{:S(2)}, u32[]{:S(2)}) async-start(f32[32,8,128]{2,1,0:T(8,128)} %get-tuple-element.43), calls=%async_computation.1 | async-start | bytes 262144 | tf_op jit(solution)/shard_map/all_to_all | solution.py:589
  22.6 0.9 %copy-start.1 = (bf16[384,256]{1,0:T(8,128)(2,1)S(1)}, bf16[384,256]{1,0:T(8,128)(2,1)}, u32[]{:S(2)}) copy-start(bf16[384,256]{1,0:T(8,128)(2,1)} %constant.7.clone.w2) | copy-start | bytes 589828
  22.6 1.0 %copy-start.2 = (bf16[128,768]{1,0:T(8,128)(2,1)S(1)}, bf16[128,768]{1,0:T(8,128)(2,1)}, u32[]{:S(2)}) copy-start(bf16[128,768]{1,0:T(8,128)(2,1)} %constant.6.clone.w1) | copy-start | bytes 589828
  33.4 11.0 %all-to-all-start.2 = ((f32[288,1,128]{2,1,0:T(1,128)}), f32[288,1,128]{2,1,0:T(1,128)S(1)}, u32[]{:S(2)}, u32[]{:S(2)}) async-start(f32[288,1,128]{2,1,0:T(1,128)} %get-tuple-element.54), calls=%async_computation.2 | async-start | bytes 294912 | tf_op jit(solution)/shard_map/all_to_all | solution.py:589
  45.6 10.8 %all-to-all-start.3 = ((f32[32,8,128]{2,1,0:T(8,128)}), f32[32,8,128]{2,1,0:T(8,128)S(1)}, u32[]{:S(2)}, u32[]{:S(2)}) async-start(f32[32,8,128]{2,1,0:T(8,128)} %get-tuple-element.59), calls=%async_computation.3 | async-start | bytes 262144 | tf_op jit(solution)/shard_map/all_to_all | solution.py:589
  59.0 11.0 %all-to-all-start.4 = ((f32[288,1,128]{2,1,0:T(1,128)}), f32[288,1,128]{2,1,0:T(1,128)S(1)}, u32[]{:S(2)}, u32[]{:S(2)}) async-start(f32[288,1,128]{2,1,0:T(1,128)} %get-tuple-element.66), calls=%async_computation.4 | async-start | bytes 294912 | tf_op jit(solution)/shard_map/all_to_all | solution.py:589

commit v2 on v1

--- a/solution.py
+++ b/solution.py
@@ -201,9 +201,13 @@
     term, diag = element_sums(mass[...], region[...], density, stiff, squares)
     value_pad[:NPE] = diag
     rows[...] = turned(value_pad)
-    for g in range(cfg["pairs"]):
-        row = jnp.concatenate([rows[2 * g : 2 * g + 1, :], rows[2 * g + 1 : 2 * g + 2, :]], axis=1)
-        own_diag[g : g + 1, :] = scatter_rows(spread(row), idx, g)[:1]
+    for g in range(0, cfg["pairs"], 2):
+        lines = [
+            spread(jnp.concatenate([rows[2 * k : 2 * k + 1, :], rows[2 * k + 1 : 2 * k + 2, :]], axis=1))
+            for k in (g, g + 1)
+        ]
+        for k, sums in enumerate(scatter_pairs(lines, idx, g)):
+            own_diag[g + k : g + k + 1, :] = sums[:1]
     for d in range(3):
         value_pad[:NPE] = stiff[d]
         cols = slice(d * LANES, (d + 1) * LANES)
@@ -241,6 +245,23 @@
     return sums[:ROWS] + sums[ROWS:]
 
 
+def scatter_pairs(rows, idx, g):
+    node = iota((LANES, LANES), 0)
+    spots = [
+        jnp.concatenate(
+            [jnp.where(node == idx[e : e + 1, :], 1.0, 0.0) for e in (2 * pair, 2 * pair + 1)], axis=1
+        ).astype(jnp.bfloat16)
+        for pair in (g, g + 1)
+    ]
+    parts = []
+    for values in rows:
+        high = values.astype(jnp.bfloat16).astype(jnp.float32)
+        parts += [high, values - high]
+    sums = nt_dot(jnp.concatenate(parts, axis=0).astype(jnp.bfloat16), jnp.concatenate(spots, axis=0))
+    own = (sums[: 2 * ROWS, :LANES], sums[2 * ROWS :, LANES:])
+    return [x[:ROWS] + x[ROWS:] for x in own]
+
+
 def peers_of(cfg, peer_row):
     lane = iota((1, LANES), 1)
     return [jnp.max(jnp.where(lane == p, peer_row[...], 0)) for p in range(cfg["peers"])]
@@ -345,7 +366,7 @@
     both2[wide:] = weights2[...]
 
 
-CHUNK = 64
+CHUNK = 16
 
 
 def apply_half(values, result, st, mt, weights1, weights2):
@@ -435,6 +456,9 @@
     pick(cfg, out, base_s, node_row, at_slots)
 
 
+RETURN_STEP = 32
+
+
 def returned_sums(cfg, peer, node_row, recv, left, hot):
     windows = cfg["pairs"]
     node, value = node_row[...], received_rows(cfg, peer, recv)
@@ -444,16 +468,17 @@
     hot[:, :wide] = lanes
     hot[:, wide:] = lanes
     block = spread(node >> 7)
-    for g in range(0, windows, 2):
-        rows = slice(g * ROWS, (g + 2) * ROWS)
-        even, odd = block == g, block == g + 1
-        left[rows, :wide] = jnp.concatenate(
-            [jnp.where(even, high, 0.0), jnp.where(odd, high, 0.0)], axis=0
-        ).astype(jnp.bfloat16)
-        left[rows, wide:] = jnp.concatenate(
-            [jnp.where(even, low, 0.0), jnp.where(odd, low, 0.0)], axis=0
-        ).astype(jnp.bfloat16)
-    return nt_dot(left[...], hot[...])
+    for start in range(0, windows, RETURN_STEP):
+        for g in range(start, start + RETURN_STEP, 2):
+            rows = slice(g * ROWS, (g + 2) * ROWS)
+            even, odd = block == g, block == g + 1
+            left[rows, :wide] = jnp.concatenate(
+                [jnp.where(even, high, 0.0), jnp.where(odd, high, 0.0)], axis=0
+            ).astype(jnp.bfloat16)
+            left[rows, wide:] = jnp.concatenate(
+                [jnp.where(even, low, 0.0), jnp.where(odd, low, 0.0)], axis=0
+            ).astype(jnp.bfloat16)
+        yield start, nt_dot(left[start * ROWS : (start + RETURN_STEP) * ROWS], hot[...])
 
 
 def dot_totals(recv):
@@ -488,8 +513,14 @@
     return jnp.concatenate([tile] * (wide // LANES), axis=1)
 
 
+def window_sums(*operands):
+    for start, sums in returned_sums(*operands):
+        for k in range(RETURN_STEP):
+            yield start + k, sums[k * ROWS : (k + 1) * ROWS]
+
+
 def next_fields_body(
-    cfg, peer_row, node_row, recv, own_hbm, right_hbm, inverse, coefs, w, z1, energy, left, hot, sums, right, own, arrived
+    cfg, peer_row, node_row, recv, own_hbm, right_hbm, inverse, coefs, w, z1, energy, left, hot, right, own, arrived
 ):
     fetches = [
         pltpu.make_async_copy(there, here, arrived.at[k]) for k, (there, here) in enumerate(((right_hbm, right), (own_hbm, own)))
@@ -497,15 +528,13 @@
     for fetch in fetches:
         fetch.start()
     peer = peers_of(cfg, peer_row)
-    windows = cfg["pairs"]
-    sums[...] = returned_sums(cfg, peer, node_row, recv, left, hot)
     alpha = coefs[0]
     for fetch in fetches:
         fetch.wait()
     acc = jnp.zeros((ROWS, LANES), jnp.float32)
-    for g in range(windows):
+    for g, sums in window_sums(cfg, peer, node_row, recv, left, hot):
         cols = slice(g * LANES, (g + 1) * LANES)
-        image = own[:, cols] + sums[g * ROWS : (g + 1) * ROWS]
+        image = own[:, cols] + sums
         w[:, cols] = image
         left_over = right[:, cols] - alpha * image
         scaled = left_over * spread(inverse[g : g + 1, :])
@@ -519,7 +548,7 @@
 
 def last_body(
     cfg, peer_row, node_row, recv, own, right_hbm, inverse, w_hbm, z1, coefs,
-    solution_hbm, residual_hbm, left, hot, sums, right, w, arrived, solution, residual, sent,
+    solution_hbm, residual_hbm, left, hot, right, w, arrived, solution, residual, sent,
 ):
     fetches = [
         pltpu.make_async_copy(there, here, arrived.at[k]) for k, (there, here) in enumerate(((right_hbm, right), (w_hbm, w)))
@@ -528,7 +557,6 @@
         fetch.start()
     peer = peers_of(cfg, peer_row)
     windows = cfg["pairs"]
-    sums[...] = returned_sums(cfg, peer, node_row, recv, left, hot)
     energy_next, curve_next = dot_totals(recv)
     alpha, energy_now = coefs[0], coefs[1]
     beta = energy_next / energy_now
@@ -536,9 +564,9 @@
     copies = []
     for fetch in fetches:
         fetch.wait()
-    for g in range(windows):
+    for g, sums in window_sums(cfg, peer, node_row, recv, left, hot):
         cols = slice(g * LANES, (g + 1) * LANES)
-        image = own[:, cols] + sums[g * ROWS : (g + 1) * ROWS]
+        image = own[:, cols] + sums
         start, before = right[:, cols], w[:, cols]
         z0 = start * spread(inverse[g : g + 1, :])
         residual[:, cols] = (start - alpha * before) - step * (image + beta * before)
@@ -653,7 +681,7 @@
     wide = 2 * peers * slots
     scratch = [
         pltpu.VMEM((vectors * pairs, wide), jnp.bfloat16), pltpu.VMEM((LANES, wide), jnp.bfloat16),
-        pltpu.VMEM((vectors * pairs, LANES), f32), pltpu.VMEM(*field), pltpu.VMEM(*field),
+        pltpu.VMEM(*field), pltpu.VMEM(*field),
         pltpu.SemaphoreType.DMA((2,)),
     ]
     inner, curve = inner_part(z)

time: 73.9 us -> 73.9 us (level)
  no operation moved by 1% of the time
where the time goes in v2:
time: 73.9 us; the launch traced here: 73.4 us
  Pallas kernels  33 us (45%)
  waiting for transfers between devices  19.7 us (27%)
  starting transfers between devices  19.4 us (26%)
  between operations  0.88 us (1%)
    pallas_call x13, Pallas kernels, run(): kernel(*[pltpu.with_memory_space_constraint(operand, pltpu.VMEM if k in r...  33 us
    all_to_all x5, waiting for transfers between devices, exchange(): lax.all_to_all(values, 'dom', split_axis=0, concat_axis=0, tiled=True)  19.7 us
    all_to_all x5, starting transfers between devices, exchange(): lax.all_to_all(values, 'dom', split_axis=0, concat_axis=0, tiled=True)  19.4 us
  transfers between devices with their start and end apart: 5, of which 5 were waited for; matrix products, arithmetic and copies ran while one was open for 0% of the time, Pallas kernels for 27%

profile of v2, /device:TPU:0, one launch (start us, length us, event | category | flops | bytes accessed | tf_op | source)
XLA Modules:
  0.0 73.4 jit_solution(6699368904791155586)
XLA Ops:
  0.6 2.2 %ghost_diag.1 = (f32[32,1,128]{2,1,0:T(1,128)}, s32[8,128]{1,0:T(8,128)S(1)}, s32[1,128]{1,0:T(1,128)S(1)}, s32[5,1,128]{2,1,0:T(1,128)}, s32[1,640]{1,0:T(1,128)S(1)}) custom-call(s32[1,5]{1,0:T(1,128)} %peer.3, f32[3]{0:T(128)} %density.3, s32[125,256]{1,0:T(8,128)} %nodes.3, f32[3,125,256]{2,1,0:T(8,128)} %stiff.3, f32[125,256]{1,0:T(8,128)} %mass.3, ...), custom_call_target="tpu_custom_call" | custom-call | tf_op jit(solution)/shard_map/ghost_diag/pallas_call | solution.py:125
  2.9 7.3 %all-to-all-start = ((f32[32,1,128]{2,1,0:T(1,128)}), f32[32,1,128]{2,1,0:T(1,128)S(1)}, u32[]{:S(2)}, u32[]{:S(2)}) async-start(f32[32,1,128]{2,1,0:T(1,128)} %get-tuple-element.38), calls=%async_computation | async-start | bytes 32768 | tf_op jit(solution)/shard_map/all_to_all | solution.py:617
  10.2 5.2 %tables.1 = (s32[256,128]{1,0:T(8,128)S(1)}, f32[128,384]{1,0:T(8,128)S(1)}, f32[128,128]{1,0:T(8,128)S(1)}, f32[128,384]{1,0:T(8,128)}, f32[128,128]{1,0:T(8,12...) custom-call(s32[1,5]{1,0:T(1,128)} %peer.3, ...), custom_call_target="tpu_custom_call" | custom-call | tf_op jit(solution)/shard_map/tables/pallas_call | solution.py:125
  15.4 1.9 %all-to-all-done.recv = f32[32,1,128]{2,1,0:T(1,128)S(1)} async-done(((f32[32,1,128]{2,1,0:T(1,128)}), f32[32,1,128]{2,1,0:T(1,128)S(1)}, u32[]{:S(2)}, u32[]{:S(2)}) %all-to-all-start) | async-done | bytes 16416 | tf_op jit(solution)/shard_map/all_to_all | solution.py:617
  17.3 0.0 copy-start
  17.3 1.4 %start.1 = (f32[32,8,128]{2,1,0:T(8,128)}, f32[8,640]{1,0:T(8,128)S(1)}) custom-call(s32[1,128]{1,0:T(1,128)S(1)} %get-tuple-element.36.peer_row, f32[32,1,128]{2,1,0:T(1,128)S(1)} %all-to-all-done.recv, f32[8,640]{1,0:T(8,128)S(1)} %get-tuple-element.40.right_at, f32[8,640]{1,0:T(8,128)S(1)} %get-tuple-element.41.diag_at, ...), custom_call_target="tpu_custom_call" | custom-call | tf_op jit(solution)/shard_map/start/pallas_call | solution.py:125
  18.7 4.0 %all-to-all-start.1 = ((f32[32,8,128]{2,1,0:T(8,128)}), f32[32,8,128]{2,1,0:T(8,128)S(1)}, u32[]{:S(2)}, u32[]{:S(2)}) async-start(f32[32,8,128]{2,1,0:T(8,128)} %get-tuple-element.43), calls=%async_computation.1 | async-start | bytes 262144 | tf_op jit(solution)/shard_map/all_to_all | solution.py:617
  22.7 0.0 copy-done
  22.7 0.0 copy-start.1
  22.7 0.0 copy-start.2
  22.7 0.7 first_fields.1
  23.4 0.2 copy-done.1
  23.6 0.1 copy-done.2
  23.7 2.2 %inner.2 = (f32[1024,128]{1,0:T(8,128)S(1)}, f32[8,128]{1,0:T(8,128)S(1)}) custom-call(f32[8,16384]{1,0:T(8,128)S(1)} %get-tuple-element.45.z, s32[256,128]{1,0:T(8,128)S(1)} %get-tuple-element.46.idx, f32[128,384]{1,0:T(8,128)} %get-tuple-element.51.st, f32[128,128]{1,0:T(8,128)} %get-tuple-element.52.mt, bf16[128,768]{1,0:T(8,128)(2,1)S(1)} %copy-done.2, ...), custom_call_target="tpu_custom_call" | custom-call | tf_op jit(solution)/shard_map/inner/pallas_call | solution.py:125
  25.9 4.9 %all-to-all-done.1.recv = f32[32,8,128]{2,1,0:T(8,128)S(1)} async-done(((f32[32,8,128]{2,1,0:T(8,128)}), f32[32,8,128]{2,1,0:T(8,128)S(1)}, u32[]{:S(2)}, u32[]{:S(2)}) %all-to-all-start.1) | async-done | bytes 131104 | tf_op jit(solution)/shard_map/all_to_all | solution.py:617
  30.9 2.6 %edge.2 = (f32[1024,128]{1,0:T(8,128)S(1)}, f32[288,1,128]{2,1,0:T(1,128)}) custom-call(s32[1,128]{1,0:T(1,128)S(1)} %get-tuple-element.36.peer_row, f32[32,8,128]{2,1,0:T(8,128)S(1)} %all-to-all-done.1.recv, f32[8,16384]{1,0:T(8,128)S(1)} %get-tuple-element.45.z, s32[256,128]{1,0:T(8,128)S(1)} %get-tuple-element.46.idx, ...), custom_call_target="tpu_custom_call" | custom-call | tf_op jit(solution)/shard_map/edge/pallas_call | solution.py:125
  33.5 2.6 %all-to-all-start.2 = ((f32[288,1,128]{2,1,0:T(1,128)}), f32[288,1,128]{2,1,0:T(1,128)S(1)}, u32[]{:S(2)}, u32[]{:S(2)}) async-start(f32[288,1,128]{2,1,0:T(1,128)} %get-tuple-element.54), calls=%async_computation.2 | async-start | bytes 294912 | tf_op jit(solution)/shard_map/all_to_all | solution.py:617
  36.1 4.5 %edge_scatter_pick.1 = (f32[8,16384]{1,0:T(8,128)}, f32[8,640]{1,0:T(8,128)S(1)}) custom-call(s32[5,1,128]{2,1,0:T(1,128)} %get-tuple-element.39.base_s, s32[1,640]{1,0:T(1,128)S(1)} %get-tuple-element.37.node_row, f32[1024,128]{1,0:T(8,128)S(1)} %get-tuple-element.56.result, s32[256,128]{1,0:T(8,128)S(1)} %get-tuple-element.46.idx, ...), custom_call_target="tpu_custom_call" | custom-call | tf_op jit(solution)/shard_map/edge_scatter_pick/pallas_call | solution.py:125
  40.5 4.0 %all-to-all-done.2.recv = f32[288,1,128]{2,1,0:T(1,128)S(1)} async-done(((f32[288,1,128]{2,1,0:T(1,128)}), f32[288,1,128]{2,1,0:T(1,128)S(1)}, u32[]{:S(2)}, u32[]{:S(2)}) %all-to-all-start.2) | async-done | bytes 147488 | tf_op jit(solution)/shard_map/all_to_all | solution.py:617
  44.5 1.2 %step.1 = (f32[32,8,128]{2,1,0:T(8,128)}, f32[2,8,128]{2,1,0:T(8,128)S(1)}) custom-call(s32[1,128]{1,0:T(1,128)S(1)} %get-tuple-element.36.peer_row, f32[288,1,128]{2,1,0:T(1,128)S(1)} %all-to-all-done.2.recv, f32[8,640]{1,0:T(8,128)S(1)} %get-tuple-element.40.right_at, f32[8,640]{1,0:T(8,128)S(1)} %get-tuple-element.55.inverse_at, ...), custom_call_target="tpu_custom_call" | custom-call | tf_op jit(solution)/shard_map/step/pallas_call | solution.py:125
  45.7 2.7 %all-to-all-start.3 = ((f32[32,8,128]{2,1,0:T(8,128)}), f32[32,8,128]{2,1,0:T(8,128)S(1)}, u32[]{:S(2)}, u32[]{:S(2)}) async-start(f32[32,8,128]{2,1,0:T(8,128)} %get-tuple-element.59), calls=%async_computation.3 | async-start | bytes 262144 | tf_op jit(solution)/shard_map/all_to_all | solution.py:617
  48.4 2.9 %next_fields.1 = (f32[8,16384]{1,0:T(8,128)}, f32[8,16384]{1,0:T(8,128)S(1)}, f32[8,128]{1,0:T(8,128)S(1)}) custom-call(s32[1,128]{1,0:T(1,128)S(1)} %get-tuple-element.36.peer_row, s32[1,640]{1,0:T(1,128)S(1)} %get-tuple-element.37.node_row, f32[288,1,128]{2,1,0:T(1,128)S(1)} %all-to-all-done.2.recv, f32[8,16384]{1,0:T(8,128)} %get-tuple-element.60.own_hbm, ...), custom_call_target="tpu_custom_call" | custom-call | tf_op jit(solution)/shard_map/next_fields/pallas_call | solution.py:125
  51.4 2.2 %inner.3 = (f32[1024,128]{1,0:T(8,128)S(1)}, f32[8,128]{1,0:T(8,128)S(1)}) custom-call(f32[8,16384]{1,0:T(8,128)S(1)} %get-tuple-element.63.z.z1, s32[256,128]{1,0:T(8,128)S(1)} %get-tuple-element.46.idx, f32[128,384]{1,0:T(8,128)} %get-tuple-element.51.st, f32[128,128]{1,0:T(8,128)} %get-tuple-element.52.mt, bf16[128,768]{1,0:T(8,128)(2,1)S(1)} %copy-done.2, ...), custom_call_target="tpu_custom_call" | custom-call | tf_op jit(solution)/shard_map/inner/pallas_call | solution.py:125
  53.6 2.8 %all-to-all-done.3.recv = f32[32,8,128]{2,1,0:T(8,128)S(1)} async-done(((f32[32,8,128]{2,1,0:T(8,128)}), f32[32,8,128]{2,1,0:T(8,128)S(1)}, u32[]{:S(2)}, u32[]{:S(2)}) %all-to-all-start.3) | async-done | bytes 131104 | tf_op jit(solution)/shard_map/all_to_all | solution.py:617
  56.4 2.6 %edge.3 = (f32[1024,128]{1,0:T(8,128)S(1)}, f32[288,1,128]{2,1,0:T(1,128)}) custom-call(s32[1,128]{1,0:T(1,128)S(1)} %get-tuple-element.36.peer_row, f32[32,8,128]{2,1,0:T(8,128)S(1)} %all-to-all-done.3.recv, f32[8,16384]{1,0:T(8,128)S(1)} %get-tuple-element.63.z.z1, s32[256,128]{1,0:T(8,128)S(1)} %get-tuple-element.46.idx, ...), custom_call_target="tpu_custom_call" | custom-call | tf_op jit(solution)/shard_map/edge/pallas_call | solution.py:125
  59.1 2.8 %all-to-all-start.4 = ((f32[288,1,128]{2,1,0:T(1,128)}), f32[288,1,128]{2,1,0:T(1,128)S(1)}, u32[]{:S(2)}, u32[]{:S(2)}) async-start(f32[288,1,128]{2,1,0:T(1,128)} %get-tuple-element.66), calls=%async_computation.4 | async-start | bytes 294912 | tf_op jit(solution)/shard_map/all_to_all | solution.py:617
  61.9 2.3 %edge_scatter.1.own = f32[8,16384]{1,0:T(8,128)S(1)} custom-call(f32[1024,128]{1,0:T(8,128)S(1)} %get-tuple-element.67.result, s32[256,128]{1,0:T(8,128)S(1)} %get-tuple-element.46.idx, f32[1024,128]{1,0:T(8,128)S(1)} %get-tuple-element.68.inner), custom_call_target="tpu_custom_call" | custom-call | tf_op jit(solution)/shard_map/edge_scatter/pallas_call | solution.py:125
  64.2 6.1 %all-to-all-done.4.recv = f32[288,1,128]{2,1,0:T(1,128)S(1)} async-done(((f32[288,1,128]{2,1,0:T(1,128)}), f32[288,1,128]{2,1,0:T(1,128)S(1)}, u32[]{:S(2)}, u32[]{:S(2)}) %all-to-all-start.4) | async-done | bytes 147488 | tf_op jit(solution)/shard_map/all_to_all | solution.py:617
  70.3 2.9 %last.1 = (f32[8,16384]{1,0:T(8,128)}, f32[8,16384]{1,0:T(8,128)}) custom-call(s32[1,128]{1,0:T(1,128)S(1)} %get-tuple-element.36.peer_row, s32[1,640]{1,0:T(1,128)S(1)} %get-tuple-element.37.node_row, f32[288,1,128]{2,1,0:T(1,128)S(1)} %all-to-all-done.4.recv, f32[8,16384]{1,0:T(8,128)S(1)} %edge_scatter.1.own, f32[8,16384]{1,0:T(8,128)} %right_hbm.3, ...), custom_call_target="tpu_custom_call" | custom-call | tf_op jit(solution)/shard_map/last/pallas_call | solution.py:125
Async XLA Ops:
  2.9 14.4 %all-to-all-start = ((f32[32,1,128]{2,1,0:T(1,128)}), f32[32,1,128]{2,1,0:T(1,128)S(1)}, u32[]{:S(2)}, u32[]{:S(2)}) async-start(f32[32,1,128]{2,1,0:T(1,128)} %get-tuple-element.38), calls=%async_computation | async-start | bytes 32768 | tf_op jit(solution)/shard_map/all_to_all | solution.py:617
  17.3 5.4 %copy-start = (f32[8,16384]{1,0:T(8,128)S(1)}, f32[8,16384]{1,0:T(8,128)}, u32[]{:S(2)}) copy-start(f32[8,16384]{1,0:T(8,128)} %right_hbm.3) | copy-start | bytes 1572868
  18.7 12.2 %all-to-all-start.1 = ((f32[32,8,128]{2,1,0:T(8,128)}), f32[32,8,128]{2,1,0:T(8,128)S(1)}, u32[]{:S(2)}, u32[]{:S(2)}) async-start(f32[32,8,128]{2,1,0:T(8,128)} %get-tuple-element.43), calls=%async_computation.1 | async-start | bytes 262144 | tf_op jit(solution)/shard_map/all_to_all | solution.py:617
  22.7 0.9 %copy-start.1 = (bf16[384,256]{1,0:T(8,128)(2,1)S(1)}, bf16[384,256]{1,0:T(8,128)(2,1)}, u32[]{:S(2)}) copy-start(bf16[384,256]{1,0:T(8,128)(2,1)} %constant.7.clone.w2) | copy-start | bytes 589828
  22.7 1.0 %copy-start.2 = (bf16[128,768]{1,0:T(8,128)(2,1)S(1)}, bf16[128,768]{1,0:T(8,128)(2,1)}, u32[]{:S(2)}) copy-start(bf16[128,768]{1,0:T(8,128)(2,1)} %constant.6.clone.w1) | copy-start | bytes 589828
  33.5 11.0 %all-to-all-start.2 = ((f32[288,1,128]{2,1,0:T(1,128)}), f32[288,1,128]{2,1,0:T(1,128)S(1)}, u32[]{:S(2)}, u32[]{:S(2)}) async-start(f32[288,1,128]{2,1,0:T(1,128)} %get-tuple-element.54), calls=%async_computation.2 | async-start | bytes 294912 | tf_op jit(solution)/shard_map/all_to_all | solution.py:617
  45.7 10.8 %all-to-all-start.3 = ((f32[32,8,128]{2,1,0:T(8,128)}), f32[32,8,128]{2,1,0:T(8,128)S(1)}, u32[]{:S(2)}, u32[]{:S(2)}) async-start(f32[32,8,128]{2,1,0:T(8,128)} %get-tuple-element.59), calls=%async_computation.3 | async-start | bytes 262144 | tf_op jit(solution)/shard_map/all_to_all | solution.py:617
  59.1 11.2 %all-to-all-start.4 = ((f32[288,1,128]{2,1,0:T(1,128)}), f32[288,1,128]{2,1,0:T(1,128)S(1)}, u32[]{:S(2)}, u32[]{:S(2)}) async-start(f32[288,1,128]{2,1,0:T(1,128)} %get-tuple-element.66), calls=%async_computation.4 | async-start | bytes 294912 | tf_op jit(solution)/shard_map/all_to_all | solution.py:617

commit v3 on v2

--- a/solution.py
+++ b/solution.py
@@ -183,7 +183,7 @@
 
 def tables_body(
     cfg, peer, density, nodes, stiff, mass, region, squares, base_s, node_row, right,
-    idx, st_edge, mt_edge, st_inner, mt_inner, own_diag, right_at, diag_at, same,
+    idx, mt_edge, mt_inner, own_diag, right_at, diag_at, same,
     code_pad, value_pad, rows,
 ):
     code_pad[...] = jnp.full(code_pad.shape, NONE, jnp.int32)
@@ -208,15 +208,10 @@
         ]
         for k, sums in enumerate(scatter_pairs(lines, idx, g)):
             own_diag[g + k : g + k + 1, :] = sums[:1]
-    for d in range(3):
-        value_pad[:NPE] = stiff[d]
-        cols = slice(d * LANES, (d + 1) * LANES)
-        st_edge[:, cols] = value_pad[:, :LANES].T
-        st_inner[:, cols] = value_pad[:, LANES:].T
+    pick(cfg, right, base_s, node_row, right_at)
     value_pad[:NPE] = term
     mt_edge[...] = value_pad[:, :LANES].T
     mt_inner[...] = value_pad[:, LANES:].T
-    pick(cfg, right, base_s, node_row, right_at)
     node = node_row[...]
     wide = node.shape[1]
     hot = jnp.where(iota((LANES, wide), 0) == (node & (LANES - 1)), 1.0, 0.0).astype(jnp.bfloat16)
@@ -322,7 +317,13 @@
     put_slots(cfg, peer, right_at[...] * inverse, out)
 
 
-def first_fields_body(cfg, peer_row, node_row, recv, own_diag, right, inverse, z, energy):
+def first_fields_body(
+    cfg, peer_row, node_row, recv, own_diag, right, stiff_hbm, inverse, z, energy, st_edge, st_inner,
+    stiff, value_pad, arrived,
+):
+    fetch = pltpu.make_async_copy(stiff_hbm, stiff, arrived)
+    fetch.start()
+    value_pad[...] = jnp.zeros(value_pad.shape, jnp.float32)
     peer = peers_of(cfg, peer_row)
     windows = cfg["pairs"]
     node, got = node_row[...], received_diag(cfg, peer, recv)
@@ -339,6 +340,12 @@
         z[:, cols] = scaled
         acc = acc + right[:, cols] * scaled
     energy[...] = acc
+    fetch.wait()
+    for d in range(3):
+        value_pad[:NPE] = stiff[d]
+        cols = slice(d * LANES, (d + 1) * LANES)
+        st_edge[:, cols] = value_pad[:, :LANES].T
+        st_inner[:, cols] = value_pad[:, LANES:].T
 
 
 def apply_rows(values, st, mt, weights1, weights2):
@@ -529,10 +536,11 @@
         fetch.start()
     peer = peers_of(cfg, peer_row)
     alpha = coefs[0]
-    for fetch in fetches:
-        fetch.wait()
     acc = jnp.zeros((ROWS, LANES), jnp.float32)
     for g, sums in window_sums(cfg, peer, node_row, recv, left, hot):
+        if g == 0:
+            for fetch in fetches:
+                fetch.wait()
         cols = slice(g * LANES, (g + 1) * LANES)
         image = own[:, cols] + sums
         w[:, cols] = image
@@ -635,15 +643,14 @@
     recv = exchange(send)
     slots_all = ((vectors, peers * slots), f32)
     edge_count = elem_count // 2
-    idx, st_edge, mt_edge, st_inner, mt_inner, own_diag, right_at, diag_at, same = call(
+    idx, mt_edge, mt_inner, own_diag, right_at, diag_at, same = call(
         bind(tables_body), "tables", [S, S] + [V] * 5 + [S, V, V],
         [
             ((elem_count, LANES), i32),
-            ((edge_count, 3 * LANES), f32), ((edge_count, LANES), f32),
-            ((elem_count - edge_count, 3 * LANES), f32), ((elem_count - edge_count, LANES), f32),
+            ((edge_count, LANES), f32), ((elem_count - edge_count, LANES), f32),
             square, slots_all, slots_all, ((peers * slots, peers * slots), jnp.bfloat16),
         ],
-        (0, 1, 2, 5, 6, 7, 8),
+        (0, 1, 3, 4, 5, 6),
         [
             pltpu.VMEM((LANES, elem_count), i32), pltpu.VMEM((LANES, elem_count), f32),
             pltpu.VMEM((elem_count, LANES), f32),
@@ -657,9 +664,18 @@
     )(peer_row, recv, right_at, diag_at, same)
     diag_recv = recv
     recv = exchange(send)
-    inverse, z, energy = call(
-        bind(first_fields_body), "first_fields", [V] * 5, [square, field, tile], range(3), (), range(5),
-    )(peer_row, node_row, diag_recv, own_diag, right_side)
+    inverse, z, energy, st_edge, st_inner = call(
+        bind(first_fields_body), "first_fields", [V] * 5 + [hbm()],
+        [
+            square, field, tile, ((edge_count, 3 * LANES), f32), ((elem_count - edge_count, 3 * LANES), f32),
+        ],
+        range(4),
+        [
+            pltpu.VMEM(stiffness.shape, f32), pltpu.VMEM((LANES, elem_count), f32),
+            pltpu.SemaphoreType.DMA(()),
+        ],
+        range(5),
+    )(peer_row, node_row, diag_recv, own_diag, right_side, stiffness)
 
     weight_rows = [
         pltpu.VMEM((2 * LANES, 6 * LANES), jnp.bfloat16), pltpu.VMEM((6 * LANES, 2 * LANES), jnp.bfloat16)

time: 73.9 us -> 74 us (level)
  Pallas kernels: 33 us -> 34.9 us
  waiting for transfers between devices: 19.7 us -> 18.2 us
    pallas_call x13, Pallas kernels: 33 us -> 34.9 us  [run(): kernel(*[pltpu.with_memory_space_constraint(operand, pltpu.VMEM if k in r...]
    all_to_all x5, waiting for transfers between devices: 19.7 us -> 18.2 us  [exchange(): lax.all_to_all(values, 'dom', split_axis=0, concat_axis=0, tiled=True)]
  transfers between devices with their start and end apart: 5 -> 5, of which waited for: 5 -> 5; matrix products, arithmetic and copies ran while one was open for 0% -> 0% of each run, Pallas kernels for 27% -> 30%
where the time goes in v3:
time: 74 us; the launch traced here: 73.5 us
  Pallas kernels  34.9 us (47%)
  starting transfers between devices  19.5 us (26%)
  waiting for transfers between devices  18.2 us (25%)
  between operations  0.9 us (1%)
    pallas_call x13, Pallas kernels, run(): kernel(*[pltpu.with_memory_space_constraint(operand, pltpu.VMEM if k in r...  34.9 us
    all_to_all x5, starting transfers between devices, exchange(): lax.all_to_all(values, 'dom', split_axis=0, concat_axis=0, tiled=True)  19.5 us
    all_to_all x5, waiting for transfers between devices, exchange(): lax.all_to_all(values, 'dom', split_axis=0, concat_axis=0, tiled=True)  18.2 us
  transfers between devices with their start and end apart: 5, of which 5 were waited for; matrix products, arithmetic and copies ran while one was open for 0% of the time, Pallas kernels for 30%

profile of v3, /device:TPU:0, one launch (start us, length us, event | category | flops | bytes accessed | tf_op | source)
XLA Modules:
  0.0 73.5 jit_solution(4695058785321788574)
XLA Ops:
  0.6 2.2 %ghost_diag.1 = (f32[32,1,128]{2,1,0:T(1,128)}, s32[8,128]{1,0:T(8,128)S(1)}, s32[1,128]{1,0:T(1,128)S(1)}, s32[5,1,128]{2,1,0:T(1,128)}, s32[1,640]{1,0:T(1,128)S(1)}) custom-call(s32[1,5]{1,0:T(1,128)} %peer.3, f32[3]{0:T(128)} %density.3, s32[125,256]{1,0:T(8,128)} %nodes.3, f32[3,125,256]{2,1,0:T(8,128)} %stiff_hbm.1, f32[125,256]{1,0:T(8,128)} %mass.3, ...), custom_call_target="tpu_custom_call" | custom-call | tf_op jit(solution)/shard_map/ghost_diag/pallas_call | solution.py:125
  2.9 7.3 %all-to-all-start = ((f32[32,1,128]{2,1,0:T(1,128)}), f32[32,1,128]{2,1,0:T(1,128)S(1)}, u32[]{:S(2)}, u32[]{:S(2)}) async-start(f32[32,1,128]{2,1,0:T(1,128)} %get-tuple-element.38), calls=%async_computation | async-start | bytes 32768 | tf_op jit(solution)/shard_map/all_to_all | solution.py:625
  10.2 5.1 %tables.1 = (s32[256,128]{1,0:T(8,128)S(1)}, f32[128,128]{1,0:T(8,128)S(1)}, f32[128,128]{1,0:T(8,128)}, f32[128,128]{1,0:T(8,128)S(1)}, f32[8,640]{1,0:T(8,128)...) custom-call(s32[1,5]{1,0:T(1,128)} %peer.3, f32[3]{0:T(128)} %density.3, s32[125,256]{1,0:T(8,128)} %nodes.3, ...), custom_call_target="tpu_custom_call" | custom-call | tf_op jit(solution)/shard_map/tables/pallas_call | solution.py:125
  15.4 2.0 %all-to-all-done.recv = f32[32,1,128]{2,1,0:T(1,128)S(1)} async-done(((f32[32,1,128]{2,1,0:T(1,128)}), f32[32,1,128]{2,1,0:T(1,128)S(1)}, u32[]{:S(2)}, u32[]{:S(2)}) %all-to-all-start) | async-done | bytes 16416 | tf_op jit(solution)/shard_map/all_to_all | solution.py:625
  17.3 0.0 copy-start
  17.3 1.4 %start.1 = (f32[32,8,128]{2,1,0:T(8,128)}, f32[8,640]{1,0:T(8,128)S(1)}) custom-call(s32[1,128]{1,0:T(1,128)S(1)} %get-tuple-element.36.peer_row, f32[32,1,128]{2,1,0:T(1,128)S(1)} %all-to-all-done.recv, f32[8,640]{1,0:T(8,128)S(1)} %get-tuple-element.40.right_at, f32[8,640]{1,0:T(8,128)S(1)} %get-tuple-element.41.diag_at, ...), custom_call_target="tpu_custom_call" | custom-call | tf_op jit(solution)/shard_map/start/pallas_call | solution.py:125
  18.7 3.9 %all-to-all-start.1 = ((f32[32,8,128]{2,1,0:T(8,128)}), f32[32,8,128]{2,1,0:T(8,128)S(1)}, u32[]{:S(2)}, u32[]{:S(2)}) async-start(f32[32,8,128]{2,1,0:T(8,128)} %get-tuple-element.43), calls=%async_computation.1 | async-start | bytes 262144 | tf_op jit(solution)/shard_map/all_to_all | solution.py:625
  22.6 0.0 copy-done
  22.6 0.0 copy-start.1
  22.6 0.0 copy-start.2
  22.6 2.4 %first_fields.1 = (f32[128,128]{1,0:T(8,128)S(1)}, f32[8,16384]{1,0:T(8,128)S(1)}, f32[8,128]{1,0:T(8,128)S(1)}, f32[128,384]{1,0:T(8,128)S(1)}, f32[128,384]{1,0:T(8,128)}) custom-call(s32[1,128]{1,0:T(1,128)S(1)} %get-tuple-element.36.peer_row, s32[1,640]{1,0:T(1,128)S(1)} %get-tuple-element.37.node_row, f32[32,1,128]{2,1,0:T(1,128)S(1)} %all-to-all-done.recv, ...), custom_call_target="tpu_custom_call" | custom-call | tf_op jit(solution)/shard_map/first_fields/pallas_call | solution.py:125
  25.1 0.0 copy-done.1
  25.1 0.0 copy-done.2
  25.1 2.2 %inner.2 = (f32[1024,128]{1,0:T(8,128)S(1)}, f32[8,128]{1,0:T(8,128)S(1)}) custom-call(f32[8,16384]{1,0:T(8,128)S(1)} %get-tuple-element.45.z, s32[256,128]{1,0:T(8,128)S(1)} %get-tuple-element.46.idx, f32[128,384]{1,0:T(8,128)} %get-tuple-element.51.st, f32[128,128]{1,0:T(8,128)} %get-tuple-element.52.mt, bf16[128,768]{1,0:T(8,128)(2,1)S(1)} %copy-done.2, ...), custom_call_target="tpu_custom_call" | custom-call | tf_op jit(solution)/shard_map/inner/pallas_call | solution.py:125
  27.3 3.5 %all-to-all-done.1.recv = f32[32,8,128]{2,1,0:T(8,128)S(1)} async-done(((f32[32,8,128]{2,1,0:T(8,128)}), f32[32,8,128]{2,1,0:T(8,128)S(1)}, u32[]{:S(2)}, u32[]{:S(2)}) %all-to-all-start.1) | async-done | bytes 131104 | tf_op jit(solution)/shard_map/all_to_all | solution.py:625
  30.8 2.6 %edge.2 = (f32[1024,128]{1,0:T(8,128)S(1)}, f32[288,1,128]{2,1,0:T(1,128)}) custom-call(s32[1,128]{1,0:T(1,128)S(1)} %get-tuple-element.36.peer_row, f32[32,8,128]{2,1,0:T(8,128)S(1)} %all-to-all-done.1.recv, f32[8,16384]{1,0:T(8,128)S(1)} %get-tuple-element.45.z, s32[256,128]{1,0:T(8,128)S(1)} %get-tuple-element.46.idx, ...), custom_call_target="tpu_custom_call" | custom-call | tf_op jit(solution)/shard_map/edge/pallas_call | solution.py:125
  33.4 2.6 %all-to-all-start.2 = ((f32[288,1,128]{2,1,0:T(1,128)}), f32[288,1,128]{2,1,0:T(1,128)S(1)}, u32[]{:S(2)}, u32[]{:S(2)}) async-start(f32[288,1,128]{2,1,0:T(1,128)} %get-tuple-element.54), calls=%async_computation.2 | async-start | bytes 294912 | tf_op jit(solution)/shard_map/all_to_all | solution.py:625
  36.0 4.5 %edge_scatter_pick.1 = (f32[8,16384]{1,0:T(8,128)}, f32[8,640]{1,0:T(8,128)S(1)}) custom-call(s32[5,1,128]{2,1,0:T(1,128)} %get-tuple-element.39.base_s, s32[1,640]{1,0:T(1,128)S(1)} %get-tuple-element.37.node_row, f32[1024,128]{1,0:T(8,128)S(1)} %get-tuple-element.56.result, s32[256,128]{1,0:T(8,128)S(1)} %get-tuple-element.46.idx, ...), custom_call_target="tpu_custom_call" | custom-call | tf_op jit(solution)/shard_map/edge_scatter_pick/pallas_call | solution.py:125
  40.5 4.0 %all-to-all-done.2.recv = f32[288,1,128]{2,1,0:T(1,128)S(1)} async-done(((f32[288,1,128]{2,1,0:T(1,128)}), f32[288,1,128]{2,1,0:T(1,128)S(1)}, u32[]{:S(2)}, u32[]{:S(2)}) %all-to-all-start.2) | async-done | bytes 147488 | tf_op jit(solution)/shard_map/all_to_all | solution.py:625
  44.4 1.2 %step.1 = (f32[32,8,128]{2,1,0:T(8,128)}, f32[2,8,128]{2,1,0:T(8,128)S(1)}) custom-call(s32[1,128]{1,0:T(1,128)S(1)} %get-tuple-element.36.peer_row, f32[288,1,128]{2,1,0:T(1,128)S(1)} %all-to-all-done.2.recv, f32[8,640]{1,0:T(8,128)S(1)} %get-tuple-element.40.right_at, f32[8,640]{1,0:T(8,128)S(1)} %get-tuple-element.55.inverse_at, ...), custom_call_target="tpu_custom_call" | custom-call | tf_op jit(solution)/shard_map/step/pallas_call | solution.py:125
  45.6 2.7 %all-to-all-start.3 = ((f32[32,8,128]{2,1,0:T(8,128)}), f32[32,8,128]{2,1,0:T(8,128)S(1)}, u32[]{:S(2)}, u32[]{:S(2)}) async-start(f32[32,8,128]{2,1,0:T(8,128)} %get-tuple-element.59), calls=%async_computation.3 | async-start | bytes 262144 | tf_op jit(solution)/shard_map/all_to_all | solution.py:625
  48.3 3.1 %next_fields.1 = (f32[8,16384]{1,0:T(8,128)}, f32[8,16384]{1,0:T(8,128)S(1)}, f32[8,128]{1,0:T(8,128)S(1)}) custom-call(s32[1,128]{1,0:T(1,128)S(1)} %get-tuple-element.36.peer_row, s32[1,640]{1,0:T(1,128)S(1)} %get-tuple-element.37.node_row, f32[288,1,128]{2,1,0:T(1,128)S(1)} %all-to-all-done.2.recv, f32[8,16384]{1,0:T(8,128)} %get-tuple-element.60.own_hbm, ...), custom_call_target="tpu_custom_call" | custom-call | tf_op jit(solution)/shard_map/next_fields/pallas_call | solution.py:125
  51.4 2.2 %inner.3 = (f32[1024,128]{1,0:T(8,128)S(1)}, f32[8,128]{1,0:T(8,128)S(1)}) custom-call(f32[8,16384]{1,0:T(8,128)S(1)} %get-tuple-element.63.z.z1, s32[256,128]{1,0:T(8,128)S(1)} %get-tuple-element.46.idx, f32[128,384]{1,0:T(8,128)} %get-tuple-element.51.st, f32[128,128]{1,0:T(8,128)} %get-tuple-element.52.mt, bf16[128,768]{1,0:T(8,128)(2,1)S(1)} %copy-done.2, ...), custom_call_target="tpu_custom_call" | custom-call | tf_op jit(solution)/shard_map/inner/pallas_call | solution.py:125
  53.7 2.7 %all-to-all-done.3.recv = f32[32,8,128]{2,1,0:T(8,128)S(1)} async-done(((f32[32,8,128]{2,1,0:T(8,128)}), f32[32,8,128]{2,1,0:T(8,128)S(1)}, u32[]{:S(2)}, u32[]{:S(2)}) %all-to-all-start.3) | async-done | bytes 131104 | tf_op jit(solution)/shard_map/all_to_all | solution.py:625
  56.4 2.6 %edge.3 = (f32[1024,128]{1,0:T(8,128)S(1)}, f32[288,1,128]{2,1,0:T(1,128)}) custom-call(s32[1,128]{1,0:T(1,128)S(1)} %get-tuple-element.36.peer_row, f32[32,8,128]{2,1,0:T(8,128)S(1)} %all-to-all-done.3.recv, f32[8,16384]{1,0:T(8,128)S(1)} %get-tuple-element.63.z.z1, s32[256,128]{1,0:T(8,128)S(1)} %get-tuple-element.46.idx, ...), custom_call_target="tpu_custom_call" | custom-call | tf_op jit(solution)/shard_map/edge/pallas_call | solution.py:125
  59.0 3.0 %all-to-all-start.4 = ((f32[288,1,128]{2,1,0:T(1,128)}), f32[288,1,128]{2,1,0:T(1,128)S(1)}, u32[]{:S(2)}, u32[]{:S(2)}) async-start(f32[288,1,128]{2,1,0:T(1,128)} %get-tuple-element.66), calls=%async_computation.4 | async-start | bytes 294912 | tf_op jit(solution)/shard_map/all_to_all | solution.py:625
  62.0 2.3 %edge_scatter.1.own = f32[8,16384]{1,0:T(8,128)S(1)} custom-call(f32[1024,128]{1,0:T(8,128)S(1)} %get-tuple-element.67.result, s32[256,128]{1,0:T(8,128)S(1)} %get-tuple-element.46.idx, f32[1024,128]{1,0:T(8,128)S(1)} %get-tuple-element.68.inner), custom_call_target="tpu_custom_call" | custom-call | tf_op jit(solution)/shard_map/edge_scatter/pallas_call | solution.py:125
  64.3 6.1 %all-to-all-done.4.recv = f32[288,1,128]{2,1,0:T(1,128)S(1)} async-done(((f32[288,1,128]{2,1,0:T(1,128)}), f32[288,1,128]{2,1,0:T(1,128)S(1)}, u32[]{:S(2)}, u32[]{:S(2)}) %all-to-all-start.4) | async-done | bytes 147488 | tf_op jit(solution)/shard_map/all_to_all | solution.py:625
  70.4 2.9 %last.1 = (f32[8,16384]{1,0:T(8,128)}, f32[8,16384]{1,0:T(8,128)}) custom-call(s32[1,128]{1,0:T(1,128)S(1)} %get-tuple-element.36.peer_row, s32[1,640]{1,0:T(1,128)S(1)} %get-tuple-element.37.node_row, f32[288,1,128]{2,1,0:T(1,128)S(1)} %all-to-all-done.4.recv, f32[8,16384]{1,0:T(8,128)S(1)} %edge_scatter.1.own, f32[8,16384]{1,0:T(8,128)} %right_hbm.3, ...), custom_call_target="tpu_custom_call" | custom-call | tf_op jit(solution)/shard_map/last/pallas_call | solution.py:125
Async XLA Ops:
  2.9 14.4 %all-to-all-start = ((f32[32,1,128]{2,1,0:T(1,128)}), f32[32,1,128]{2,1,0:T(1,128)S(1)}, u32[]{:S(2)}, u32[]{:S(2)}) async-start(f32[32,1,128]{2,1,0:T(1,128)} %get-tuple-element.38), calls=%async_computation | async-start | bytes 32768 | tf_op jit(solution)/shard_map/all_to_all | solution.py:625
  17.3 5.3 %copy-start = (f32[8,16384]{1,0:T(8,128)S(1)}, f32[8,16384]{1,0:T(8,128)}, u32[]{:S(2)}) copy-start(f32[8,16384]{1,0:T(8,128)} %right_hbm.3) | copy-start | bytes 1572868
  18.7 12.1 %all-to-all-start.1 = ((f32[32,8,128]{2,1,0:T(8,128)}), f32[32,8,128]{2,1,0:T(8,128)S(1)}, u32[]{:S(2)}, u32[]{:S(2)}) async-start(f32[32,8,128]{2,1,0:T(8,128)} %get-tuple-element.43), calls=%async_computation.1 | async-start | bytes 262144 | tf_op jit(solution)/shard_map/all_to_all | solution.py:625
  22.6 2.5 %copy-start.1 = (bf16[384,256]{1,0:T(8,128)(2,1)S(1)}, bf16[384,256]{1,0:T(8,128)(2,1)}, u32[]{:S(2)}) copy-start(bf16[384,256]{1,0:T(8,128)(2,1)} %constant.7.clone.w2) | copy-start | bytes 589828
  22.6 2.5 %copy-start.2 = (bf16[128,768]{1,0:T(8,128)(2,1)S(1)}, bf16[128,768]{1,0:T(8,128)(2,1)}, u32[]{:S(2)}) copy-start(bf16[128,768]{1,0:T(8,128)(2,1)} %constant.6.clone.w1) | copy-start | bytes 589828
  33.4 11.0 %all-to-all-start.2 = ((f32[288,1,128]{2,1,0:T(1,128)}), f32[288,1,128]{2,1,0:T(1,128)S(1)}, u32[]{:S(2)}, u32[]{:S(2)}) async-start(f32[288,1,128]{2,1,0:T(1,128)} %get-tuple-element.54), calls=%async_computation.2 | async-start | bytes 294912 | tf_op jit(solution)/shard_map/all_to_all | solution.py:625
  45.6 10.8 %all-to-all-start.3 = ((f32[32,8,128]{2,1,0:T(8,128)}), f32[32,8,128]{2,1,0:T(8,128)S(1)}, u32[]{:S(2)}, u32[]{:S(2)}) async-start(f32[32,8,128]{2,1,0:T(8,128)} %get-tuple-element.59), calls=%async_computation.3 | async-start | bytes 262144 | tf_op jit(solution)/shard_map/all_to_all | solution.py:625
  59.0 11.4 %all-to-all-start.4 = ((f32[288,1,128]{2,1,0:T(1,128)}), f32[288,1,128]{2,1,0:T(1,128)S(1)}, u32[]{:S(2)}, u32[]{:S(2)}) async-start(f32[288,1,128]{2,1,0:T(1,128)} %get-tuple-element.66), calls=%async_computation.4 | async-start | bytes 294912 | tf_op jit(solution)/shard_map/all_to_all | solution.py:625

commit v4 on v2

--- a/solution.py
+++ b/solution.py
@@ -208,6 +208,7 @@
         ]
         for k, sums in enumerate(scatter_pairs(lines, idx, g)):
             own_diag[g + k : g + k + 1, :] = sums[:1]
+    pick(cfg, right, base_s, node_row, right_at)
     for d in range(3):
         value_pad[:NPE] = stiff[d]
         cols = slice(d * LANES, (d + 1) * LANES)
@@ -216,7 +217,6 @@
     value_pad[:NPE] = term
     mt_edge[...] = value_pad[:, :LANES].T
     mt_inner[...] = value_pad[:, LANES:].T
-    pick(cfg, right, base_s, node_row, right_at)
     node = node_row[...]
     wide = node.shape[1]
     hot = jnp.where(iota((LANES, wide), 0) == (node & (LANES - 1)), 1.0, 0.0).astype(jnp.bfloat16)
@@ -459,7 +459,7 @@
 RETURN_STEP = 32
 
 
-def returned_sums(cfg, peer, node_row, recv, left, hot):
+def returned_sums(cfg, peer, node_row, recv, left, hot, step):
     windows = cfg["pairs"]
     node, value = node_row[...], received_rows(cfg, peer, recv)
     wide = node.shape[1]
@@ -468,8 +468,8 @@
     hot[:, :wide] = lanes
     hot[:, wide:] = lanes
     block = spread(node >> 7)
-    for start in range(0, windows, RETURN_STEP):
-        for g in range(start, start + RETURN_STEP, 2):
+    for start in range(0, windows, step):
+        for g in range(start, start + step, 2):
             rows = slice(g * ROWS, (g + 2) * ROWS)
             even, odd = block == g, block == g + 1
             left[rows, :wide] = jnp.concatenate(
@@ -478,7 +478,7 @@
             left[rows, wide:] = jnp.concatenate(
                 [jnp.where(even, low, 0.0), jnp.where(odd, low, 0.0)], axis=0
             ).astype(jnp.bfloat16)
-        yield start, nt_dot(left[start * ROWS : (start + RETURN_STEP) * ROWS], hot[...])
+        yield start, nt_dot(left[start * ROWS : (start + step) * ROWS], hot[...])
 
 
 def dot_totals(recv):
@@ -513,9 +513,9 @@
     return jnp.concatenate([tile] * (wide // LANES), axis=1)
 
 
-def window_sums(*operands):
-    for start, sums in returned_sums(*operands):
-        for k in range(RETURN_STEP):
+def window_sums(*operands, step):
+    for start, sums in returned_sums(*operands, step):
+        for k in range(step):
             yield start + k, sums[k * ROWS : (k + 1) * ROWS]
 
 
@@ -529,10 +529,11 @@
         fetch.start()
     peer = peers_of(cfg, peer_row)
     alpha = coefs[0]
-    for fetch in fetches:
-        fetch.wait()
     acc = jnp.zeros((ROWS, LANES), jnp.float32)
-    for g, sums in window_sums(cfg, peer, node_row, recv, left, hot):
+    for g, sums in window_sums(cfg, peer, node_row, recv, left, hot, step=cfg["pairs"]):
+        if g == 0:
+            for fetch in fetches:
+                fetch.wait()
         cols = slice(g * LANES, (g + 1) * LANES)
         image = own[:, cols] + sums
         w[:, cols] = image
@@ -564,7 +565,7 @@
     copies = []
     for fetch in fetches:
         fetch.wait()
-    for g, sums in window_sums(cfg, peer, node_row, recv, left, hot):
+    for g, sums in window_sums(cfg, peer, node_row, recv, left, hot, step=RETURN_STEP):
         cols = slice(g * LANES, (g + 1) * LANES)
         image = own[:, cols] + sums
         start, before = right[:, cols], w[:, cols]

time: 73.9 us -> 73.7 us (level)
  no operation moved by 1% of the time
where the time goes in v4:
time: 73.7 us; the launch traced here: 73.2 us
  Pallas kernels  32.6 us (44%)
  waiting for transfers between devices  20.2 us (27%)
  starting transfers between devices  19.2 us (26%)
  between operations  0.88 us (1%)
    pallas_call x13, Pallas kernels, run(): kernel(*[pltpu.with_memory_space_constraint(operand, pltpu.VMEM if k in r...  32.6 us
    all_to_all x5, waiting for transfers between devices, exchange(): lax.all_to_all(values, 'dom', split_axis=0, concat_axis=0, tiled=True)  20.2 us
    all_to_all x5, starting transfers between devices, exchange(): lax.all_to_all(values, 'dom', split_axis=0, concat_axis=0, tiled=True)  19.2 us
  transfers between devices with their start and end apart: 5, of which 5 were waited for; matrix products, arithmetic and copies ran while one was open for 0% of the time, Pallas kernels for 27%

profile of v4, /device:TPU:0, one launch (start us, length us, event | category | flops | bytes accessed | tf_op | source)
XLA Modules:
  0.0 73.2 jit_solution(4983525952210053693)
XLA Ops:
  0.6 2.2 %ghost_diag.1 = (f32[32,1,128]{2,1,0:T(1,128)}, s32[8,128]{1,0:T(8,128)S(1)}, s32[1,128]{1,0:T(1,128)S(1)}, s32[5,1,128]{2,1,0:T(1,128)}, s32[1,640]{1,0:T(1,128)S(1)}) custom-call(s32[1,5]{1,0:T(1,128)} %peer.3, f32[3]{0:T(128)} %density.3, s32[125,256]{1,0:T(8,128)} %nodes.3, f32[3,125,256]{2,1,0:T(8,128)} %stiff.3, f32[125,256]{1,0:T(8,128)} %mass.3, ...), custom_call_target="tpu_custom_call" | custom-call | tf_op jit(solution)/shard_map/ghost_diag/pallas_call | solution.py:125
  2.9 7.3 %all-to-all-start = ((f32[32,1,128]{2,1,0:T(1,128)}), f32[32,1,128]{2,1,0:T(1,128)S(1)}, u32[]{:S(2)}, u32[]{:S(2)}) async-start(f32[32,1,128]{2,1,0:T(1,128)} %get-tuple-element.38), calls=%async_computation | async-start | bytes 32768 | tf_op jit(solution)/shard_map/all_to_all | solution.py:618
  10.2 5.2 %tables.1 = (s32[256,128]{1,0:T(8,128)S(1)}, f32[128,384]{1,0:T(8,128)S(1)}, f32[128,128]{1,0:T(8,128)S(1)}, f32[128,384]{1,0:T(8,128)}, f32[128,128]{1,0:T(8,12...) custom-call(s32[1,5]{1,0:T(1,128)} %peer.3, ...), custom_call_target="tpu_custom_call" | custom-call | tf_op jit(solution)/shard_map/tables/pallas_call | solution.py:125
  15.4 1.9 %all-to-all-done.recv = f32[32,1,128]{2,1,0:T(1,128)S(1)} async-done(((f32[32,1,128]{2,1,0:T(1,128)}), f32[32,1,128]{2,1,0:T(1,128)S(1)}, u32[]{:S(2)}, u32[]{:S(2)}) %all-to-all-start) | async-done | bytes 16416 | tf_op jit(solution)/shard_map/all_to_all | solution.py:618
  17.3 0.0 copy-start
  17.3 1.4 %start.1 = (f32[32,8,128]{2,1,0:T(8,128)}, f32[8,640]{1,0:T(8,128)S(1)}) custom-call(s32[1,128]{1,0:T(1,128)S(1)} %get-tuple-element.36.peer_row, f32[32,1,128]{2,1,0:T(1,128)S(1)} %all-to-all-done.recv, f32[8,640]{1,0:T(8,128)S(1)} %get-tuple-element.40.right_at, f32[8,640]{1,0:T(8,128)S(1)} %get-tuple-element.41.diag_at, ...), custom_call_target="tpu_custom_call" | custom-call | tf_op jit(solution)/shard_map/start/pallas_call | solution.py:125
  18.7 4.0 %all-to-all-start.1 = ((f32[32,8,128]{2,1,0:T(8,128)}), f32[32,8,128]{2,1,0:T(8,128)S(1)}, u32[]{:S(2)}, u32[]{:S(2)}) async-start(f32[32,8,128]{2,1,0:T(8,128)} %get-tuple-element.43), calls=%async_computation.1 | async-start | bytes 262144 | tf_op jit(solution)/shard_map/all_to_all | solution.py:618
  22.7 0.0 copy-done
  22.7 0.0 copy-start.1
  22.7 0.0 copy-start.2
  22.7 0.7 first_fields.1
  23.4 0.2 copy-done.1
  23.6 0.1 copy-done.2
  23.7 2.2 %inner.2 = (f32[1024,128]{1,0:T(8,128)S(1)}, f32[8,128]{1,0:T(8,128)S(1)}) custom-call(f32[8,16384]{1,0:T(8,128)S(1)} %get-tuple-element.45.z, s32[256,128]{1,0:T(8,128)S(1)} %get-tuple-element.46.idx, f32[128,384]{1,0:T(8,128)} %get-tuple-element.51.st, f32[128,128]{1,0:T(8,128)} %get-tuple-element.52.mt, bf16[128,768]{1,0:T(8,128)(2,1)S(1)} %copy-done.2, ...), custom_call_target="tpu_custom_call" | custom-call | tf_op jit(solution)/shard_map/inner/pallas_call | solution.py:125
  25.9 4.9 %all-to-all-done.1.recv = f32[32,8,128]{2,1,0:T(8,128)S(1)} async-done(((f32[32,8,128]{2,1,0:T(8,128)}), f32[32,8,128]{2,1,0:T(8,128)S(1)}, u32[]{:S(2)}, u32[]{:S(2)}) %all-to-all-start.1) | async-done | bytes 131104 | tf_op jit(solution)/shard_map/all_to_all | solution.py:618
  30.9 2.6 %edge.2 = (f32[1024,128]{1,0:T(8,128)S(1)}, f32[288,1,128]{2,1,0:T(1,128)}) custom-call(s32[1,128]{1,0:T(1,128)S(1)} %get-tuple-element.36.peer_row, f32[32,8,128]{2,1,0:T(8,128)S(1)} %all-to-all-done.1.recv, f32[8,16384]{1,0:T(8,128)S(1)} %get-tuple-element.45.z, s32[256,128]{1,0:T(8,128)S(1)} %get-tuple-element.46.idx, ...), custom_call_target="tpu_custom_call" | custom-call | tf_op jit(solution)/shard_map/edge/pallas_call | solution.py:125
  33.5 2.6 %all-to-all-start.2 = ((f32[288,1,128]{2,1,0:T(1,128)}), f32[288,1,128]{2,1,0:T(1,128)S(1)}, u32[]{:S(2)}, u32[]{:S(2)}) async-start(f32[288,1,128]{2,1,0:T(1,128)} %get-tuple-element.54), calls=%async_computation.2 | async-start | bytes 294912 | tf_op jit(solution)/shard_map/all_to_all | solution.py:618
  36.1 4.5 %edge_scatter_pick.1 = (f32[8,16384]{1,0:T(8,128)}, f32[8,640]{1,0:T(8,128)S(1)}) custom-call(s32[5,1,128]{2,1,0:T(1,128)} %get-tuple-element.39.base_s, s32[1,640]{1,0:T(1,128)S(1)} %get-tuple-element.37.node_row, f32[1024,128]{1,0:T(8,128)S(1)} %get-tuple-element.56.result, s32[256,128]{1,0:T(8,128)S(1)} %get-tuple-element.46.idx, ...), custom_call_target="tpu_custom_call" | custom-call | tf_op jit(solution)/shard_map/edge_scatter_pick/pallas_call | solution.py:125
  40.5 4.0 %all-to-all-done.2.recv = f32[288,1,128]{2,1,0:T(1,128)S(1)} async-done(((f32[288,1,128]{2,1,0:T(1,128)}), f32[288,1,128]{2,1,0:T(1,128)S(1)}, u32[]{:S(2)}, u32[]{:S(2)}) %all-to-all-start.2) | async-done | bytes 147488 | tf_op jit(solution)/shard_map/all_to_all | solution.py:618
  44.5 1.2 %step.1 = (f32[32,8,128]{2,1,0:T(8,128)}, f32[2,8,128]{2,1,0:T(8,128)S(1)}) custom-call(s32[1,128]{1,0:T(1,128)S(1)} %get-tuple-element.36.peer_row, f32[288,1,128]{2,1,0:T(1,128)S(1)} %all-to-all-done.2.recv, f32[8,640]{1,0:T(8,128)S(1)} %get-tuple-element.40.right_at, f32[8,640]{1,0:T(8,128)S(1)} %get-tuple-element.55.inverse_at, ...), custom_call_target="tpu_custom_call" | custom-call | tf_op jit(solution)/shard_map/step/pallas_call | solution.py:125
  45.7 2.7 %all-to-all-start.3 = ((f32[32,8,128]{2,1,0:T(8,128)}), f32[32,8,128]{2,1,0:T(8,128)S(1)}, u32[]{:S(2)}, u32[]{:S(2)}) async-start(f32[32,8,128]{2,1,0:T(8,128)} %get-tuple-element.59), calls=%async_computation.3 | async-start | bytes 262144 | tf_op jit(solution)/shard_map/all_to_all | solution.py:618
  48.4 2.5 %next_fields.1 = (f32[8,16384]{1,0:T(8,128)}, f32[8,16384]{1,0:T(8,128)S(1)}, f32[8,128]{1,0:T(8,128)S(1)}) custom-call(s32[1,128]{1,0:T(1,128)S(1)} %get-tuple-element.36.peer_row, s32[1,640]{1,0:T(1,128)S(1)} %get-tuple-element.37.node_row, f32[288,1,128]{2,1,0:T(1,128)S(1)} %all-to-all-done.2.recv, f32[8,16384]{1,0:T(8,128)} %get-tuple-element.60.own_hbm, ...), custom_call_target="tpu_custom_call" | custom-call | tf_op jit(solution)/shard_map/next_fields/pallas_call | solution.py:125
  50.9 2.2 %inner.3 = (f32[1024,128]{1,0:T(8,128)S(1)}, f32[8,128]{1,0:T(8,128)S(1)}) custom-call(f32[8,16384]{1,0:T(8,128)S(1)} %get-tuple-element.63.z.z1, s32[256,128]{1,0:T(8,128)S(1)} %get-tuple-element.46.idx, f32[128,384]{1,0:T(8,128)} %get-tuple-element.51.st, f32[128,128]{1,0:T(8,128)} %get-tuple-element.52.mt, bf16[128,768]{1,0:T(8,128)(2,1)S(1)} %copy-done.2, ...), custom_call_target="tpu_custom_call" | custom-call | tf_op jit(solution)/shard_map/inner/pallas_call | solution.py:125
  53.2 3.3 %all-to-all-done.3.recv = f32[32,8,128]{2,1,0:T(8,128)S(1)} async-done(((f32[32,8,128]{2,1,0:T(8,128)}), f32[32,8,128]{2,1,0:T(8,128)S(1)}, u32[]{:S(2)}, u32[]{:S(2)}) %all-to-all-start.3) | async-done | bytes 131104 | tf_op jit(solution)/shard_map/all_to_all | solution.py:618
  56.5 2.6 %edge.3 = (f32[1024,128]{1,0:T(8,128)S(1)}, f32[288,1,128]{2,1,0:T(1,128)}) custom-call(s32[1,128]{1,0:T(1,128)S(1)} %get-tuple-element.36.peer_row, f32[32,8,128]{2,1,0:T(8,128)S(1)} %all-to-all-done.3.recv, f32[8,16384]{1,0:T(8,128)S(1)} %get-tuple-element.63.z.z1, s32[256,128]{1,0:T(8,128)S(1)} %get-tuple-element.46.idx, ...), custom_call_target="tpu_custom_call" | custom-call | tf_op jit(solution)/shard_map/edge/pallas_call | solution.py:125
  59.1 2.6 %all-to-all-start.4 = ((f32[288,1,128]{2,1,0:T(1,128)}), f32[288,1,128]{2,1,0:T(1,128)S(1)}, u32[]{:S(2)}, u32[]{:S(2)}) async-start(f32[288,1,128]{2,1,0:T(1,128)} %get-tuple-element.66), calls=%async_computation.4 | async-start | bytes 294912 | tf_op jit(solution)/shard_map/all_to_all | solution.py:618
  61.7 2.3 %edge_scatter.1.own = f32[8,16384]{1,0:T(8,128)S(1)} custom-call(f32[1024,128]{1,0:T(8,128)S(1)} %get-tuple-element.67.result, s32[256,128]{1,0:T(8,128)S(1)} %get-tuple-element.46.idx, f32[1024,128]{1,0:T(8,128)S(1)} %get-tuple-element.68.inner), custom_call_target="tpu_custom_call" | custom-call | tf_op jit(solution)/shard_map/edge_scatter/pallas_call | solution.py:125
  64.0 6.1 %all-to-all-done.4.recv = f32[288,1,128]{2,1,0:T(1,128)S(1)} async-done(((f32[288,1,128]{2,1,0:T(1,128)}), f32[288,1,128]{2,1,0:T(1,128)S(1)}, u32[]{:S(2)}, u32[]{:S(2)}) %all-to-all-start.4) | async-done | bytes 147488 | tf_op jit(solution)/shard_map/all_to_all | solution.py:618
  70.1 2.9 %last.1 = (f32[8,16384]{1,0:T(8,128)}, f32[8,16384]{1,0:T(8,128)}) custom-call(s32[1,128]{1,0:T(1,128)S(1)} %get-tuple-element.36.peer_row, s32[1,640]{1,0:T(1,128)S(1)} %get-tuple-element.37.node_row, f32[288,1,128]{2,1,0:T(1,128)S(1)} %all-to-all-done.4.recv, f32[8,16384]{1,0:T(8,128)S(1)} %edge_scatter.1.own, f32[8,16384]{1,0:T(8,128)} %right_hbm.3, ...), custom_call_target="tpu_custom_call" | custom-call | tf_op jit(solution)/shard_map/last/pallas_call | solution.py:125
Async XLA Ops:
  2.9 14.4 %all-to-all-start = ((f32[32,1,128]{2,1,0:T(1,128)}), f32[32,1,128]{2,1,0:T(1,128)S(1)}, u32[]{:S(2)}, u32[]{:S(2)}) async-start(f32[32,1,128]{2,1,0:T(1,128)} %get-tuple-element.38), calls=%async_computation | async-start | bytes 32768 | tf_op jit(solution)/shard_map/all_to_all | solution.py:618
  17.3 5.4 %copy-start = (f32[8,16384]{1,0:T(8,128)S(1)}, f32[8,16384]{1,0:T(8,128)}, u32[]{:S(2)}) copy-start(f32[8,16384]{1,0:T(8,128)} %right_hbm.3) | copy-start | bytes 1572868
  18.7 12.2 %all-to-all-start.1 = ((f32[32,8,128]{2,1,0:T(8,128)}), f32[32,8,128]{2,1,0:T(8,128)S(1)}, u32[]{:S(2)}, u32[]{:S(2)}) async-start(f32[32,8,128]{2,1,0:T(8,128)} %get-tuple-element.43), calls=%async_computation.1 | async-start | bytes 262144 | tf_op jit(solution)/shard_map/all_to_all | solution.py:618
  22.7 0.9 %copy-start.1 = (bf16[384,256]{1,0:T(8,128)(2,1)S(1)}, bf16[384,256]{1,0:T(8,128)(2,1)}, u32[]{:S(2)}) copy-start(bf16[384,256]{1,0:T(8,128)(2,1)} %constant.7.clone.w2) | copy-start | bytes 589828
  22.7 1.0 %copy-start.2 = (bf16[128,768]{1,0:T(8,128)(2,1)S(1)}, bf16[128,768]{1,0:T(8,128)(2,1)}, u32[]{:S(2)}) copy-start(bf16[128,768]{1,0:T(8,128)(2,1)} %constant.6.clone.w1) | copy-start | bytes 589828
  33.5 11.0 %all-to-all-start.2 = ((f32[288,1,128]{2,1,0:T(1,128)}), f32[288,1,128]{2,1,0:T(1,128)S(1)}, u32[]{:S(2)}, u32[]{:S(2)}) async-start(f32[288,1,128]{2,1,0:T(1,128)} %get-tuple-element.54), calls=%async_computation.2 | async-start | bytes 294912 | tf_op jit(solution)/shard_map/all_to_all | solution.py:618
  45.7 10.8 %all-to-all-start.3 = ((f32[32,8,128]{2,1,0:T(8,128)}), f32[32,8,128]{2,1,0:T(8,128)S(1)}, u32[]{:S(2)}, u32[]{:S(2)}) async-start(f32[32,8,128]{2,1,0:T(8,128)} %get-tuple-element.59), calls=%async_computation.3 | async-start | bytes 262144 | tf_op jit(solution)/shard_map/all_to_all | solution.py:618
  59.1 11.0 %all-to-all-start.4 = ((f32[288,1,128]{2,1,0:T(1,128)}), f32[288,1,128]{2,1,0:T(1,128)S(1)}, u32[]{:S(2)}, u32[]{:S(2)}) async-start(f32[288,1,128]{2,1,0:T(1,128)} %get-tuple-element.66), calls=%async_computation.4 | async-start | bytes 294912 | tf_op jit(solution)/shard_map/all_to_all | solution.py:618

commit v5 on v4

--- a/solution.py
+++ b/solution.py
@@ -182,10 +182,16 @@
 
 
 def tables_body(
-    cfg, peer, density, nodes, stiff, mass, region, squares, base_s, node_row, right,
+    cfg, peer, density, nodes, stiff_hbm, mass, region, squares, base_s, node_row, right_hbm,
     idx, st_edge, mt_edge, st_inner, mt_inner, own_diag, right_at, diag_at, same,
-    code_pad, value_pad, rows,
+    code_pad, value_pad, rows, stiff, right, arrived,
 ):
+    fetches = [
+        pltpu.make_async_copy(stiff_hbm, stiff, arrived.at[0]),
+        pltpu.make_async_copy(right_hbm, right, arrived.at[1]),
+    ]
+    for fetch in fetches:
+        fetch.start()
     code_pad[...] = jnp.full(code_pad.shape, NONE, jnp.int32)
     value_pad[...] = jnp.zeros(value_pad.shape, jnp.float32)
 
@@ -198,6 +204,8 @@
             nodes[:, cols], b * LANES, peer, cfg["own"], cfg["peers"], cfg["window"]
         )
     idx[...] = turned(code_pad)
+    for fetch in fetches:
+        fetch.wait()
     term, diag = element_sums(mass[...], region[...], density, stiff, squares)
     value_pad[:NPE] = diag
     rows[...] = turned(value_pad)
@@ -637,7 +645,7 @@
     slots_all = ((vectors, peers * slots), f32)
     edge_count = elem_count // 2
     idx, st_edge, mt_edge, st_inner, mt_inner, own_diag, right_at, diag_at, same = call(
-        bind(tables_body), "tables", [S, S] + [V] * 5 + [S, V, V],
+        bind(tables_body), "tables", [S, S, V, hbm(), V, V, V, S, V, hbm()],
         [
             ((elem_count, LANES), i32),
             ((edge_count, 3 * LANES), f32), ((edge_count, LANES), f32),
@@ -647,7 +655,8 @@
         (0, 1, 2, 5, 6, 7, 8),
         [
             pltpu.VMEM((LANES, elem_count), i32), pltpu.VMEM((LANES, elem_count), f32),
-            pltpu.VMEM((elem_count, LANES), f32),
+            pltpu.VMEM((elem_count, LANES), f32), pltpu.VMEM(stiffness.shape, f32), pltpu.VMEM(*field),
+            pltpu.SemaphoreType.DMA((2,)),
         ],
         (8,),
     )(peer_rank, density, elem_nodes, stiffness, mass, regions, squares, base, node_row, right_side)

time: 73.7 us -> 74.6 us (1.012)
  starting transfers between devices: 19.2 us -> 20.1 us
  Pallas kernels: 32.6 us -> 33.5 us
  waiting for transfers between devices: 20.2 us -> 19.3 us
    all_to_all x5, starting transfers between devices: 19.2 us -> 20.1 us  [exchange(): lax.all_to_all(values, 'dom', split_axis=0, concat_axis=0, tiled=True)]
    all_to_all x5, waiting for transfers between devices: 20.2 us -> 19.3 us  [exchange(): lax.all_to_all(values, 'dom', split_axis=0, concat_axis=0, tiled=True)]
    pallas_call x13, Pallas kernels: 32.6 us -> 33.5 us  [run(): kernel(*[pltpu.with_memory_space_constraint(operand, pltpu.VMEM if k in r...]
  transfers between devices with their start and end apart: 5 -> 5, of which waited for: 5 -> 5; matrix products, arithmetic and copies ran while one was open for 0% -> 0% of each run, Pallas kernels for 27% -> 28%
where the time goes in v5:
time: 74.6 us; the launch traced here: 74.1 us
  Pallas kernels  33.5 us (45%)
  starting transfers between devices  20.1 us (27%)
  waiting for transfers between devices  19.3 us (26%)
  between operations  0.89 us (1%)
    pallas_call x13, Pallas kernels, run(): kernel(*[pltpu.with_memory_space_constraint(operand, pltpu.VMEM if k in r...  33.5 us
    all_to_all x5, starting transfers between devices, exchange(): lax.all_to_all(values, 'dom', split_axis=0, concat_axis=0, tiled=True)  20.1 us
    all_to_all x5, waiting for transfers between devices, exchange(): lax.all_to_all(values, 'dom', split_axis=0, concat_axis=0, tiled=True)  19.3 us
  transfers between devices with their start and end apart: 5, of which 5 were waited for; matrix products, arithmetic and copies ran while one was open for 0% of the time, Pallas kernels for 28%

profile of v5, /device:TPU:0, one launch (start us, length us, event | category | flops | bytes accessed | tf_op | source)
XLA Modules:
  0.0 74.1 jit_solution(15440556758372687304)
XLA Ops:
  0.6 2.2 %ghost_diag.1 = (f32[32,1,128]{2,1,0:T(1,128)}, s32[8,128]{1,0:T(8,128)S(1)}, s32[1,128]{1,0:T(1,128)S(1)}, s32[5,1,128]{2,1,0:T(1,128)}, s32[1,640]{1,0:T(1,128)S(1)}) custom-call(s32[1,5]{1,0:T(1,128)} %peer.3, f32[3]{0:T(128)} %density.3, s32[125,256]{1,0:T(8,128)} %nodes.3, f32[3,125,256]{2,1,0:T(8,128)} %stiff_hbm.1, f32[125,256]{1,0:T(8,128)} %mass.3, ...), custom_call_target="tpu_custom_call" | custom-call | tf_op jit(solution)/shard_map/ghost_diag/pallas_call | solution.py:125
  2.9 7.3 %all-to-all-start = ((f32[32,1,128]{2,1,0:T(1,128)}), f32[32,1,128]{2,1,0:T(1,128)S(1)}, u32[]{:S(2)}, u32[]{:S(2)}) async-start(f32[32,1,128]{2,1,0:T(1,128)} %get-tuple-element.38), calls=%async_computation | async-start | bytes 32768 | tf_op jit(solution)/shard_map/all_to_all | solution.py:626
  10.2 6.1 %tables.1 = (s32[256,128]{1,0:T(8,128)S(1)}, f32[128,384]{1,0:T(8,128)S(1)}, f32[128,128]{1,0:T(8,128)S(1)}, f32[128,384]{1,0:T(8,128)}, f32[128,128]{1,0:T(8,12...) custom-call(s32[1,5]{1,0:T(1,128)} %peer.3, ...), custom_call_target="tpu_custom_call" | custom-call | tf_op jit(solution)/shard_map/tables/pallas_call | solution.py:125
  16.3 1.0 %all-to-all-done.recv = f32[32,1,128]{2,1,0:T(1,128)S(1)} async-done(((f32[32,1,128]{2,1,0:T(1,128)}), f32[32,1,128]{2,1,0:T(1,128)S(1)}, u32[]{:S(2)}, u32[]{:S(2)}) %all-to-all-start) | async-done | bytes 16416 | tf_op jit(solution)/shard_map/all_to_all | solution.py:626
  17.3 0.0 copy-start
  17.3 1.4 %start.1 = (f32[32,8,128]{2,1,0:T(8,128)}, f32[8,640]{1,0:T(8,128)S(1)}) custom-call(s32[1,128]{1,0:T(1,128)S(1)} %get-tuple-element.36.peer_row, f32[32,1,128]{2,1,0:T(1,128)S(1)} %all-to-all-done.recv, f32[8,640]{1,0:T(8,128)S(1)} %get-tuple-element.40.right_at, f32[8,640]{1,0:T(8,128)S(1)} %get-tuple-element.41.diag_at, ...), custom_call_target="tpu_custom_call" | custom-call | tf_op jit(solution)/shard_map/start/pallas_call | solution.py:125
  18.7 4.9 %all-to-all-start.1 = ((f32[32,8,128]{2,1,0:T(8,128)}), f32[32,8,128]{2,1,0:T(8,128)S(1)}, u32[]{:S(2)}, u32[]{:S(2)}) async-start(f32[32,8,128]{2,1,0:T(8,128)} %get-tuple-element.43), calls=%async_computation.1 | async-start | bytes 262144 | tf_op jit(solution)/shard_map/all_to_all | solution.py:626
  23.6 0.0 copy-done
  23.6 0.0 copy-start.1
  23.6 0.0 copy-start.2
  23.6 0.7 first_fields.1
  24.3 0.2 copy-done.1
  24.5 0.1 copy-done.2
  24.6 2.2 %inner.2 = (f32[1024,128]{1,0:T(8,128)S(1)}, f32[8,128]{1,0:T(8,128)S(1)}) custom-call(f32[8,16384]{1,0:T(8,128)S(1)} %get-tuple-element.45.z, s32[256,128]{1,0:T(8,128)S(1)} %get-tuple-element.46.idx, f32[128,384]{1,0:T(8,128)} %get-tuple-element.51.st, f32[128,128]{1,0:T(8,128)} %get-tuple-element.52.mt, bf16[128,768]{1,0:T(8,128)(2,1)S(1)} %copy-done.2, ...), custom_call_target="tpu_custom_call" | custom-call | tf_op jit(solution)/shard_map/inner/pallas_call | solution.py:125
  26.8 4.9 %all-to-all-done.1.recv = f32[32,8,128]{2,1,0:T(8,128)S(1)} async-done(((f32[32,8,128]{2,1,0:T(8,128)}), f32[32,8,128]{2,1,0:T(8,128)S(1)}, u32[]{:S(2)}, u32[]{:S(2)}) %all-to-all-start.1) | async-done | bytes 131104 | tf_op jit(solution)/shard_map/all_to_all | solution.py:626
  31.8 2.6 %edge.2 = (f32[1024,128]{1,0:T(8,128)S(1)}, f32[288,1,128]{2,1,0:T(1,128)}) custom-call(s32[1,128]{1,0:T(1,128)S(1)} %get-tuple-element.36.peer_row, f32[32,8,128]{2,1,0:T(8,128)S(1)} %all-to-all-done.1.recv, f32[8,16384]{1,0:T(8,128)S(1)} %get-tuple-element.45.z, s32[256,128]{1,0:T(8,128)S(1)} %get-tuple-element.46.idx, ...), custom_call_target="tpu_custom_call" | custom-call | tf_op jit(solution)/shard_map/edge/pallas_call | solution.py:125
  34.4 2.6 %all-to-all-start.2 = ((f32[288,1,128]{2,1,0:T(1,128)}), f32[288,1,128]{2,1,0:T(1,128)S(1)}, u32[]{:S(2)}, u32[]{:S(2)}) async-start(f32[288,1,128]{2,1,0:T(1,128)} %get-tuple-element.54), calls=%async_computation.2 | async-start | bytes 294912 | tf_op jit(solution)/shard_map/all_to_all | solution.py:626
  37.0 4.5 %edge_scatter_pick.1 = (f32[8,16384]{1,0:T(8,128)}, f32[8,640]{1,0:T(8,128)S(1)}) custom-call(s32[5,1,128]{2,1,0:T(1,128)} %get-tuple-element.39.base_s, s32[1,640]{1,0:T(1,128)S(1)} %get-tuple-element.37.node_row, f32[1024,128]{1,0:T(8,128)S(1)} %get-tuple-element.56.result, s32[256,128]{1,0:T(8,128)S(1)} %get-tuple-element.46.idx, ...), custom_call_target="tpu_custom_call" | custom-call | tf_op jit(solution)/shard_map/edge_scatter_pick/pallas_call | solution.py:125
  41.4 4.0 %all-to-all-done.2.recv = f32[288,1,128]{2,1,0:T(1,128)S(1)} async-done(((f32[288,1,128]{2,1,0:T(1,128)}), f32[288,1,128]{2,1,0:T(1,128)S(1)}, u32[]{:S(2)}, u32[]{:S(2)}) %all-to-all-start.2) | async-done | bytes 147488 | tf_op jit(solution)/shard_map/all_to_all | solution.py:626
  45.4 1.2 %step.1 = (f32[32,8,128]{2,1,0:T(8,128)}, f32[2,8,128]{2,1,0:T(8,128)S(1)}) custom-call(s32[1,128]{1,0:T(1,128)S(1)} %get-tuple-element.36.peer_row, f32[288,1,128]{2,1,0:T(1,128)S(1)} %all-to-all-done.2.recv, f32[8,640]{1,0:T(8,128)S(1)} %get-tuple-element.40.right_at, f32[8,640]{1,0:T(8,128)S(1)} %get-tuple-element.55.inverse_at, ...), custom_call_target="tpu_custom_call" | custom-call | tf_op jit(solution)/shard_map/step/pallas_call | solution.py:125
  46.6 2.7 %all-to-all-start.3 = ((f32[32,8,128]{2,1,0:T(8,128)}), f32[32,8,128]{2,1,0:T(8,128)S(1)}, u32[]{:S(2)}, u32[]{:S(2)}) async-start(f32[32,8,128]{2,1,0:T(8,128)} %get-tuple-element.59), calls=%async_computation.3 | async-start | bytes 262144 | tf_op jit(solution)/shard_map/all_to_all | solution.py:626
  49.3 2.5 %next_fields.1 = (f32[8,16384]{1,0:T(8,128)}, f32[8,16384]{1,0:T(8,128)S(1)}, f32[8,128]{1,0:T(8,128)S(1)}) custom-call(s32[1,128]{1,0:T(1,128)S(1)} %get-tuple-element.36.peer_row, s32[1,640]{1,0:T(1,128)S(1)} %get-tuple-element.37.node_row, f32[288,1,128]{2,1,0:T(1,128)S(1)} %all-to-all-done.2.recv, f32[8,16384]{1,0:T(8,128)} %get-tuple-element.60.own_hbm, ...), custom_call_target="tpu_custom_call" | custom-call | tf_op jit(solution)/shard_map/next_fields/pallas_call | solution.py:125
  51.8 2.2 %inner.3 = (f32[1024,128]{1,0:T(8,128)S(1)}, f32[8,128]{1,0:T(8,128)S(1)}) custom-call(f32[8,16384]{1,0:T(8,128)S(1)} %get-tuple-element.63.z.z1, s32[256,128]{1,0:T(8,128)S(1)} %get-tuple-element.46.idx, f32[128,384]{1,0:T(8,128)} %get-tuple-element.51.st, f32[128,128]{1,0:T(8,128)} %get-tuple-element.52.mt, bf16[128,768]{1,0:T(8,128)(2,1)S(1)} %copy-done.2, ...), custom_call_target="tpu_custom_call" | custom-call | tf_op jit(solution)/shard_map/inner/pallas_call | solution.py:125
  54.1 3.3 %all-to-all-done.3.recv = f32[32,8,128]{2,1,0:T(8,128)S(1)} async-done(((f32[32,8,128]{2,1,0:T(8,128)}), f32[32,8,128]{2,1,0:T(8,128)S(1)}, u32[]{:S(2)}, u32[]{:S(2)}) %all-to-all-start.3) | async-done | bytes 131104 | tf_op jit(solution)/shard_map/all_to_all | solution.py:626
  57.3 2.6 %edge.3 = (f32[1024,128]{1,0:T(8,128)S(1)}, f32[288,1,128]{2,1,0:T(1,128)}) custom-call(s32[1,128]{1,0:T(1,128)S(1)} %get-tuple-element.36.peer_row, f32[32,8,128]{2,1,0:T(8,128)S(1)} %all-to-all-done.3.recv, f32[8,16384]{1,0:T(8,128)S(1)} %get-tuple-element.63.z.z1, s32[256,128]{1,0:T(8,128)S(1)} %get-tuple-element.46.idx, ...), custom_call_target="tpu_custom_call" | custom-call | tf_op jit(solution)/shard_map/edge/pallas_call | solution.py:125
  60.0 2.6 %all-to-all-start.4 = ((f32[288,1,128]{2,1,0:T(1,128)}), f32[288,1,128]{2,1,0:T(1,128)S(1)}, u32[]{:S(2)}, u32[]{:S(2)}) async-start(f32[288,1,128]{2,1,0:T(1,128)} %get-tuple-element.66), calls=%async_computation.4 | async-start | bytes 294912 | tf_op jit(solution)/shard_map/all_to_all | solution.py:626
  62.6 2.3 %edge_scatter.1.own = f32[8,16384]{1,0:T(8,128)S(1)} custom-call(f32[1024,128]{1,0:T(8,128)S(1)} %get-tuple-element.67.result, s32[256,128]{1,0:T(8,128)S(1)} %get-tuple-element.46.idx, f32[1024,128]{1,0:T(8,128)S(1)} %get-tuple-element.68.inner), custom_call_target="tpu_custom_call" | custom-call | tf_op jit(solution)/shard_map/edge_scatter/pallas_call | solution.py:125
  64.9 6.1 %all-to-all-done.4.recv = f32[288,1,128]{2,1,0:T(1,128)S(1)} async-done(((f32[288,1,128]{2,1,0:T(1,128)}), f32[288,1,128]{2,1,0:T(1,128)S(1)}, u32[]{:S(2)}, u32[]{:S(2)}) %all-to-all-start.4) | async-done | bytes 147488 | tf_op jit(solution)/shard_map/all_to_all | solution.py:626
  71.0 2.9 %last.1 = (f32[8,16384]{1,0:T(8,128)}, f32[8,16384]{1,0:T(8,128)}) custom-call(s32[1,128]{1,0:T(1,128)S(1)} %get-tuple-element.36.peer_row, s32[1,640]{1,0:T(1,128)S(1)} %get-tuple-element.37.node_row, f32[288,1,128]{2,1,0:T(1,128)S(1)} %all-to-all-done.4.recv, f32[8,16384]{1,0:T(8,128)S(1)} %edge_scatter.1.own, f32[8,16384]{1,0:T(8,128)} %right_hbm.5, ...), custom_call_target="tpu_custom_call" | custom-call | tf_op jit(solution)/shard_map/last/pallas_call | solution.py:125
Async XLA Ops:
  2.9 14.4 %all-to-all-start = ((f32[32,1,128]{2,1,0:T(1,128)}), f32[32,1,128]{2,1,0:T(1,128)S(1)}, u32[]{:S(2)}, u32[]{:S(2)}) async-start(f32[32,1,128]{2,1,0:T(1,128)} %get-tuple-element.38), calls=%async_computation | async-start | bytes 32768 | tf_op jit(solution)/shard_map/all_to_all | solution.py:626
  17.3 6.3 %copy-start = (f32[8,16384]{1,0:T(8,128)S(1)}, f32[8,16384]{1,0:T(8,128)}, u32[]{:S(2)}) copy-start(f32[8,16384]{1,0:T(8,128)} %right_hbm.5) | copy-start | bytes 1572868
  18.7 13.1 %all-to-all-start.1 = ((f32[32,8,128]{2,1,0:T(8,128)}), f32[32,8,128]{2,1,0:T(8,128)S(1)}, u32[]{:S(2)}, u32[]{:S(2)}) async-start(f32[32,8,128]{2,1,0:T(8,128)} %get-tuple-element.43), calls=%async_computation.1 | async-start | bytes 262144 | tf_op jit(solution)/shard_map/all_to_all | solution.py:626
  23.6 0.9 %copy-start.1 = (bf16[384,256]{1,0:T(8,128)(2,1)S(1)}, bf16[384,256]{1,0:T(8,128)(2,1)}, u32[]{:S(2)}) copy-start(bf16[384,256]{1,0:T(8,128)(2,1)} %constant.7.clone.w2) | copy-start | bytes 589828
  23.6 1.0 %copy-start.2 = (bf16[128,768]{1,0:T(8,128)(2,1)S(1)}, bf16[128,768]{1,0:T(8,128)(2,1)}, u32[]{:S(2)}) copy-start(bf16[128,768]{1,0:T(8,128)(2,1)} %constant.6.clone.w1) | copy-start | bytes 589828
  34.4 11.0 %all-to-all-start.2 = ((f32[288,1,128]{2,1,0:T(1,128)}), f32[288,1,128]{2,1,0:T(1,128)S(1)}, u32[]{:S(2)}, u32[]{:S(2)}) async-start(f32[288,1,128]{2,1,0:T(1,128)} %get-tuple-element.54), calls=%async_computation.2 | async-start | bytes 294912 | tf_op jit(solution)/shard_map/all_to_all | solution.py:626
  46.6 10.8 %all-to-all-start.3 = ((f32[32,8,128]{2,1,0:T(8,128)}), f32[32,8,128]{2,1,0:T(8,128)S(1)}, u32[]{:S(2)}, u32[]{:S(2)}) async-start(f32[32,8,128]{2,1,0:T(8,128)} %get-tuple-element.59), calls=%async_computation.3 | async-start | bytes 262144 | tf_op jit(solution)/shard_map/all_to_all | solution.py:626
  60.0 11.0 %all-to-all-start.4 = ((f32[288,1,128]{2,1,0:T(1,128)}), f32[288,1,128]{2,1,0:T(1,128)S(1)}, u32[]{:S(2)}, u32[]{:S(2)}) async-start(f32[288,1,128]{2,1,0:T(1,128)} %get-tuple-element.66), calls=%async_computation.4 | async-start | bytes 294912 | tf_op jit(solution)/shard_map/all_to_all | solution.py:626

commit v6 on v4

--- a/solution.py
+++ b/solution.py
@@ -201,14 +201,9 @@
     term, diag = element_sums(mass[...], region[...], density, stiff, squares)
     value_pad[:NPE] = diag
     rows[...] = turned(value_pad)
-    for g in range(0, cfg["pairs"], 2):
-        lines = [
-            spread(jnp.concatenate([rows[2 * k : 2 * k + 1, :], rows[2 * k + 1 : 2 * k + 2, :]], axis=1))
-            for k in (g, g + 1)
-        ]
-        for k, sums in enumerate(scatter_pairs(lines, idx, g)):
-            own_diag[g + k : g + k + 1, :] = sums[:1]
-    pick(cfg, right, base_s, node_row, right_at)
+    for g in range(cfg["pairs"]):
+        row = jnp.concatenate([rows[2 * g : 2 * g + 1, :], rows[2 * g + 1 : 2 * g + 2, :]], axis=1)
+        own_diag[g : g + 1, :] = scatter_rows(spread(row), idx, g)[:1]
     for d in range(3):
         value_pad[:NPE] = stiff[d]
         cols = slice(d * LANES, (d + 1) * LANES)
@@ -217,6 +212,7 @@
     value_pad[:NPE] = term
     mt_edge[...] = value_pad[:, :LANES].T
     mt_inner[...] = value_pad[:, LANES:].T
+    pick(cfg, right, base_s, node_row, right_at)
     node = node_row[...]
     wide = node.shape[1]
     hot = jnp.where(iota((LANES, wide), 0) == (node & (LANES - 1)), 1.0, 0.0).astype(jnp.bfloat16)
@@ -243,23 +239,6 @@
     both = jnp.concatenate([high, rows - high], axis=0).astype(jnp.bfloat16)
     sums = lax.dot_general(both, spots, (((1,), (1,)), ((), ())), preferred_element_type=jnp.float32)
     return sums[:ROWS] + sums[ROWS:]
-
-
-def scatter_pairs(rows, idx, g):
-    node = iota((LANES, LANES), 0)
-    spots = [
-        jnp.concatenate(
-            [jnp.where(node == idx[e : e + 1, :], 1.0, 0.0) for e in (2 * pair, 2 * pair + 1)], axis=1
-        ).astype(jnp.bfloat16)
-        for pair in (g, g + 1)
-    ]
-    parts = []
-    for values in rows:
-        high = values.astype(jnp.bfloat16).astype(jnp.float32)
-        parts += [high, values - high]
-    sums = nt_dot(jnp.concatenate(parts, axis=0).astype(jnp.bfloat16), jnp.concatenate(spots, axis=0))
-    own = (sums[: 2 * ROWS, :LANES], sums[2 * ROWS :, LANES:])
-    return [x[:ROWS] + x[ROWS:] for x in own]
 
 
 def peers_of(cfg, peer_row):

time: 73.7 us -> 73.6 us (level)
  no operation moved by 1% of the time
where the time goes in v6:
time: 73.6 us; the launch traced here: 73 us
  Pallas kernels  32.5 us (44%)
  waiting for transfers between devices  20.3 us (28%)
  starting transfers between devices  19.1 us (26%)
  between operations  0.88 us (1%)
    pallas_call x13, Pallas kernels, run(): kernel(*[pltpu.with_memory_space_constraint(operand, pltpu.VMEM if k in r...  32.5 us
    all_to_all x5, waiting for transfers between devices, exchange(): lax.all_to_all(values, 'dom', split_axis=0, concat_axis=0, tiled=True)  20.3 us
    all_to_all x5, starting transfers between devices, exchange(): lax.all_to_all(values, 'dom', split_axis=0, concat_axis=0, tiled=True)  19.1 us
  transfers between devices with their start and end apart: 5, of which 5 were waited for; matrix products, arithmetic and copies ran while one was open for 0% of the time, Pallas kernels for 27%

profile of v6, /device:TPU:0, one launch (start us, length us, event | category | flops | bytes accessed | tf_op | source)
XLA Modules:
  0.0 73.0 jit_solution(8474700645830782683)
XLA Ops:
  0.6 2.2 %ghost_diag.1 = (f32[32,1,128]{2,1,0:T(1,128)}, s32[8,128]{1,0:T(8,128)S(1)}, s32[1,128]{1,0:T(1,128)S(1)}, s32[5,1,128]{2,1,0:T(1,128)}, s32[1,640]{1,0:T(1,128)S(1)}) custom-call(s32[1,5]{1,0:T(1,128)} %peer.3, f32[3]{0:T(128)} %density.3, s32[125,256]{1,0:T(8,128)} %nodes.3, f32[3,125,256]{2,1,0:T(8,128)} %stiff.3, f32[125,256]{1,0:T(8,128)} %mass.3, ...), custom_call_target="tpu_custom_call" | custom-call | tf_op jit(solution)/shard_map/ghost_diag/pallas_call | solution.py:125
  2.9 7.3 %all-to-all-start = ((f32[32,1,128]{2,1,0:T(1,128)}), f32[32,1,128]{2,1,0:T(1,128)S(1)}, u32[]{:S(2)}, u32[]{:S(2)}) async-start(f32[32,1,128]{2,1,0:T(1,128)} %get-tuple-element.38), calls=%async_computation | async-start | bytes 32768 | tf_op jit(solution)/shard_map/all_to_all | solution.py:597
  10.2 5.1 %tables.1 = (s32[256,128]{1,0:T(8,128)S(1)}, f32[128,384]{1,0:T(8,128)S(1)}, f32[128,128]{1,0:T(8,128)S(1)}, f32[128,384]{1,0:T(8,128)}, f32[128,128]{1,0:T(8,12...) custom-call(s32[1,5]{1,0:T(1,128)} %peer.3, ...), custom_call_target="tpu_custom_call" | custom-call | tf_op jit(solution)/shard_map/tables/pallas_call | solution.py:125
  15.3 2.0 %all-to-all-done.recv = f32[32,1,128]{2,1,0:T(1,128)S(1)} async-done(((f32[32,1,128]{2,1,0:T(1,128)}), f32[32,1,128]{2,1,0:T(1,128)S(1)}, u32[]{:S(2)}, u32[]{:S(2)}) %all-to-all-start) | async-done | bytes 16416 | tf_op jit(solution)/shard_map/all_to_all | solution.py:597
  17.3 0.0 copy-start
  17.3 1.4 %start.1 = (f32[32,8,128]{2,1,0:T(8,128)}, f32[8,640]{1,0:T(8,128)S(1)}) custom-call(s32[1,128]{1,0:T(1,128)S(1)} %get-tuple-element.36.peer_row, f32[32,1,128]{2,1,0:T(1,128)S(1)} %all-to-all-done.recv, f32[8,640]{1,0:T(8,128)S(1)} %get-tuple-element.40.right_at, f32[8,640]{1,0:T(8,128)S(1)} %get-tuple-element.41.diag_at, ...), custom_call_target="tpu_custom_call" | custom-call | tf_op jit(solution)/shard_map/start/pallas_call | solution.py:125
  18.7 3.8 %all-to-all-start.1 = ((f32[32,8,128]{2,1,0:T(8,128)}), f32[32,8,128]{2,1,0:T(8,128)S(1)}, u32[]{:S(2)}, u32[]{:S(2)}) async-start(f32[32,8,128]{2,1,0:T(8,128)} %get-tuple-element.43), calls=%async_computation.1 | async-start | bytes 262144 | tf_op jit(solution)/shard_map/all_to_all | solution.py:597
  22.5 0.0 copy-done
  22.6 0.0 copy-start.1
  22.6 0.0 copy-start.2
  22.6 0.7 first_fields.1
  23.3 0.2 copy-done.1
  23.5 0.1 copy-done.2
  23.6 2.2 %inner.2 = (f32[1024,128]{1,0:T(8,128)S(1)}, f32[8,128]{1,0:T(8,128)S(1)}) custom-call(f32[8,16384]{1,0:T(8,128)S(1)} %get-tuple-element.45.z, s32[256,128]{1,0:T(8,128)S(1)} %get-tuple-element.46.idx, f32[128,384]{1,0:T(8,128)} %get-tuple-element.51.st, f32[128,128]{1,0:T(8,128)} %get-tuple-element.52.mt, bf16[128,768]{1,0:T(8,128)(2,1)S(1)} %copy-done.2, ...), custom_call_target="tpu_custom_call" | custom-call | tf_op jit(solution)/shard_map/inner/pallas_call | solution.py:125
  25.8 4.9 %all-to-all-done.1.recv = f32[32,8,128]{2,1,0:T(8,128)S(1)} async-done(((f32[32,8,128]{2,1,0:T(8,128)}), f32[32,8,128]{2,1,0:T(8,128)S(1)}, u32[]{:S(2)}, u32[]{:S(2)}) %all-to-all-start.1) | async-done | bytes 131104 | tf_op jit(solution)/shard_map/all_to_all | solution.py:597
  30.7 2.6 %edge.2 = (f32[1024,128]{1,0:T(8,128)S(1)}, f32[288,1,128]{2,1,0:T(1,128)}) custom-call(s32[1,128]{1,0:T(1,128)S(1)} %get-tuple-element.36.peer_row, f32[32,8,128]{2,1,0:T(8,128)S(1)} %all-to-all-done.1.recv, f32[8,16384]{1,0:T(8,128)S(1)} %get-tuple-element.45.z, s32[256,128]{1,0:T(8,128)S(1)} %get-tuple-element.46.idx, ...), custom_call_target="tpu_custom_call" | custom-call | tf_op jit(solution)/shard_map/edge/pallas_call | solution.py:125
  33.4 2.6 %all-to-all-start.2 = ((f32[288,1,128]{2,1,0:T(1,128)}), f32[288,1,128]{2,1,0:T(1,128)S(1)}, u32[]{:S(2)}, u32[]{:S(2)}) async-start(f32[288,1,128]{2,1,0:T(1,128)} %get-tuple-element.54), calls=%async_computation.2 | async-start | bytes 294912 | tf_op jit(solution)/shard_map/all_to_all | solution.py:597
  36.0 4.5 %edge_scatter_pick.1 = (f32[8,16384]{1,0:T(8,128)}, f32[8,640]{1,0:T(8,128)S(1)}) custom-call(s32[5,1,128]{2,1,0:T(1,128)} %get-tuple-element.39.base_s, s32[1,640]{1,0:T(1,128)S(1)} %get-tuple-element.37.node_row, f32[1024,128]{1,0:T(8,128)S(1)} %get-tuple-element.56.result, s32[256,128]{1,0:T(8,128)S(1)} %get-tuple-element.46.idx, ...), custom_call_target="tpu_custom_call" | custom-call | tf_op jit(solution)/shard_map/edge_scatter_pick/pallas_call | solution.py:125
  40.4 4.0 %all-to-all-done.2.recv = f32[288,1,128]{2,1,0:T(1,128)S(1)} async-done(((f32[288,1,128]{2,1,0:T(1,128)}), f32[288,1,128]{2,1,0:T(1,128)S(1)}, u32[]{:S(2)}, u32[]{:S(2)}) %all-to-all-start.2) | async-done | bytes 147488 | tf_op jit(solution)/shard_map/all_to_all | solution.py:597
  44.4 1.2 %step.1 = (f32[32,8,128]{2,1,0:T(8,128)}, f32[2,8,128]{2,1,0:T(8,128)S(1)}) custom-call(s32[1,128]{1,0:T(1,128)S(1)} %get-tuple-element.36.peer_row, f32[288,1,128]{2,1,0:T(1,128)S(1)} %all-to-all-done.2.recv, f32[8,640]{1,0:T(8,128)S(1)} %get-tuple-element.40.right_at, f32[8,640]{1,0:T(8,128)S(1)} %get-tuple-element.55.inverse_at, ...), custom_call_target="tpu_custom_call" | custom-call | tf_op jit(solution)/shard_map/step/pallas_call | solution.py:125
  45.6 2.7 %all-to-all-start.3 = ((f32[32,8,128]{2,1,0:T(8,128)}), f32[32,8,128]{2,1,0:T(8,128)S(1)}, u32[]{:S(2)}, u32[]{:S(2)}) async-start(f32[32,8,128]{2,1,0:T(8,128)} %get-tuple-element.59), calls=%async_computation.3 | async-start | bytes 262144 | tf_op jit(solution)/shard_map/all_to_all | solution.py:597
  48.3 2.5 %next_fields.1 = (f32[8,16384]{1,0:T(8,128)}, f32[8,16384]{1,0:T(8,128)S(1)}, f32[8,128]{1,0:T(8,128)S(1)}) custom-call(s32[1,128]{1,0:T(1,128)S(1)} %get-tuple-element.36.peer_row, s32[1,640]{1,0:T(1,128)S(1)} %get-tuple-element.37.node_row, f32[288,1,128]{2,1,0:T(1,128)S(1)} %all-to-all-done.2.recv, f32[8,16384]{1,0:T(8,128)} %get-tuple-element.60.own_hbm, ...), custom_call_target="tpu_custom_call" | custom-call | tf_op jit(solution)/shard_map/next_fields/pallas_call | solution.py:125
  50.8 2.2 %inner.3 = (f32[1024,128]{1,0:T(8,128)S(1)}, f32[8,128]{1,0:T(8,128)S(1)}) custom-call(f32[8,16384]{1,0:T(8,128)S(1)} %get-tuple-element.63.z.z1, s32[256,128]{1,0:T(8,128)S(1)} %get-tuple-element.46.idx, f32[128,384]{1,0:T(8,128)} %get-tuple-element.51.st, f32[128,128]{1,0:T(8,128)} %get-tuple-element.52.mt, bf16[128,768]{1,0:T(8,128)(2,1)S(1)} %copy-done.2, ...), custom_call_target="tpu_custom_call" | custom-call | tf_op jit(solution)/shard_map/inner/pallas_call | solution.py:125
  53.0 3.3 %all-to-all-done.3.recv = f32[32,8,128]{2,1,0:T(8,128)S(1)} async-done(((f32[32,8,128]{2,1,0:T(8,128)}), f32[32,8,128]{2,1,0:T(8,128)S(1)}, u32[]{:S(2)}, u32[]{:S(2)}) %all-to-all-start.3) | async-done | bytes 131104 | tf_op jit(solution)/shard_map/all_to_all | solution.py:597
  56.3 2.6 %edge.3 = (f32[1024,128]{1,0:T(8,128)S(1)}, f32[288,1,128]{2,1,0:T(1,128)}) custom-call(s32[1,128]{1,0:T(1,128)S(1)} %get-tuple-element.36.peer_row, f32[32,8,128]{2,1,0:T(8,128)S(1)} %all-to-all-done.3.recv, f32[8,16384]{1,0:T(8,128)S(1)} %get-tuple-element.63.z.z1, s32[256,128]{1,0:T(8,128)S(1)} %get-tuple-element.46.idx, ...), custom_call_target="tpu_custom_call" | custom-call | tf_op jit(solution)/shard_map/edge/pallas_call | solution.py:125
  59.0 2.6 %all-to-all-start.4 = ((f32[288,1,128]{2,1,0:T(1,128)}), f32[288,1,128]{2,1,0:T(1,128)S(1)}, u32[]{:S(2)}, u32[]{:S(2)}) async-start(f32[288,1,128]{2,1,0:T(1,128)} %get-tuple-element.66), calls=%async_computation.4 | async-start | bytes 294912 | tf_op jit(solution)/shard_map/all_to_all | solution.py:597
  61.6 2.3 %edge_scatter.1.own = f32[8,16384]{1,0:T(8,128)S(1)} custom-call(f32[1024,128]{1,0:T(8,128)S(1)} %get-tuple-element.67.result, s32[256,128]{1,0:T(8,128)S(1)} %get-tuple-element.46.idx, f32[1024,128]{1,0:T(8,128)S(1)} %get-tuple-element.68.inner), custom_call_target="tpu_custom_call" | custom-call | tf_op jit(solution)/shard_map/edge_scatter/pallas_call | solution.py:125
  63.8 6.1 %all-to-all-done.4.recv = f32[288,1,128]{2,1,0:T(1,128)S(1)} async-done(((f32[288,1,128]{2,1,0:T(1,128)}), f32[288,1,128]{2,1,0:T(1,128)S(1)}, u32[]{:S(2)}, u32[]{:S(2)}) %all-to-all-start.4) | async-done | bytes 147488 | tf_op jit(solution)/shard_map/all_to_all | solution.py:597
  70.0 2.9 %last.1 = (f32[8,16384]{1,0:T(8,128)}, f32[8,16384]{1,0:T(8,128)}) custom-call(s32[1,128]{1,0:T(1,128)S(1)} %get-tuple-element.36.peer_row, s32[1,640]{1,0:T(1,128)S(1)} %get-tuple-element.37.node_row, f32[288,1,128]{2,1,0:T(1,128)S(1)} %all-to-all-done.4.recv, f32[8,16384]{1,0:T(8,128)S(1)} %edge_scatter.1.own, f32[8,16384]{1,0:T(8,128)} %right_hbm.3, ...), custom_call_target="tpu_custom_call" | custom-call | tf_op jit(solution)/shard_map/last/pallas_call | solution.py:125
Async XLA Ops:
  2.9 14.4 %all-to-all-start = ((f32[32,1,128]{2,1,0:T(1,128)}), f32[32,1,128]{2,1,0:T(1,128)S(1)}, u32[]{:S(2)}, u32[]{:S(2)}) async-start(f32[32,1,128]{2,1,0:T(1,128)} %get-tuple-element.38), calls=%async_computation | async-start | bytes 32768 | tf_op jit(solution)/shard_map/all_to_all | solution.py:597
  17.3 5.2 %copy-start = (f32[8,16384]{1,0:T(8,128)S(1)}, f32[8,16384]{1,0:T(8,128)}, u32[]{:S(2)}) copy-start(f32[8,16384]{1,0:T(8,128)} %right_hbm.3) | copy-start | bytes 1572868
  18.7 12.1 %all-to-all-start.1 = ((f32[32,8,128]{2,1,0:T(8,128)}), f32[32,8,128]{2,1,0:T(8,128)S(1)}, u32[]{:S(2)}, u32[]{:S(2)}) async-start(f32[32,8,128]{2,1,0:T(8,128)} %get-tuple-element.43), calls=%async_computation.1 | async-start | bytes 262144 | tf_op jit(solution)/shard_map/all_to_all | solution.py:597
  22.6 0.9 %copy-start.1 = (bf16[384,256]{1,0:T(8,128)(2,1)S(1)}, bf16[384,256]{1,0:T(8,128)(2,1)}, u32[]{:S(2)}) copy-start(bf16[384,256]{1,0:T(8,128)(2,1)} %constant.7.clone.w2) | copy-start | bytes 589828
  22.6 1.0 %copy-start.2 = (bf16[128,768]{1,0:T(8,128)(2,1)S(1)}, bf16[128,768]{1,0:T(8,128)(2,1)}, u32[]{:S(2)}) copy-start(bf16[128,768]{1,0:T(8,128)(2,1)} %constant.6.clone.w1) | copy-start | bytes 589828
  33.4 11.0 %all-to-all-start.2 = ((f32[288,1,128]{2,1,0:T(1,128)}), f32[288,1,128]{2,1,0:T(1,128)S(1)}, u32[]{:S(2)}, u32[]{:S(2)}) async-start(f32[288,1,128]{2,1,0:T(1,128)} %get-tuple-element.54), calls=%async_computation.2 | async-start | bytes 294912 | tf_op jit(solution)/shard_map/all_to_all | solution.py:597
  45.6 10.8 %all-to-all-start.3 = ((f32[32,8,128]{2,1,0:T(8,128)}), f32[32,8,128]{2,1,0:T(8,128)S(1)}, u32[]{:S(2)}, u32[]{:S(2)}) async-start(f32[32,8,128]{2,1,0:T(8,128)} %get-tuple-element.59), calls=%async_computation.3 | async-start | bytes 262144 | tf_op jit(solution)/shard_map/all_to_all | solution.py:597
  59.0 11.0 %all-to-all-start.4 = ((f32[288,1,128]{2,1,0:T(1,128)}), f32[288,1,128]{2,1,0:T(1,128)S(1)}, u32[]{:S(2)}, u32[]{:S(2)}) async-start(f32[288,1,128]{2,1,0:T(1,128)} %get-tuple-element.66), calls=%async_computation.4 | async-start | bytes 294912 | tf_op jit(solution)/shard_map/all_to_all | solution.py:597
